TPU v7x, 32 devices: a whole 2x2x4 slice. The times are simulated.
32 devices in a mesh: dp: 16 (over z, x, core), seq: 2 (over y).
Axes of the slice: x: 2, y: 2, z: 4, core: 2. Of those that a mesh axis runs over, the one named last changes fastest.
Arguments:
- frames_in: bfloat16 [16, 1500, 768], P('dp', 'seq'), may hold values from -6 to 6
- ln1_gain: bfloat16 [768], P('dp'), may hold values from 0.25 to 1.75
- ln1_bias: bfloat16 [768], P('dp'), may hold values from -1.75 to 1.75
- w_qkv: bfloat16 [768, 2304], P('dp'), may hold values from -2 to 2
- b_qv: bfloat16 [1536], P('dp'), may hold values from -1.25 to 1.25
- w_o: bfloat16 [768, 768], P('dp'), may hold values from -0.875 to 0.875
- b_o: bfloat16 [768], P('dp'), may hold values from -1.75 to 1.75
- ln2_gain: bfloat16 [768], P('dp'), may hold values from 0.25 to 1.75
- ln2_bias: bfloat16 [768], P('dp'), may hold values from -1.75 to 1.75
- w_fc1: bfloat16 [768, 3072], P('dp'), may hold values from -0.21875 to 0.21875
- b_fc1: bfloat16 [3072], P('dp'), may hold values from -3 to 3
- w_fc2: bfloat16 [3072, 768], P('dp'), may hold values from -0.109375 to 0.109375
- b_fc2: bfloat16 [768], P('dp'), may hold values from -1.75 to 1.75
- cotangent: bfloat16 [16, 1500, 768], P('dp', 'seq'), may hold values from -6 to 6
Outputs:
- frames_out: bfloat16 [16, 1500, 768], P('dp', 'seq')
- grad_frames: float32 [16, 1500, 768], P('dp', 'seq')
- grad_ln1_gain: float32 [768], P('dp')
- grad_ln1_bias: float32 [768], P('dp')
- grad_w_qkv: float32 [768, 2304], P('dp')
- grad_b_qv: float32 [1536], P('dp')
- grad_w_o: float32 [768, 768], P('dp')
- grad_b_o: float32 [768], P('dp')
- grad_ln2_gain: float32 [768], P('dp')
- grad_ln2_bias: float32 [768], P('dp')
- grad_w_fc1: float32 [768, 3072], P('dp')
- grad_b_fc1: float32 [3072], P('dp')
- grad_w_fc2: float32 [3072, 768], P('dp')
- grad_b_fc2: float32 [768], P('dp')
All inputs are finite; a program needn't handle non-finite values.
Results may differ from a plain program's by a relative error of at most 0.0095.
Values may be sent and summed in bfloat16 or wider, within the bound.
No kernel may reach another device: no remote copies, remote signals or barrier semaphores. Data moves between devices by JAX's collectives and lax.ppermute only.
A program may use at most 192 MiB of HBM per device.

v0:
```python
import math

import jax
import jax.numpy as jnp
from jax import lax
from jax.sharding import PartitionSpec as P

HEADS = 12


EPSILON = 1e-05


def normalize(values, gain, shift):
    center = jnp.mean(values, axis=-1, keepdims=True)
    centered = values - center
    variance = jnp.mean(centered * centered, axis=-1, keepdims=True)
    inverse = lax.rsqrt(variance + EPSILON)
    normed = centered * inverse
    return (normed, inverse, normed * gain + shift)


def norm_back(grad_out, normed, inverse, gain):
    weighted = grad_out * gain
    first = jnp.mean(weighted, axis=-1, keepdims=True)
    second = jnp.mean(weighted * normed, axis=-1, keepdims=True)
    return inverse * (weighted - first - normed * second)


def gelu_cdf(values):
    return 0.5 * (1.0 + lax.erf(values * (1.0 / math.sqrt(2.0))))


def gelu_slope(values):
    density = jnp.exp(-0.5 * values * values) * (1.0 / math.sqrt(2.0 * math.pi))
    return gelu_cdf(values) + values * density


def head_forward(operands):
    query, key_rows, value_rows = operands
    factor = 1.0 / math.sqrt(query.shape[-1])
    scores = jnp.dot(query, key_rows.T, preferred_element_type=jnp.float32) * factor
    row_peak = jnp.max(scores, axis=-1, keepdims=True)
    row_total = jnp.sum(jnp.exp(scores - row_peak), axis=-1, keepdims=True)
    logsum = row_peak + jnp.log(row_total)
    weights_low = jnp.exp(scores - logsum).astype(jnp.bfloat16)
    context = jnp.dot(weights_low, value_rows, preferred_element_type=jnp.float32).astype(
        jnp.bfloat16
    )
    return (context, logsum[:, 0])


def head_backward(operands):
    query, key_rows, value_rows, context, grad_context, logsum = operands
    factor = 1.0 / math.sqrt(query.shape[-1])
    scores = jnp.dot(query, key_rows.T, preferred_element_type=jnp.float32) * factor
    weights_full = jnp.exp(scores - logsum[:, None])
    weights_low = weights_full.astype(jnp.bfloat16)
    grad_values = jnp.dot(weights_low.T, grad_context, preferred_element_type=jnp.float32).astype(
        jnp.bfloat16
    )
    grad_weights = jnp.dot(grad_context, value_rows.T, preferred_element_type=jnp.float32)
    delta = jnp.sum(
        grad_context.astype(jnp.float32) * context.astype(jnp.float32), axis=-1, keepdims=True
    )
    grad_scores = (weights_full * (grad_weights - delta)).astype(jnp.bfloat16)
    grad_query = (
        jnp.dot(grad_scores, key_rows, preferred_element_type=jnp.float32) * factor
    ).astype(jnp.bfloat16)
    grad_keys = (jnp.dot(grad_scores.T, query, preferred_element_type=jnp.float32) * factor).astype(
        jnp.bfloat16
    )
    return (grad_query, grad_keys, grad_values)


def to_heads(block, head_size):
    clip_count, frame_count, group_width = block.shape
    split = block.reshape(clip_count, frame_count, group_width // head_size, head_size)
    return split.transpose(0, 2, 1, 3).reshape(
        clip_count * (group_width // head_size), frame_count, head_size
    )


def from_heads(block, clip_count):
    stacked, frame_count, head_size = block.shape
    group_heads = stacked // clip_count
    joined = block.reshape(clip_count, group_heads, frame_count, head_size).transpose(0, 2, 1, 3)
    return joined.reshape(clip_count, frame_count, group_heads * head_size)


def shards(
    frames_in,
    ln1_gain,
    ln1_bias,
    w_qkv,
    b_qv,
    w_o,
    b_o,
    ln2_gain,
    ln2_bias,
    w_fc1,
    b_fc1,
    w_fc2,
    b_fc2,
    cotangent,
):
    clip_count, local_frames, features = frames_in.shape
    head_size = features // HEADS
    token_rows = clip_count * local_frames
    shape_local = (clip_count, local_frames, features)
    attn_full = (
        lax.all_gather(w_qkv, "dp", axis=0, tiled=True),
        lax.all_gather(w_o, "dp", axis=0, tiled=True),
        lax.all_gather(ln1_gain, "dp", axis=0, tiled=True),
        lax.all_gather(ln1_bias, "dp", axis=0, tiled=True),
        lax.all_gather(b_qv, "dp", axis=0, tiled=True),
        lax.all_gather(b_o, "dp", axis=0, tiled=True),
    )
    qkv_full, out_full, gain_low_one, shift_low_one, bias_qv_low, bias_out_low = attn_full
    gain_one = gain_low_one.astype(jnp.float32)
    shift_one = shift_low_one.astype(jnp.float32)
    bias_wide = bias_qv_low.astype(jnp.float32)
    bias_out = bias_out_low.astype(jnp.float32)
    inputs = frames_in.reshape(token_rows, features).astype(jnp.float32)
    normed_one, inverse_one, hidden_one = normalize(inputs, gain_one, shift_one)
    hidden_one = hidden_one.astype(jnp.bfloat16)
    projected = jnp.dot(hidden_one, qkv_full, preferred_element_type=jnp.float32)
    query = (projected[:, :features] + bias_wide[:features]).astype(jnp.bfloat16)
    key_rows = projected[:, features : 2 * features].astype(jnp.bfloat16)
    value_rows = (projected[:, 2 * features :] + bias_wide[features:]).astype(jnp.bfloat16)
    query_group, key_group, value_group = (
        lax.all_to_all(query.reshape(shape_local), "seq", split_axis=2, concat_axis=1, tiled=True),
        lax.all_to_all(
            key_rows.reshape(shape_local), "seq", split_axis=2, concat_axis=1, tiled=True
        ),
        lax.all_to_all(
            value_rows.reshape(shape_local), "seq", split_axis=2, concat_axis=1, tiled=True
        ),
    )
    query_heads = to_heads(query_group, head_size)
    key_heads = to_heads(key_group, head_size)
    value_heads = to_heads(value_group, head_size)
    context_heads, logsum = lax.map(head_forward, (query_heads, key_heads, value_heads))
    context_heads = lax.optimization_barrier(context_heads)
    context = lax.all_to_all(
        from_heads(context_heads, clip_count), "seq", split_axis=1, concat_axis=2, tiled=True
    )
    context = context.reshape(token_rows, features)
    residual = inputs + jnp.dot(context, out_full, preferred_element_type=jnp.float32) + bias_out
    mlp_full = (
        lax.all_gather(w_fc1, "dp", axis=0, tiled=True),
        lax.all_gather(w_fc2, "dp", axis=0, tiled=True),
        lax.all_gather(ln2_gain, "dp", axis=0, tiled=True),
        lax.all_gather(ln2_bias, "dp", axis=0, tiled=True),
        lax.all_gather(b_fc1, "dp", axis=0, tiled=True),
        lax.all_gather(b_fc2, "dp", axis=0, tiled=True),
    )
    fc1_full, fc2_full, gain_low_two, shift_low_two, bias_fc1_low, bias_fc2_low = mlp_full
    gain_two = gain_low_two.astype(jnp.float32)
    shift_two = shift_low_two.astype(jnp.float32)
    normed_two, inverse_two, hidden_two = normalize(residual, gain_two, shift_two)
    hidden_two = hidden_two.astype(jnp.bfloat16)
    pre_act = jnp.dot(
        hidden_two, fc1_full, preferred_element_type=jnp.float32
    ) + bias_fc1_low.astype(jnp.float32)
    activated = (pre_act * gelu_cdf(pre_act)).astype(jnp.bfloat16)
    output = (
        residual
        + jnp.dot(activated, fc2_full, preferred_element_type=jnp.float32)
        + bias_fc2_low.astype(jnp.float32)
    )
    frames_out = output.astype(jnp.bfloat16).reshape(shape_local)
    grad_low = cotangent.reshape(token_rows, features)
    grad_full = grad_low.astype(jnp.float32)
    grad_bias_fc2 = jnp.sum(grad_full, axis=0)
    grad_weight_fc2 = jnp.dot(activated.T, grad_low, preferred_element_type=jnp.float32)
    grad_pre = jnp.dot(grad_low, fc2_full.T, preferred_element_type=jnp.float32) * gelu_slope(
        pre_act
    )
    grad_bias_fc1 = jnp.sum(grad_pre, axis=0)
    grad_pre_low = grad_pre.astype(jnp.bfloat16)
    grad_weight_fc1 = jnp.dot(hidden_two.T, grad_pre_low, preferred_element_type=jnp.float32)
    grad_hidden_two = jnp.dot(grad_pre_low, fc1_full.T, preferred_element_type=jnp.float32)
    grad_gain_two = jnp.sum(grad_hidden_two * normed_two, axis=0)
    grad_shift_two = jnp.sum(grad_hidden_two, axis=0)
    grad_residual = grad_full + norm_back(grad_hidden_two, normed_two, inverse_two, gain_two)
    mlp_terms = (
        grad_weight_fc1,
        grad_weight_fc2,
        grad_gain_two,
        grad_shift_two,
        grad_bias_fc1,
        grad_bias_fc2,
    )
    mlp_summed = lax.psum(
        (mlp_terms[0], mlp_terms[1], mlp_terms[2], mlp_terms[3], mlp_terms[4], mlp_terms[5]), "seq"
    )
    mlp_grads = (
        lax.psum_scatter(mlp_summed[0], "dp", scatter_dimension=0, tiled=True),
        lax.psum_scatter(mlp_summed[1], "dp", scatter_dimension=0, tiled=True),
        lax.psum_scatter(mlp_summed[2], "dp", scatter_dimension=0, tiled=True),
        lax.psum_scatter(mlp_summed[3], "dp", scatter_dimension=0, tiled=True),
        lax.psum_scatter(mlp_summed[4], "dp", scatter_dimension=0, tiled=True),
        lax.psum_scatter(mlp_summed[5], "dp", scatter_dimension=0, tiled=True),
    )
    grad_bias_out = jnp.sum(grad_residual, axis=0)
    grad_residual_low = grad_residual.astype(jnp.bfloat16)
    grad_weight_out = jnp.dot(context.T, grad_residual_low, preferred_element_type=jnp.float32)
    grad_context = jnp.dot(
        grad_residual_low, out_full.T, preferred_element_type=jnp.float32
    ).astype(jnp.bfloat16)
    grad_context_group = lax.all_to_all(
        grad_context.reshape(shape_local), "seq", split_axis=2, concat_axis=1, tiled=True
    )
    back_heads = lax.map(
        head_backward,
        (
            query_heads,
            key_heads,
            value_heads,
            context_heads,
            to_heads(grad_context_group, head_size),
            logsum,
        ),
    )
    grad_query_back, grad_keys_back, grad_values_back = (
        lax.all_to_all(
            from_heads(back_heads[0], clip_count), "seq", split_axis=1, concat_axis=2, tiled=True
        ),
        lax.all_to_all(
            from_heads(back_heads[1], clip_count), "seq", split_axis=1, concat_axis=2, tiled=True
        ),
        lax.all_to_all(
            from_heads(back_heads[2], clip_count), "seq", split_axis=1, concat_axis=2, tiled=True
        ),
    )
    grad_query = grad_query_back.reshape(token_rows, features)
    grad_keys = grad_keys_back.reshape(token_rows, features)
    grad_values = grad_values_back.reshape(token_rows, features)
    grad_bias_qv = jnp.concatenate(
        [
            jnp.sum(grad_query.astype(jnp.float32), axis=0),
            jnp.sum(grad_values.astype(jnp.float32), axis=0),
        ]
    )
    grad_projected = jnp.concatenate([grad_query, grad_keys, grad_values], axis=1)
    grad_weight_qkv = jnp.dot(hidden_one.T, grad_projected, preferred_element_type=jnp.float32)
    grad_hidden_one = jnp.dot(grad_projected, qkv_full.T, preferred_element_type=jnp.float32)
    grad_gain_one = jnp.sum(grad_hidden_one * normed_one, axis=0)
    grad_shift_one = jnp.sum(grad_hidden_one, axis=0)
    grad_input = grad_residual + norm_back(grad_hidden_one, normed_one, inverse_one, gain_one)
    attn_terms = (
        grad_weight_qkv,
        grad_weight_out,
        grad_gain_one,
        grad_shift_one,
        grad_bias_qv,
        grad_bias_out,
    )
    attn_summed = lax.psum(
        (attn_terms[0], attn_terms[1], attn_terms[2], attn_terms[3], attn_terms[4], attn_terms[5]),
        "seq",
    )
    attn_grads = (
        lax.psum_scatter(attn_summed[0], "dp", scatter_dimension=0, tiled=True),
        lax.psum_scatter(attn_summed[1], "dp", scatter_dimension=0, tiled=True),
        lax.psum_scatter(attn_summed[2], "dp", scatter_dimension=0, tiled=True),
        lax.psum_scatter(attn_summed[3], "dp", scatter_dimension=0, tiled=True),
        lax.psum_scatter(attn_summed[4], "dp", scatter_dimension=0, tiled=True),
        lax.psum_scatter(attn_summed[5], "dp", scatter_dimension=0, tiled=True),
    )
    return (
        frames_out,
        grad_input.reshape(shape_local),
        attn_grads[2],
        attn_grads[3],
        attn_grads[0],
        attn_grads[4],
        attn_grads[1],
        attn_grads[5],
        mlp_grads[2],
        mlp_grads[3],
        mlp_grads[0],
        mlp_grads[4],
        mlp_grads[1],
        mlp_grads[5],
    )


def solution(mesh):
    in_specs = (
        P("dp", "seq", None),
        P("dp"),
        P("dp"),
        P("dp", None),
        P("dp"),
        P("dp", None),
        P("dp"),
        P("dp"),
        P("dp"),
        P("dp", None),
        P("dp"),
        P("dp", None),
        P("dp"),
        P("dp", "seq", None),
    )
    out_specs = (
        P("dp", "seq", None),
        P("dp", "seq", None),
        P("dp"),
        P("dp"),
        P("dp", None),
        P("dp"),
        P("dp", None),
        P("dp"),
        P("dp"),
        P("dp"),
        P("dp", None),
        P("dp"),
        P("dp", None),
        P("dp"),
    )
    return jax.shard_map(shards, mesh=mesh, in_specs=in_specs, out_specs=out_specs, check_vma=False)
```

profile of v0, /device:TPU:0, one launch (start us, length us, event | category | flops | bytes accessed | tf_op | source)
XLA Modules:
  0.0 1038.6 jit_solution(15430332601258797024)
XLA Ops:
  19.4 64.0 %all-reduce.19 = (bf16[1536]{0:T(1024)(128)(2,1)S(1)}, bf16[768]{0:T(1024)(128)(2,1)S(1)}, bf16[768]{0:T(1024)(128)(2,1)S(1)}, bf16[768]{0:T(1024)(128)(2,1)S(1)...) all-reduce(bf16[1536]{0:T(1024)(128)(2,1)S(1)} %dynamic-update-slic, ...), channel_id=1, replica_groups=mesh['dp'=16,'seq'=2] {'dp'}, use_global_device_ids=true, to_apply=%add.2 | all-reduce | flops 9216 | bytes 36864
  99.0 9.1 reduce.13
  122.0 9.1 reduce.15
  146.3 9.1 reduce.14
  164.6 5.4 reshape.283
  213.2 42.6 %while.26 = (s32[]{:T(128)}, bf16[6,1500,64]{1,2,0:T(8,128)(2,1)}, f32[6,1500]{1,0:T(8,128)S(1)}, bf16[6,1500,64]{2,1,0:T(8,128)(2,1)S(1)}, bf16[6,1500,64]{2,1,...) while((s32[]{:T(128)}, bf16[6,1500,64]{1,2,0:T(8,128)(2,1)}, ...), condition=%wide.region_5.6_spmd, body=%wide.region_2.5_spmd.sunk | while | flops 589594496 | bytes 28419816 | solution.py:143
  255.8 6.6 copy.85
  262.4 10.9 %reduce.16 = bf16[1500,384]{1,0:T(8,128)(2,1)} reduce(bf16[1500,1,384]{2,1,0:T(2,128)(2,1)} %bitcast.268, bf16[]{:T(256)} %broadcast.144), dimensions={1}, to_apply=%bitcast.180.reduce_sub_computation | reduce | bytes 2304002
  281.6 10.9 %all-to-all-done.3 = bf16[2,2,144000]{2,1,0:T(2,128)(2,1)} async-done(((bf16[2,2,144000]{2,1,0:T(2,128)(2,1)}), bf16[2,2,144000]{2,1,0:T(2,128)(2,1)}, u32[]{:S(2)}, u32[]{:S(2)}) %all-to-all-start.3) | async-done | bytes 1152032 | tf_op jit(solution)/shard_map/all_to_all | solution.py:145
  292.5 5.7 reshape.289
  298.1 10.9 %bitcast_reduce_fusion.3 = bf16[1500,384]{1,0:T(8,128)(2,1)} fusion(bf16[1500,1,384]{2,1,0:T(2,128)(2,1)} %reshape.289), kind=kLoop, calls=%fused_computation.142 | loop fusion | bytes 2304000 | tf_op jit(solution)/shard_map/all_to_all | solution.py:145
  318.6 10.8 %multiply_convert_fusion = (bf16[750,3072]{1,0:T(8,128)(2,1)}, f32[750,3072]{1,0:T(8,128)}) fusion(f32[3072]{0:T(1024)S(1)} %convert_element_type.111, bf16[768,3072]{1,0:T(8,128)(2,1)} %all-gather.9.cloned.1.call-done, f32[750,768]{1,0:T(8,128)} %copy-done, f32[768]{0:T(1024)S(1)} %convert_element_type.109, f32[768]{0:T(1024)S(1)} %convert_element_type.108, ...), kind=kOutput, calls=%fused_computation.62 | convolution fusion | flops 3555648000 | bytes 20871024 | tf_op jit(solution)/shard_map/dot_general | solution.py:163
  329.5 10.2 fusion.96
  353.5 9.1 reduce.17
  393.2 93.8 %while.27 = (s32[]{:T(128)}, bf16[6,1500,64]{1,2,0:T(8,128)(2,1)}, bf16[6,1500,64]{1,2,0:T(8,128)(2,1)}, bf16[6,1500,64]{1,2,0:T(8,128)(2,1)}, bf16[6,1500,64]{2...) while((s32[]{:T(128)}, bf16[6,1500,64]{1,2,0:T(8,128)(2,1)}, ...), condition=%wide.region_12.13_spmd, body=%wide.region_10.12_spmd.sunk | while | flops 1454362368 | bytes 45485876 | solution.py:215
  487.0 6.8 copy.94
  493.8 10.0 reduce.20
  516.3 9.9 reduce.19
  538.7 8.8 reduce.18
  559.1 10.1 bitcast_reduce_fusion
  576.6 9.9 bitcast_reduce_fusion.1
  594.0 9.9 bitcast_reduce_fusion.2
  607.3 8.3 fusion.72
  617.3 8.9 fusion.68
  626.3 10.9 %fusion.79 = f32[3072,768]{1,0:T(8,128)} fusion(bf16[750,3072]{1,0:T(8,128)(2,1)} %get-tuple-element.303, bf16[1,750,768]{2,1,0:T(8,128)(2,1)} %param.31), kind=kOutput, calls=%fused_computation.114 | convolution fusion | flops 3538944000 | bytes 15197184 | tf_op jit(solution)/shard_map/dot_general | solution.py:176
  639.4 9.1 fusion.75
  650.3 60.8 %reduce-scatter.5.cloned.1.call-done = f32[48,2304]{1,0:T(8,128)} async-done(((f32[768,2304]{1,0:T(8,128)}), f32[48,2304]{1,0:T(8,128)}) %reduce-scatter.5.cloned.1.call-update) | async-done | bytes 442384 | tf_op jit(solution)/shard_map/reduce_scatter | solution.py:265
  711.1 115.0 %reduce-scatter.9.cloned.1.call-done = f32[48,3072]{1,0:T(8,128)} async-done(((f32[768,3072]{1,0:T(8,128)}), f32[48,3072]{1,0:T(8,128)}) %reduce-scatter.9.cloned.1.call-update) | async-done | bytes 589840 | tf_op jit(solution)/shard_map/reduce_scatter | solution.py:199
  826.2 115.0 %reduce-scatter.11.cloned.1.call-done = f32[192,768]{1,0:T(8,128)} async-done(((f32[3072,768]{1,0:T(8,128)}), f32[192,768]{1,0:T(8,128)}) %reduce-scatter.11.cloned.1.call-update) | async-done | bytes 589840 | tf_op jit(solution)/shard_map/reduce_scatter | solution.py:200
  941.3 7.9 fusion.63
  949.3 60.9 %all-reduce.16 = (f32[768]{0:T(1024)S(1)}, f32[768]{0:T(1024)}, f32[1536]{0:T(1024)S(1)}, f32[768]{0:T(1024)}, f32[768]{0:T(1024)}, /*index=5*/f32[768]{0:T(1024)}, f32[3072]{0:T(1024)S(1)}, f32[768]{0:T(1024)}) all-reduce(f32[768]{0:T(1024)S(1)} %get-tuple-element.222, ...), channel_id=2, replica_groups=mesh['dp'=16,'seq'=2] {'dp'}, use_global_device_ids=true, to_apply=%region_17.18.clone | all-reduce | flops 9216 | bytes 73728
  1020.1 5.5 all-reduce.17
  (310 shorter events, 380.2 us)
Async XLA Ops:
  7.2 77.7 %copy-start.4 = (bf16[1,750,768]{2,1,0:T(8,128)(2,1)S(1)}, bf16[1,750,768]{2,1,0:T(8,128)(2,1)}, u32[]{:S(2)}) copy-start(bf16[1,750,768]{2,1,0:T(8,128)(2,1)} %param.18) | copy-start | bytes 3456004
  7.2 78.3 %all-gather.5.cloned.1.call-start = ((), (), s32[]{:S(2)}) async-start(), calls=%async_computation.12 | async-start | bytes 3760128 | tf_op jit(solution)/shard_map/all_gather | solution.py:112
  7.9 306.0 %all-gather.7.cloned.1.call-start = ((), (), s32[]{:S(2)}) async-start(), calls=%async_computation.13 | async-start | bytes 1253376 | tf_op jit(solution)/shard_map/all_gather | solution.py:113
  8.7 309.9 %all-gather.9.cloned.1.call-start = ((), (), s32[]{:S(2)}) async-start(), calls=%async_computation.14 | async-start | bytes 5013504 | tf_op jit(solution)/shard_map/all_gather | solution.py:151
  83.4 7.2 copy-start.25
  112.7 22.6 %all-to-all-start = ((bf16[2,2,144000]{2,1,0:T(2,128)(2,1)}), bf16[2,2,144000]{2,1,0:T(2,128)(2,1)}, u32[]{:S(2)}, u32[]{:S(2)}) async-start(bf16[2,2,144000]{2,1,0:T(2,128)(2,1)} %reshape.282), calls=%async_computation | async-start | bytes 2304000 | tf_op jit(solution)/shard_map/all_to_all | solution.py:132
  135.2 24.3 %all-to-all-start.2 = ((bf16[2,2,144000]{2,1,0:T(2,128)(2,1)}), bf16[2,2,144000]{2,1,0:T(2,128)(2,1)}, u32[]{:S(2)}, u32[]{:S(2)}) async-start(bf16[2,2,144000]{2,1,0:T(2,128)(2,1)} %reshape.286), calls=%async_computation.2 | async-start | bytes 2304000 | tf_op jit(solution)/shard_map/all_to_all | solution.py:136
  159.6 35.1 %all-to-all-start.1 = ((bf16[2,2,144000]{2,1,0:T(2,128)(2,1)}), bf16[2,2,144000]{2,1,0:T(2,128)(2,1)}, u32[]{:S(2)}, u32[]{:S(2)}) async-start(bf16[2,2,144000]{2,1,0:T(2,128)(2,1)} %reshape.284), calls=%async_computation.1 | async-start | bytes 2304000 | tf_op jit(solution)/shard_map/all_to_all | solution.py:133
  164.0 165.4 %all-gather.11.cloned.1.call-start = ((), (), s32[]{:S(2)}) async-start(), calls=%async_computation.15 | async-start | bytes 5013504 | tf_op jit(solution)/shard_map/all_gather | solution.py:152
  277.1 15.4 %all-to-all-start.3 = ((bf16[2,2,144000]{2,1,0:T(2,128)(2,1)}), bf16[2,2,144000]{2,1,0:T(2,128)(2,1)}, u32[]{:S(2)}, u32[]{:S(2)}) async-start(bf16[2,2,144000]{2,1,0:T(2,128)(2,1)} %reshape.288), calls=%async_computation.3 | async-start | bytes 2304000 | tf_op jit(solution)/shard_map/all_to_all | solution.py:145
  318.6 10.9 %copy-start.14 = (bf16[1,750,768]{2,1,0:T(8,128)(2,1)S(1)}, bf16[1,750,768]{2,1,0:T(8,128)(2,1)}, u32[]{:S(2)}) copy-start(bf16[1,750,768]{2,1,0:T(8,128)(2,1)} %param.31) | copy-start | bytes 3456004
  329.5 10.2 copy-start.1
  329.5 10.2 copy-start.30
  367.2 13.5 %all-to-all-start.4 = ((bf16[2,2,144000]{2,1,0:T(2,128)(2,1)}), bf16[2,2,144000]{2,1,0:T(2,128)(2,1)S(1)}, u32[]{:S(2)}, u32[]{:S(2)}) async-start(bf16[2,2,144000]{2,1,0:T(2,128)(2,1)} %reshape.290), calls=%async_computation.4 | async-start | bytes 2304000 | tf_op jit(solution)/shard_map/all_to_all | solution.py:212
  370.8 279.5 %reduce-scatter.7.cloned.1.call-start = ((), (), s32[]{:S(2)}) async-start(), calls=%async_computation.17 | async-start | bytes 2506752 | tf_op jit(solution)/shard_map/reduce_scatter | solution.py:266
  503.8 8.3 copy-start.10
  507.7 22.4 %all-to-all-start.5 = ((bf16[2,2,144000]{2,1,0:T(2,128)(2,1)}), bf16[2,2,144000]{2,1,0:T(2,128)(2,1)}, u32[]{:S(2)}, u32[]{:S(2)}) async-start(bf16[2,2,144000]{2,1,0:T(2,128)(2,1)} %reshape.296), calls=%async_computation.5 | async-start | bytes 2304000 | tf_op jit(solution)/shard_map/all_to_all | solution.py:227
  526.1 8.4 copy-start.11
  530.0 24.5 %all-to-all-start.6 = ((bf16[2,2,144000]{2,1,0:T(2,128)(2,1)}), bf16[2,2,144000]{2,1,0:T(2,128)(2,1)}, u32[]{:S(2)}, u32[]{:S(2)}) async-start(bf16[2,2,144000]{2,1,0:T(2,128)(2,1)} %reshape.294), calls=%async_computation.6 | async-start | bytes 2304000 | tf_op jit(solution)/shard_map/all_to_all | solution.py:230
  554.6 34.9 %all-to-all-start.7 = ((bf16[2,2,144000]{2,1,0:T(2,128)(2,1)}), bf16[2,2,144000]{2,1,0:T(2,128)(2,1)}, u32[]{:S(2)}, u32[]{:S(2)}) async-start(bf16[2,2,144000]{2,1,0:T(2,128)(2,1)} %reshape.292), calls=%async_computation.7 | async-start | bytes 2304000 | tf_op jit(solution)/shard_map/all_to_all | solution.py:233
  559.1 152.1 %reduce-scatter.5.cloned.1.call-start = ((), (), s32[]{:S(2)}) async-start(), calls=%async_computation.16 | async-start | bytes 7520256 | tf_op jit(solution)/shard_map/reduce_scatter | solution.py:265
  605.4 10.2 copy-start.3
  615.7 210.5 %reduce-scatter.9.cloned.1.call-start = ((), (), s32[]{:S(2)}) async-start(), calls=%async_computation.18 | async-start | bytes 10027008 | tf_op jit(solution)/shard_map/reduce_scatter | solution.py:199
  626.2 315.0 %reduce-scatter.11.cloned.1.call-start = ((), (), s32[]{:S(2)}) async-start(), calls=%async_computation.19 | async-start | bytes 10027008 | tf_op jit(solution)/shard_map/reduce_scatter | solution.py:200
  637.2 388.5 %all-reduce.22.cloned.1.call-start = ((), (), s32[]{:S(2)}) async-start(), calls=%async_computation.20 | async-start | bytes 3538944 | tf_op jit(solution)/shard_map/psum | solution.py:260
  648.5 292.8 %copy-start.6 = (bf16[1,750,768]{2,1,0:T(8,128)(2,1)S(1)}, bf16[1,750,768]{2,1,0:T(8,128)(2,1)}, u32[]{:S(2)}) copy-start(bf16[1,750,768]{2,1,0:T(8,128)(2,1)} %param.18) | copy-start | bytes 3456004
  941.2 8.0 copy-start.18
  941.2 8.0 copy-start.19
  941.2 8.0 copy-start.24
  941.3 8.0 copy-start.27
  941.3 8.0 copy-start.28
  941.3 72.7 %copy-start.8 = (f32[750,768]{1,0:T(8,128)S(1)}, f32[750,768]{1,0:T(8,128)}, u32[]{:S(2)}) copy-start(f32[750,768]{1,0:T(8,128)} %copy-done.7) | copy-start | bytes 6912004
  (17 other events, 63.1 us)
Sparse Core Ops, SparseCore 0:
  10.3 50.1 all-gather.4
  62.8 36.8 all-gather.6
  101.9 51.9 all-gather.8
  166.8 50.9 all-gather.10
  375.5 62.9 reduce-scatter.6
  615.8 95.3 reduce-scatter.4
  715.2 110.9 reduce-scatter.8
  830.3 110.8 reduce-scatter.10
  943.7 55.5 all-reduce.21
where the time goes:
time: 1050 us; the launch traced here: 1040 us
  waiting for transfers between devices  310 us (30%)
  local copies, waits for them, and re-layouts  248 us (24%)
  matrix products  200 us (19%)
  blocking collectives  130 us (12%)
  other arithmetic  95.8 us (9%)
  starting transfers between devices  35.5 us (3%)
  between operations  18.6 us (2%)
    unnamed x2, blocking collectives  125 us
    reduce_scatter x1, waiting for transfers between devices, shards(): lax.psum_scatter(mlp_summed[0], 'dp', scatter_dimension=0, tiled=True)  115 us
    reduce_scatter x1, waiting for transfers between devices, shards(): lax.psum_scatter(mlp_summed[1], 'dp', scatter_dimension=0, tiled=True)  115 us
    unnamed x115, local copies, waits for them, and re-layouts  107 us
    unnamed x8, other arithmetic  76.1 us
    reduce_scatter x1, waiting for transfers between devices, shards(): lax.psum_scatter(attn_summed[0], 'dp', scatter_dimension=0, tiled=True)  60.8 us
    reshape x4, local copies, waits for them, and re-layouts, from_heads(): return joined.reshape(clip_count, frame_count, group_heads * head_size)  21.6 us
  transfers between devices with their start and end apart: 17, of which 5 were waited for; matrix products, arithmetic and copies ran while one was open for 47% of the time, Pallas kernels for 0%

commit v1 on v0

v1 whole, which is shorter than its diff:
```python
import functools
import math

import jax
import jax.numpy as jnp
from jax import lax
from jax.experimental import pallas as pl
from jax.experimental.pallas import tpu as pltpu
from jax.sharding import PartitionSpec as P

HEADS = 12
EPSILON = 1e-05
BF = jnp.bfloat16
F32 = jnp.float32
MASKED = -1e30


def dot(a, b, ca=1, cb=0):
    return lax.dot_general(a, b, (((ca,), (cb,)), ((), ())), preferred_element_type=F32)


def split3(x):
    high = x.astype(BF).astype(F32)
    rest = x - high
    mid = rest.astype(BF).astype(F32)
    return high, mid, (rest - mid).astype(BF).astype(F32)


def forward_kernel(half, valid, q_ref, k_ref, v_ref, o_ref, lse_ref, kx_ref, vt_ref):
    rows = k_ref.shape[0]
    wide = q_ref.shape[0]

    @pl.when(pl.program_id(1) == 0)
    def _():
        kx_ref[:, :128] = k_ref[...]
        row = lax.broadcasted_iota(jnp.int32, (rows, 128), 0)
        lane = lax.broadcasted_iota(jnp.int32, (rows, 128), 1)
        padded = (lax.rem(row, half) >= valid) & (lane == 0)
        kx_ref[:, 128:] = jnp.where(padded, MASKED, 0.0).astype(BF)
        vt = v_ref[...].T
        vt_ref[0:64, :] = vt[0:64, :]
        vt_ref[64:80, :] = jnp.ones((16, rows), BF)
        vt_ref[80:144, :] = vt[64:128, :]
        vt_ref[144:160, :] = jnp.ones((16, rows), BF)

    lane = lax.broadcasted_iota(jnp.int32, (wide, 128), 1)
    q = q_ref[...] * jnp.asarray(0.125, BF)
    one = jnp.where(lane == 0, 1.0, 0.0).astype(BF)
    outs, sums = [], []
    for h in range(2):
        mine = (lane < 64) if h == 0 else (lane >= 64)
        qx = jnp.concatenate([jnp.where(mine, q, jnp.zeros_like(q)), one], axis=1)
        s = dot(kx_ref[...], qx, 1, 1)
        peak = jnp.max(s, axis=0, keepdims=True)
        p = jnp.exp(s - peak).astype(BF)
        o = dot(vt_ref[80 * h : 80 * h + 80, :], p)
        total = o[64:65, :]
        outs.append(o[0:64, :] / total)
        sums.append(peak + jnp.log(total))
    o_ref[...] = jnp.concatenate(outs, axis=0).T.astype(BF)
    lse_ref[...] = jnp.concatenate(sums + [jnp.zeros((6, wide), F32)], axis=0)[None]


def attention_forward(qkv, half, valid, wide):
    rows, width = qkv.shape
    pairs = width // 3 // 128
    return pl.pallas_call(
        functools.partial(forward_kernel, half, valid),
        grid=(pairs, rows // wide),
        in_specs=[
            pl.BlockSpec((wide, 128), lambda p, i: (i, p)),
            pl.BlockSpec((rows, 128), lambda p, i: (0, pairs + p)),
            pl.BlockSpec((rows, 128), lambda p, i: (0, 2 * pairs + p)),
        ],
        out_specs=[
            pl.BlockSpec((wide, 128), lambda p, i: (i, p)),
            pl.BlockSpec((1, 8, wide), lambda p, i: (p, 0, i)),
        ],
        out_shape=[
            jax.ShapeDtypeStruct((rows, pairs * 128), BF),
            jax.ShapeDtypeStruct((pairs, 8, rows), F32),
        ],
        scratch_shapes=[pltpu.VMEM((rows, 256), BF), pltpu.VMEM((160, rows), BF)],
        cost_estimate=pl.CostEstimate(
            flops=pairs * 2 * 4 * rows * rows * 256,
            bytes_accessed=rows * width * 2 + rows * width,
            transcendentals=pairs * 2 * rows * rows,
        ),
        name="attention_forward",
    )(qkv, qkv, qkv)


def backward_kernel(
    half, valid, q_ref, k_ref, v_ref, o_ref, do_ref, lse_ref,
    dq_ref, dk_ref, dv_ref, kt_ref, vt_ref, dkt_ref, dvt_ref,
):
    rows = k_ref.shape[0]
    wide = q_ref.shape[0]

    @pl.when(pl.program_id(1) == 0)
    def _():
        kt_ref[0:128, :] = k_ref[...].T
        vt_ref[0:128, :] = v_ref[...].T
        row = lax.broadcasted_iota(jnp.int32, (128, rows), 0)
        key = lax.broadcasted_iota(jnp.int32, (128, rows), 1)
        bias = jnp.where(lax.rem(key, half) >= valid, MASKED, 0.0)
        ones = jnp.where((row >= 1) & (row < 4), 1.0, 0.0)
        kt_ref[128:256, :] = jnp.where(row == 0, bias, ones).astype(BF)
        vt_ref[128:256, :] = ones.astype(BF)
        dkt_ref[...] = jnp.zeros_like(dkt_ref)
        dvt_ref[...] = jnp.zeros_like(dvt_ref)

    lane = lax.broadcasted_iota(jnp.int32, (wide, 128), 1)
    q = q_ref[...] * jnp.asarray(0.125, BF)
    do = do_ref[...]
    product = do.astype(F32) * o_ref[...].astype(F32)
    lse = lse_ref[0].T
    qt, dot_t = q.T, do.T

    def extra(x, first):
        a, b, c = split3(-x)
        tail = jnp.where(lane == 2, b, jnp.where(lane == 3, c, 0.0))
        return jnp.where(lane == 0, first, jnp.where(lane == 1, a, tail)).astype(BF)

    dq = []
    for h in range(2):
        mine = (lane < 64) if h == 0 else (lane >= 64)
        delta = jnp.sum(jnp.where(mine, product, 0.0), axis=1, keepdims=True)
        qx = jnp.concatenate(
            [jnp.where(mine, q, jnp.zeros_like(q)), extra(lse[:, h : h + 1], 1.0)], axis=1
        )
        dx = jnp.concatenate([jnp.where(mine, do, jnp.zeros_like(do)), extra(delta, 0.0)], axis=1)
        p = jnp.exp(dot(qx, kt_ref[...]))
        low = p.astype(BF)
        ds = (p * dot(dx, vt_ref[...])).astype(BF)
        dq.append(dot(ds, k_ref[...]))
        part = slice(64 * h, 64 * h + 64)
        dkt_ref[part, :] += dot(qt[part, :], ds)
        dvt_ref[part, :] += dot(dot_t[part, :], low)
    dq_ref[...] = (jnp.where(lane < 64, dq[0], dq[1]) * 0.125).astype(BF)

    @pl.when(pl.program_id(1) == pl.num_programs(1) - 1)
    def _():
        dk_ref[...] = dkt_ref[...].T.astype(BF)
        dv_ref[...] = dvt_ref[...].T.astype(BF)


def attention_backward(qkv, o, do, lse, half, valid, wide):
    rows, width = qkv.shape
    pairs = width // 3 // 128

    def whole(part):
        return pl.BlockSpec((rows, 128), lambda p, i: (0, part * pairs + p))

    block = pl.BlockSpec((wide, 128), lambda p, i: (i, p))
    return pl.pallas_call(
        functools.partial(backward_kernel, half, valid),
        grid=(pairs, rows // wide),
        in_specs=[
            block, whole(1), whole(2), block, block,
            pl.BlockSpec((1, 8, wide), lambda p, i: (p, 0, i)),
        ],
        out_specs=[block, whole(0), whole(0)],
        out_shape=[jax.ShapeDtypeStruct((rows, pairs * 128), BF)] * 3,
        scratch_shapes=[
            pltpu.VMEM((256, rows), BF),
            pltpu.VMEM((256, rows), BF),
            pltpu.VMEM((128, rows), F32),
            pltpu.VMEM((128, rows), F32),
        ],
        cost_estimate=pl.CostEstimate(
            flops=pairs * 2 * 8 * rows * rows * 256,
            bytes_accessed=rows * width * 4,
            transcendentals=pairs * 2 * rows * rows,
        ),
        name="attention_backward",
    )(qkv, qkv, qkv, o, do, lse)


def swap(x, axis, size, bit):
    return lax.ppermute(x, axis, [(i, i ^ bit) for i in range(size)])


def bits_of(size):
    top = size // 4
    return top, [1 << b for b in range(top.bit_length() - 2, -1, -1)]


def gather_blocks(x, size):
    me = lax.axis_index("dp")
    top, bits = bits_of(size)
    held = jnp.stack([x] + [swap(x, "dp", size, j * top) for j in (1, 2, 3)])
    where = [j * top for j in range(4)]
    for bit in bits:
        held = jnp.concatenate([held, swap(held, "dp", size, bit)])
        where = where + [w ^ bit for w in where]
    place = [0] * size
    for i, w in enumerate(where):
        place[w] = i
    return jnp.take(held, jnp.asarray(place)[me ^ jnp.arange(size)], axis=0, mode="clip")


def scatter_blocks(x, size):
    me = lax.axis_index("dp")
    top, bits = bits_of(size)
    x = x.reshape(4, *[2] * len(bits), *x.shape[1:])
    for bit in reversed(bits):
        axis = 1 + bits.index(bit)
        mine = lax.rem(me // bit, 2)
        keep = lax.dynamic_index_in_dim(x, mine, axis, keepdims=False)
        give = lax.dynamic_index_in_dim(x, 1 - mine, axis, keepdims=False)
        got = swap(give.astype(BF), "dp", size, bit)
        x = keep.astype(F32) + got.astype(F32)
    mine = me // top
    total = lax.dynamic_index_in_dim(x, mine, 0, keepdims=False)
    for j in (1, 2, 3):
        give = lax.dynamic_index_in_dim(x, mine ^ j, 0, keepdims=False)
        total = total + swap(give.astype(BF), "dp", size, j * top).astype(F32)
    return total


def normalize(values):
    center = jnp.mean(values, axis=-1, keepdims=True)
    centered = values - center
    variance = jnp.mean(centered * centered, axis=-1, keepdims=True)
    inverse = lax.rsqrt(variance + EPSILON)
    return centered * inverse, inverse


def norm_back(grad_out, normed, inverse, gain):
    weighted = grad_out * gain
    first = jnp.mean(weighted, axis=-1, keepdims=True)
    second = jnp.mean(weighted * normed, axis=-1, keepdims=True)
    return inverse * (weighted - first - normed * second)


def gelu_cdf(values):
    return 0.5 * (1.0 + lax.erf(values * (1.0 / math.sqrt(2.0))))


def gelu_slope(values):
    density = jnp.exp(-0.5 * values * values) * (1.0 / math.sqrt(2.0 * math.pi))
    return gelu_cdf(values) + values * density


def shards(
    size, frames_in, ln1_gain, ln1_bias, w_qkv, b_qv, w_o, b_o,
    ln2_gain, ln2_bias, w_fc1, b_fc1, w_fc2, b_fc2, cotangent,
):
    clips, valid, wide = frames_in.shape
    assert clips == 1
    ff = w_fc1.shape[1]
    part = w_qkv.shape[0]
    group = wide // 2
    half = -(-valid // 256) * 256
    here = lax.axis_index("seq")

    def pad(block):
        return jnp.pad(block[0], ((0, half - valid), (0, 0)))

    def other(x):
        return swap(x, "seq", 2, 1)

    def pick(x, axis, index):
        return lax.dynamic_index_in_dim(x, index, axis, keepdims=False)

    vectors = jnp.concatenate([ln1_gain, ln1_bias, b_qv, b_o, ln2_gain, ln2_bias, b_fc1, b_fc2])
    count = vectors.shape[0] // part
    columns = jnp.pad(vectors.reshape(count, part).T, ((0, 0), (0, 128 - count)))
    w_mine = pick(w_qkv.reshape(part, 3, 2, group), 2, here).reshape(part, 3 * group)
    first = gather_blocks(jnp.concatenate([w_mine, columns], axis=1), size)
    qkv_full = first[:, :, : 3 * group].reshape(wide, 3 * group)
    table = first[:, :, 3 * group : 3 * group + count].transpose(2, 0, 1).astype(F32)

    def vector(start, stop):
        return table[start:stop].transpose(1, 0, 2).reshape(-1)

    per = ff // wide
    gain_one, shift_one = vector(0, 1), vector(1, 2)
    bias_qv, bias_out = vector(2, 4), vector(4, 5)
    gain_two, shift_two = vector(5, 6), vector(6, 7)
    bias_fc1, bias_fc2 = vector(7, 7 + per), vector(7 + per, 8 + per)
    second = lax.all_gather(jnp.concatenate([w_o, w_fc1], axis=1), "dp", axis=0, tiled=True)
    out_full, fc1_full = second[:, :wide], second[:, wide:]
    fc2_full = lax.all_gather(w_fc2, "dp", axis=0, tiled=True)

    own = pad(frames_in)
    both = jnp.concatenate([own, other(own)], axis=0).astype(F32)
    normed_both, inverse_both = normalize(both)
    hidden_one = (normed_both * gain_one + shift_one).astype(BF)
    bias_mine = pick(bias_qv.reshape(2, 2, group), 1, here)
    bias_row = jnp.concatenate([bias_mine[0], jnp.zeros((group,), F32), bias_mine[1]])
    qkv = (dot(hidden_one, qkv_full) + bias_row).astype(BF)
    o, lse = attention_forward(qkv, half, valid, 512)
    o_got = other(o[half:])
    o_own = o[:half]
    context = jnp.where(
        here == 0,
        jnp.concatenate([o_own, o_got], axis=1),
        jnp.concatenate([o_got, o_own], axis=1),
    )
    residual = both[:half] + dot(context, out_full) + bias_out

    normed_two, inverse_two = normalize(residual)
    hidden_two = (normed_two * gain_two + shift_two).astype(BF)
    pre_act = dot(hidden_two, fc1_full) + bias_fc1
    activated = (pre_act * gelu_cdf(pre_act)).astype(BF)
    output = residual + dot(activated, fc2_full) + bias_fc2
    frames_out = output.astype(BF)[:valid][None]
    grad_low = pad(cotangent)
    grad_full = grad_low.astype(F32)
    grad_bias_fc2 = jnp.sum(grad_full, axis=0)
    grad_fc2 = dot(activated, grad_low, 0, 0).astype(BF)
    grad_pre = dot(grad_low, fc2_full, 1, 1) * gelu_slope(pre_act)
    grad_bias_fc1 = jnp.sum(grad_pre, axis=0)
    grad_pre_low = grad_pre.astype(BF)
    grad_fc1 = dot(hidden_two, grad_pre_low, 0, 0).astype(BF)
    grad_hidden_two = dot(grad_pre_low, fc1_full, 1, 1)
    grad_gain_two = jnp.sum(grad_hidden_two * normed_two, axis=0)
    grad_shift_two = jnp.sum(grad_hidden_two, axis=0)
    grad_residual = grad_full + norm_back(grad_hidden_two, normed_two, inverse_two, gain_two)
    grad_bias_out = jnp.sum(grad_residual, axis=0)
    grad_residual_low = grad_residual.astype(BF)
    grad_out = dot(context, grad_residual_low, 0, 0).astype(BF)
    grad_context = dot(grad_residual_low, out_full, 1, 1).astype(BF)
    grad_second = lax.psum_scatter(
        jnp.concatenate([grad_out, grad_fc1], axis=1), "dp", scatter_dimension=0, tiled=True
    )
    grad_fc2 = lax.psum_scatter(grad_fc2, "dp", scatter_dimension=0, tiled=True)

    left, right = grad_context[:, :group], grad_context[:, group:]
    do_got = other(jnp.where(here == 0, right, left))
    do = jnp.concatenate([jnp.where(here == 0, left, right), do_got], axis=0)
    dqkv = jnp.concatenate(attention_backward(qkv, o, do, lse, half, valid, 512), axis=1)
    grad_hidden_other = dot(dqkv[half:], qkv_full, 1, 1)
    grad_got = other(grad_hidden_other.astype(BF))
    grad_hidden_mine = dot(dqkv[:half], qkv_full, 1, 1)
    grad_qkv = dot(hidden_one, dqkv, 0, 0)
    sums = jnp.sum(dqkv.astype(F32), axis=0).reshape(3, group)
    grad_bias_mine = jnp.stack([sums[0], sums[2]])
    zero = jnp.zeros_like(grad_bias_mine)
    grad_bias_qv = jnp.where(
        here == 0,
        jnp.concatenate([grad_bias_mine, zero], axis=1),
        jnp.concatenate([zero, grad_bias_mine], axis=1),
    ).reshape(-1)
    grad_both = jnp.concatenate([grad_hidden_mine, grad_hidden_other], axis=0)
    grad_gain_one = jnp.sum(grad_both * normed_both, axis=0)
    grad_shift_one = jnp.sum(grad_both, axis=0)
    grad_hidden_one = grad_hidden_mine + grad_got.astype(F32)
    grad_input = grad_residual + norm_back(
        grad_hidden_one, normed_both[:half], inverse_both[:half], gain_one
    )

    grad_vectors = [
        grad_gain_one, grad_shift_one, grad_bias_qv, grad_bias_out,
        grad_gain_two, grad_shift_two, grad_bias_fc1, grad_bias_fc2,
    ]
    rows = jnp.concatenate([v.reshape(size, -1, part) for v in grad_vectors], axis=1)
    columns = jnp.pad(rows.transpose(0, 2, 1), ((0, 0), (0, 0), (0, 128 - count)))
    mine = scatter_blocks(
        jnp.concatenate([grad_qkv.reshape(size, part, 3 * group), columns], axis=2), size
    ).astype(BF)
    theirs = other(mine)
    low = jnp.where(here == 0, mine, theirs)[:, : 3 * group].reshape(part, 3, 1, group)
    high = jnp.where(here == 0, theirs, mine)[:, : 3 * group].reshape(part, 3, 1, group)
    grad_w_qkv = jnp.concatenate([low, high], axis=2).reshape(part, 6 * group).astype(F32)
    small = mine[:, 3 * group :].astype(F32) + theirs[:, 3 * group :].astype(F32)
    small = small[:, :count].T

    def piece(start, stop):
        return small[start:stop].reshape(-1)

    second_sum = grad_second.astype(F32) + other(grad_second).astype(F32)
    fc2_sum = grad_fc2.astype(F32) + other(grad_fc2).astype(F32)
    return (
        frames_out,
        grad_input[:valid][None],
        piece(0, 1),
        piece(1, 2),
        grad_w_qkv,
        piece(2, 4),
        second_sum[:, :wide],
        piece(4, 5),
        piece(5, 6),
        piece(6, 7),
        second_sum[:, wide:],
        piece(7, 7 + per),
        fc2_sum,
        piece(7 + per, 8 + per),
    )


def solution(mesh):
    frames, rows, vector = P("dp", "seq", None), P("dp", None), P("dp")
    in_specs = (
        frames, vector, vector, rows, vector, rows, vector,
        vector, vector, rows, vector, rows, vector, frames,
    )
    out_specs = (
        frames, frames, vector, vector, rows, vector, rows, vector,
        vector, vector, rows, vector, rows, vector,
    )
    return jax.shard_map(
        functools.partial(shards, mesh.shape["dp"]),
        mesh=mesh, in_specs=in_specs, out_specs=out_specs, check_vma=False,
    )
```

time: 1050 us -> 354 us (0.34)
  waiting for transfers between devices: 310 us -> 65.9 us
  local copies, waits for them, and re-layouts: 248 us -> 57.6 us
  blocking collectives: 130 us -> 0 us
  matrix products: 200 us -> 82.7 us
  Pallas kernels: 0 us -> 71.7 us
  other arithmetic: 95.8 us -> 32.8 us
  starting transfers between devices: 35.5 us -> 22.5 us
    reduce_scatter x4 -> x2, waiting for transfers between devices: 291 us -> 0.04 us  [the longest x1 0.02 us: shards(): grad_fc2 = lax.psum_scatter(grad_fc2, 'dp', scatter_dimension=0, tiled=True)]
    unnamed x2 -> x0, blocking collectives: 125 us -> none
    dot_general x54 -> x13, matrix products: 200 us -> 82.7 us  [dot(): lax.dot_general(a, b, (((ca,), (cb,)), ((), ())), preferred_element_type=...]
    unnamed x115 -> x98, local copies, waits for them, and re-layouts: 107 us -> 14.6 us
    unnamed x8 -> x2, other arithmetic: 76.1 us -> 0.71 us
    pallas_call x0 -> x2, Pallas kernels: none -> 71.7 us  [the longest x1 42.7 us: attention_backward(): pl.pallas_call(functools.partial(backward_kernel, half, valid), grid=(pai...]
    ppermute x0 -> x17, waiting for transfers between devices: none -> 65.7 us  [swap(): return lax.ppermute(x, axis, [(i, i ^ bit) for i in range(size)])]
    all_to_all x16 -> x0, local copies, waits for them, and re-layouts: 61.8 us -> none  [the longest x3 15.8 us: shards(): lax.all_to_all(from_heads(context_heads, clip_count), 'seq', split_axis=1...]
  transfers between devices with their start and end apart: 17 -> 21, of which waited for: 5 -> 11; matrix products, arithmetic and copies ran while one was open for 47% -> 47% of each run, Pallas kernels for 0% -> 21%
where the time goes in v1:
time: 354 us; the launch traced here: 348 us
  matrix products  82.7 us (23%)
  Pallas kernels  71.7 us (20%)
  waiting for transfers between devices  65.9 us (19%)
  local copies, waits for them, and re-layouts  57.6 us (16%)
  other arithmetic  32.8 us (9%)
  starting transfers between devices  22.5 us (6%)
  between operations  15.1 us (4%)
    dot_general x13, matrix products, dot(): lax.dot_general(a, b, (((ca,), (cb,)), ((), ())), preferred_element_type=...  82.7 us
    ppermute x17, waiting for transfers between devices, swap(): return lax.ppermute(x, axis, [(i, i ^ bit) for i in range(size)])  65.7 us
    pallas_call x1, Pallas kernels, attention_backward(): pl.pallas_call(functools.partial(backward_kernel, half, valid), grid=(pai...  42.7 us
    pallas_call x1, Pallas kernels, attention_forward(): pl.pallas_call(functools.partial(forward_kernel, half, valid), grid=(pair...  29 us
    ppermute x17, starting transfers between devices, swap(): return lax.ppermute(x, axis, [(i, i ^ bit) for i in range(size)])  22.4 us
    unnamed x98, local copies, waits for them, and re-layouts  14.6 us
    reshape x6, local copies, waits for them, and re-layouts, shards(): v.reshape(size, -1, part)  8.18 us
  transfers between devices with their start and end apart: 21, of which 11 were waited for; matrix products, arithmetic and copies ran while one was open for 47% of the time, Pallas kernels for 21%

profile of v1, /device:TPU:0, one launch (start us, length us, event | category | flops | bytes accessed | tf_op | source)
XLA Modules:
  0.0 348.2 jit_solution(12157249644340140300)
XLA Ops:
  10.9 5.4 %concatenate.62 = bf16[576]{0:T(1024)(128)(2,1)S(1)} concatenate(bf16[48]{0:T(256)(128)(2,1)} %param.16, bf16[48]{0:T(256)(128)(2,1)} %param.17, bf16[96]{0:T(256)(128)(2,1)} %param.19, bf16[48]{0:T(256)(128)(2,1)} %param.21, bf16[48]{0:T(256)(128)(2,1)} %param.22, bf16[48]{0:T(256)(128)(2,1)} %param.23, bf16[192]{0:T(256)(128)(2,1)} %param.25, bf16[48]{0:T(256)(128)(2,1)} %param.27), dimensions={0} | concatenate | bytes 2304 | tf_op jit(solution)/shard_map/concatenate | solution.py:267
  16.5 3.1 collective-permute-start.1
  24.9 12.4 %collective-permute-done.2 = bf16[48,1280]{1,0:T(8,128)(2,1)S(1)} collective-permute-done((bf16[48,1280]{1,0:T(8,128)(2,1)S(1)}, bf16[48,1280]{1,0:T(8,128)(2,1)S(1)}, u32[]{:S(2)}, u32[]{:S(2)}) %collective-permute-start.2) | collective-permute-done | bytes 122912 | tf_op jit(solution)/shard_map/ppermute | solution.py:181
  40.6 5.7 %collective-permute-done.4 = bf16[4,48,1280]{2,1,0:T(8,128)(2,1)S(1)} collective-permute-done((bf16[4,48,1280]{2,1,0:T(8,128)(2,1)S(1)}, bf16[4,48,1280]{2,1,0:T(8,128)(2,1)S(1)}, u32[]{:S(2)}, u32[]{:S(2)}) %collective-permute-start.4) | collective-permute-done | bytes 491552 | tf_op jit(solution)/shard_map/ppermute | solution.py:181
  51.8 3.5 %gather_fusion.1 = bf16[16,48,1280]{2,1,0:T(8,128)(2,1)} fusion(bf16[16,48,1280]{2,1,0:T(8,128)(2,1)} %constant_dynamic-update-slice_fusion.5, s32[1024]{0:T(1024)S(1)} %pad_clamp_fusion), kind=kCustom, calls=%fused_computation.1 | custom fusion | bytes 3932224 | tf_op jit(solution)/shard_map/jit(_take)/gather | solution.py:200
  55.3 2.8 slice.187
  61.1 8.9 %fusion.5.q_ref.k_ref.v_ref = bf16[1536,1152]{1,0:T(8,128)(2,1)} fusion(bf16[768,1152]{1,0:T(8,128)(2,1)} %bitcast.88, f32[1152]{0:T(1024)S(1)} %pad_maximum_fusion.5, f32[768]{0:T(1024)S(1)} %add.199, f32[768]{0:T(1024)S(1)} %mul.133, f32[1536]{0:T(1024)S(1)} %add_rsqrt_fusion, f32[1536]{0:T(1024)S(1)} %broadcast_multiply_fusion, ...), kind=kOutput, calls=%fused_computation.11 | convolution fusion | flops 2732064768 | bytes 7690752 | tf_op jit(solution)/shard_map/dot_general | solution.py:19
  70.0 29.0 %attention_forward.1 = (bf16[1536,384]{1,0:T(8,128)(2,1)}, f32[3,8,1536]{2,1,0:T(8,128)}) custom-call(bf16[1536,1152]{1,0:T(8,128)(2,1)} %fusion.5.q_ref.k_ref.v_ref, bf16[1536,1152]{1,0:T(8,128)(2,1)} %fusion.5.q_ref.k_ref.v_ref, bf16[1536,1152]{1,0:T(8,128)(2,1)} %fusion.5.q_ref.k_ref.v_ref), custom_call_target="tpu_custom_call" | custom-call | flops 14495514624 | bytes 5308416 | tf_op jit(solution)/shard_map/attention_forward/pallas_call | solution.py:67
  108.2 7.8 %collective-permute-done.6 = bf16[768,384]{1,0:T(8,128)(2,1)} collective-permute-done((bf16[768,384]{1,0:T(8,128)(2,1)S(1)}, bf16[768,384]{1,0:T(8,128)(2,1)}, u32[]{:S(2)}, u32[]{:S(2)}) %collective-permute-start.6) | collective-permute-done | bytes 589856 | tf_op jit(solution)/shard_map/ppermute | solution.py:181
  116.0 4.1 %fusion.64 = (f32[768]{0:T(1024)S(1)}, f32[768,768]{1,0:T(8,128)S(1)}) fusion(f32[768]{0:T(1024)} %add.205, bf16[768,3840]{1,0:T(8,128)(2,1)} %all-gather.3.cloned.1.call-done, bf16[768,384]{1,0:T(8,128)(2,1)} %collective-permute-done.6, bf16[768,384]{1,0:T(8,128)(2,1)} %get-tuple-element.153, pred[]{:T(512)S(6)} %eq.2, f32[1536,768]{1,0:T(8,128)} %fusion.57), kind=kOutput, calls=%fused_computation.164 | convolution fusion | flops 913046784 | bytes 7085057 | tf_op jit(solution)/shard_map/dot_general | solution.py:19
  121.0 6.9 %multiply_convert_fusion = (bf16[768,3072]{1,0:T(8,128)(2,1)S(1)}, f32[768,3072]{1,0:T(8,128)}) fusion(f32[3072]{0:T(1024)S(1)} %copy-done.37, bf16[768,3840]{1,0:T(8,128)(2,1)S(1)} %bitcast.113, f32[768,768]{1,0:T(8,128)S(1)} %get-tuple-element.176, f32[768]{0:T(1024)S(1)} %copy-done.39, f32[768]{0:T(1024)S(1)} %copy-done.30, f32[768]{0:T(1024)S(1)} %add_rsqrt_fusion.1, ...), kind=kOutput, calls=%fused_computation.8 | convolution fusion | flops 3640983552 | bytes 21262336 | tf_op jit(solution)/shard_map/dot_general | solution.py:19
  130.0 5.6 %convolution_convert_fusion = bf16[3072,768]{1,0:T(8,128)(2,1)} fusion(bf16[768,3072]{1,0:T(8,128)(2,1)S(1)} %get-tuple-element.178, bf16[750,768]{1,0:T(8,128)(2,1)S(1)} %bitcast.92), kind=kOutput, calls=%fused_computation.16 | convolution fusion | flops 3626237952 | bytes 10589184 | tf_op jit(solution)/shard_map/dot_general | solution.py:19
  137.1 11.4 %fusion.65 = (f32[3072]{0:T(1024)}, bf16[768,3072]{1,0:T(8,128)(2,1)S(1)}) fusion(f32[768,3072]{1,0:T(8,128)} %get-tuple-element.179, f32[3072]{0:T(1024)} %add.213, bf16[3072,768]{1,0:T(8,128)(2,1)} %all-gather.5.cloned.1.call-done, bf16[750,768]{1,0:T(8,128)(2,1)} %bitcast.91), kind=kOutput, calls=%fused_computation.165 | convolution fusion | flops 3652187136 | bytes 20050944 | tf_op jit(solution)/shard_map/dot_general | solution.py:19
  148.6 9.4 %multiply_reduce_fusion.1 = (f32[768]{0:T(1024)}, f32[768]{0:T(1024)S(1)}, f32[768]{0:T(1024)S(1)}, f32[768]{0:T(1024)}, f32[768,768]{1,0:T(8,128)S(1)}) fusion(f32[768,768]{1,0:T(8,128)S(1)} %get-tuple-element.176, f32[768]{0:T(1024)S(1)} %copy-done.33, f32[768]{0:T(1024)S(1)} %copy-done.24, f32[768]{0:T(1024)S(1)} %copy-done.31, ...), kind=kOutput, calls=%fused_computation.35 | convolution fusion | flops 3629184000 | bytes 14177280 | tf_op jit(solution)/shard_map/dot_general | solution.py:19
  161.2 3.5 %convolution_convert_fusion.2 = bf16[768,768]{0,1:T(8,128)(2,1)} fusion(f32[768,768]{1,0:T(8,128)S(1)} %get-tuple-element.143, bf16[768,384]{1,0:T(8,128)(2,1)} %collective-permute-done.6, bf16[768,384]{1,0:T(8,128)(2,1)S(1)} %copy-done.17, pred[]{:T(512)S(6)} %eq.2), kind=kOutput, calls=%fused_computation.64 | convolution fusion | flops 912457728 | bytes 4718593 | tf_op jit(solution)/shard_map/dot_general | solution.py:19
  167.1 3.1 convolution_convert_fusion.3
  179.7 6.9 %convolution_convert_fusion.1 = bf16[768,3072]{1,0:T(8,128)(2,1)S(1)} fusion(bf16[768,3072]{1,0:T(8,128)(2,1)} %copy-done.41, f32[768,768]{1,0:T(8,128)S(1)} %get-tuple-element.176, f32[768]{0:T(1024)} %add.210, f32[768]{0:T(1024)} %mul.139, f32[768]{0:T(1024)} %copy-done.32, f32[768]{0:T(1024)} %copy-done.23), kind=kOutput, calls=%fused_computation.17 | convolution fusion | flops 3629187072 | bytes 11808768 | tf_op jit(solution)/shard_map/dot_general | solution.py:19
  186.6 2.9 pad_maximum_fusion
  192.0 42.7 %attention_backward.1 = (bf16[1536,384]{1,0:T(8,128)(2,1)}, bf16[1536,384]{1,0:T(8,128)(2,1)}, bf16[1536,384]{1,0:T(8,128)(2,1)}) custom-call(bf16[1536,1152]{1,0:T(8,128)(2,1)} %fusion.5.q_ref.k_ref.v_ref, bf16[1536,1152]{1,0:T(8,128)(2,1)} %fusion.5.q_ref.k_ref.v_ref, bf16[1536,1152]{1,0:T(8,128)(2,1)} %fusion.5.q_ref.k_ref.v_ref, ...), custom_call_target="tpu_custom_call" | custom-call | flops 28991029248 | bytes 7077888 | tf_op jit(solution)/shard_map/attention_backward/pallas_call | solution.py:156
  240.1 4.1 %fusion.61 = (f32[768]{0:T(1024)}, bf16[768,768]{1,0:T(8,128)(2,1)}, f32[768,768]{1,0:T(8,128)}) fusion(bf16[768,1152]{1,0:T(8,128)(2,1)S(1)} %bitcast.89, bf16[1536,1152]{1,0:T(8,128)(2,1)S(1)} %constant_dynamic-update-slice_fusion.11), kind=kOutput, calls=%fused_computation.161 | convolution fusion | flops 1360133376 | bytes 7080960 | tf_op jit(solution)/shard_map/dot_general | solution.py:19
  245.3 3.2 fusion.27
  249.9 6.8 %fusion.6 = (f32[768]{0:T(1024)}, f32[1536,768]{1,0:T(8,128)}) fusion(f32[768,768]{1,0:T(8,128)} %get-tuple-element.180, f32[768,768]{1,0:T(8,128)} %fusion.27, f32[1536]{0:T(1024)S(1)} %add_rsqrt_fusion, f32[1536]{0:T(1024)S(1)} %broadcast_multiply_fusion, bf16[768,768]{1,0:T(8,128)(2,1)} %copy-done.1, bf16[768,768]{1,0:T(8,128)(2,1)S(1)} %pad.17), kind=kLoop, calls=%fused_computation.19 | loop fusion | flops 10616064 | bytes 11811840 | tf_op jit(solution)/shard_map/reduce_sum | solution.py:348
  258.1 8.1 %fusion.38 = f32[768,1152]{1,0:T(8,128)} fusion(bf16[1536,1152]{1,0:T(8,128)(2,1)} %copy-done.9, f32[768]{0:T(1024)} %copy-done.38, f32[768]{0:T(1024)} %copy-done.34, f32[1536]{0:T(1024)S(1)} %add_rsqrt_fusion, f32[1536]{0:T(1024)S(1)} %broadcast_multiply_fusion, bf16[768,768]{1,0:T(8,128)(2,1)} %copy-done.1, bf16[768,768]{1,0:T(8,128)(2,1)S(1)} %pad.17), kind=kOutput, calls=%fused_computation.78 | convolution fusion | flops 2728525824 | bytes 9455616 | tf_op jit(solution)/shard_map/dot_general | solution.py:19
  266.2 5.0 %collective-permute-done.8 = bf16[768,768]{1,0:T(8,128)(2,1)} collective-permute-done((bf16[768,768]{1,0:T(8,128)(2,1)}, bf16[768,768]{1,0:T(8,128)(2,1)}, u32[]{:S(2)}, u32[]{:S(2)}) %collective-permute-start.8) | collective-permute-done | bytes 1179680 | tf_op jit(solution)/shard_map/ppermute | solution.py:181
  271.3 4.0 %fusion.59 = (f32[768]{0:T(1024)S(1)}, f32[768]{0:T(1024)S(1)}, f32[768,768]{1,0:T(8,128)}, f32[768,768]{1,0:T(8,128)}, f32[768]{0:T(1024)S(1)}) fusion(f32[1536,768]{1,0:T(8,128)S(1)} %copy-done.3, f32[768]{0:T(1024)S(1)} %copy-done.35, f32[768,768]{1,0:T(8,128)S(1)} %copy-done.4, bf16[768,768]{1,0:T(8,128)(2,1)} %collective-permute-done.8), kind=kLoop, calls=%fused_computation.159 | loop fusion | flops 4126464 | bytes 10629120 | tf_op jit(solution)/shard_map/reduce_sum | solution.py:232
  277.6 7.5 %fusion.66 = f32[768,768]{1,0:T(8,128)S(1)} fusion(bf16[768,3072]{1,0:T(8,128)(2,1)} %copy-done.42, bf16[3072,768]{1,0:T(8,128)(2,1)} %all-gather.5.cloned.1.call-done), kind=kOutput, calls=%fused_computation.166 | convolution fusion | flops 3623878656 | bytes 11796480 | tf_op jit(solution)/shard_map/dot_general | solution.py:19
  287.9 15.2 %collective-permute-done.10 = bf16[4,48,1280]{2,1,0:T(8,128)(2,1)S(1)} collective-permute-done((bf16[4,48,1280]{2,1,0:T(8,128)(2,1)S(1)}, bf16[4,48,1280]{2,1,0:T(8,128)(2,1)S(1)}, u32[]{:S(2)}, u32[]{:S(2)}) %collective-permute-start.10) | collective-permute-done | bytes 491552 | tf_op jit(solution)/shard_map/ppermute | solution.py:181
  305.9 2.9 collective-permute-start.12
  312.5 6.3 %collective-permute-done.13 = bf16[48,1280]{1,0:T(8,128)(2,1)S(1)} collective-permute-done((bf16[48,1280]{1,0:T(8,128)(2,1)S(1)}, bf16[48,1280]{1,0:T(8,128)(2,1)S(1)}, u32[]{:S(2)}, u32[]{:S(2)}) %collective-permute-start.13) | collective-permute-done | bytes 122912 | tf_op jit(solution)/shard_map/ppermute | solution.py:181
  319.5 3.8 %copy.128 = f32[1,750,768]{2,0,1:T(1,128)} copy(f32[1,750,768]{2,1,0:T(8,128)S(1)} %fusion.14) | data formatting | bytes 4608000
  330.0 4.1 %collective-permute-done.16 = bf16[192,768]{1,0:T(8,128)(2,1)S(1)} collective-permute-done((bf16[192,768]{1,0:T(8,128)(2,1)}, bf16[192,768]{1,0:T(8,128)(2,1)S(1)}, u32[]{:S(2)}, u32[]{:S(2)}) %collective-permute-start.16) | collective-permute-done | bytes 294944 | tf_op jit(solution)/shard_map/ppermute | solution.py:181
  334.9 4.7 %collective-permute-done.15 = bf16[48,3840]{1,0:T(8,128)(2,1)S(1)} collective-permute-done((bf16[48,3840]{1,0:T(8,128)(2,1)}, bf16[48,3840]{1,0:T(8,128)(2,1)S(1)}, u32[]{:S(2)}, u32[]{:S(2)}) %collective-permute-start.15) | collective-permute-done | bytes 368672 | tf_op jit(solution)/shard_map/ppermute | solution.py:181
  (232 shorter events, 82.2 us)
Async XLA Ops:
  7.2 15.1 %copy-start.16 = (bf16[1,750,768]{2,1,0:T(8,128)(2,1)S(1)}, bf16[1,750,768]{2,1,0:T(8,128)(2,1)}, u32[]{:S(2)}) copy-start(bf16[1,750,768]{2,1,0:T(8,128)(2,1)} %param.15) | copy-start | bytes 3456004
  7.2 108.8 %all-gather.3.cloned.1.call-start = ((), (), s32[]{:S(2)}) async-start(), calls=%async_computation.2 | async-start | bytes 6266880 | tf_op jit(solution)/shard_map/all_gather | solution.py:283
  9.1 128.0 %all-gather.5.cloned.1.call-start = ((), (), s32[]{:S(2)}) async-start(), calls=%async_computation.3 | async-start | bytes 5013504 | tf_op jit(solution)/shard_map/all_gather | solution.py:285
  16.5 8.4 %collective-permute-start.1 = (bf16[48,1280]{1,0:T(8,128)(2,1)S(1)}, bf16[48,1280]{1,0:T(8,128)(2,1)S(1)}, u32[]{:S(2)}, u32[]{:S(2)}) collective-permute-start(bf16[48,1280]{1,0:T(8,128)(2,1)S(1)} %get-tuple-element.172), channel_id=1, source_target_pairs={{0,8},{2,10},{4,12},{6,14},{8,0},{10,2},{12,4},{14,6},{16,24},{18,... | collective-permute-start | bytes 368648 | tf_op jit(solution)/shard_map/ppermute | solution.py:181
  19.7 17.7 %collective-permute-start.2 = (bf16[48,1280]{1,0:T(8,128)(2,1)S(1)}, bf16[48,1280]{1,0:T(8,128)(2,1)S(1)}, u32[]{:S(2)}, u32[]{:S(2)}) collective-permute-start(bf16[48,1280]{1,0:T(8,128)(2,1)S(1)} %get-tuple-element.172), channel_id=1, source_target_pairs={{0,16},{2,18},{4,20},{6,22},{8,24},{10,26},{12,28},{14,30},{16,0},... | collective-permute-start | bytes 368648 | tf_op jit(solution)/shard_map/ppermute | solution.py:181
  22.2 15.1 %collective-permute-start.3 = (bf16[48,1280]{1,0:T(8,128)(2,1)S(1)}, bf16[48,1280]{1,0:T(8,128)(2,1)S(1)}, u32[]{:S(2)}, u32[]{:S(2)}) collective-permute-start(bf16[48,1280]{1,0:T(8,128)(2,1)S(1)} %get-tuple-element.172), channel_id=1, source_target_pairs={{0,24},{2,26},{4,28},{6,30},{8,16},{10,18},{12,20},{14,22},{16,8},... | collective-permute-start | bytes 368648 | tf_op jit(solution)/shard_map/ppermute | solution.py:181
  22.3 25.0 %copy-start = (s32[16]{0:T(128)S(1)}, s32[16]{0:T(128)}, u32[]{:S(2)}) copy-start(s32[16]{0:T(128)} %constant.117.clone) | copy-start | bytes 196
  22.3 27.2 %collective-permute-start = (bf16[768,768]{1,0:T(8,128)(2,1)S(1)}, bf16[768,768]{1,0:T(8,128)(2,1)S(1)}, u32[]{:S(2)}, u32[]{:S(2)}) collective-permute-start(bf16[768,768]{1,0:T(8,128)(2,1)S(1)} %pad.17), channel_id=1, source_target_pairs={{0,1},{1,0},{2,3},{3,2},{4,5},{5,4},{6,7},{7,6},{8,9},{9,8},{10,11... | collective-permute-start | bytes 3538952 | tf_op jit(solution)/shard_map/ppermute | solution.py:181
  24.2 299.7 %reduce-scatter.5.cloned.1.call-start = ((), (), s32[]{:S(2)}) async-start(), calls=%async_computation.5 | async-start | bytes 5013504 | tf_op jit(solution)/shard_map/reduce_scatter | solution.py:329
  37.4 8.9 %collective-permute-start.4 = (bf16[4,48,1280]{2,1,0:T(8,128)(2,1)S(1)}, bf16[4,48,1280]{2,1,0:T(8,128)(2,1)S(1)}, u32[]{:S(2)}, u32[]{:S(2)}) collective-permute-start(bf16[4,48,1280]{2,1,0:T(8,128)(2,1)S(1)} %pad_maximum_fusion.3), channel_id=1, source_target_pairs={{0,4},{2,6},{4,0},{6,2},{8,12},{10,14},{12,8},{14,10},{16,20},{18,... | collective-permute-start | bytes 1474568 | tf_op jit(solution)/shard_map/ppermute | solution.py:181
  47.3 3.5 %collective-permute-start.5 = (bf16[8,48,1280]{2,1,0:T(8,128)(2,1)}, bf16[8,48,1280]{2,1,0:T(8,128)(2,1)S(1)}, u32[]{:S(2)}, u32[]{:S(2)}) collective-permute-start(bf16[8,48,1280]{2,1,0:T(8,128)(2,1)} %get-tuple-element.159), channel_id=1, source_target_pairs={{0,2},{2,0},{4,6},{6,4},{8,10},{10,8},{12,14},{14,12},{16,18},{18,... | collective-permute-start | bytes 2949128 | tf_op jit(solution)/shard_map/ppermute | solution.py:181
  49.6 53.1 %copy-start.1 = (bf16[768,768]{1,0:T(8,128)(2,1)}, bf16[768,768]{1,0:T(8,128)(2,1)S(1)}, u32[]{:S(2)}) copy-start(bf16[768,768]{1,0:T(8,128)(2,1)S(1)} %collective-permute-done) | copy-start | bytes 3538948
  50.8 207.3 %copy-start.22 = (f32[1536]{0:T(1024)}, f32[1536]{0:T(1024)S(1)}, u32[]{:S(2)}) copy-start(f32[1536]{0:T(1024)S(1)} %add_rsqrt_fusion) | copy-start | bytes 18436
  101.2 14.9 %collective-permute-start.6 = (bf16[768,384]{1,0:T(8,128)(2,1)S(1)}, bf16[768,384]{1,0:T(8,128)(2,1)}, u32[]{:S(2)}, u32[]{:S(2)}) collective-permute-start(bf16[768,384]{1,0:T(8,128)(2,1)S(1)} %get-tuple-element.154), channel_id=1, source_target_pairs={{0,1},{1,0},{2,3},{3,2},{4,5},{5,4},{6,7},{7,6},{8,9},{9,8},{10,11... | collective-permute-start | bytes 1769480 | tf_op jit(solution)/shard_map/ppermute | solution.py:181
  135.7 190.3 %reduce-scatter.3.cloned.1.call-start = ((), (), s32[]{:S(2)}) async-start(), calls=%async_computation.4 | async-start | bytes 6266880 | tf_op jit(solution)/shard_map/reduce_scatter | solution.py:326
  171.4 18.2 %collective-permute-start.7 = (bf16[768,384]{1,0:T(8,128)(2,1)}, bf16[768,384]{1,0:T(8,128)(2,1)}, u32[]{:S(2)}, u32[]{:S(2)}) collective-permute-start(bf16[768,384]{1,0:T(8,128)(2,1)} %get-tuple-element.152), channel_id=1, source_target_pairs={{0,1},{1,0},{2,3},{3,2},{4,5},{5,4},{6,7},{7,6},{8,9},{9,8},{10,11... | collective-permute-start | bytes 1769480 | tf_op jit(solution)/shard_map/ppermute | solution.py:181
  244.2 27.0 %collective-permute-start.8 = (bf16[768,768]{1,0:T(8,128)(2,1)}, bf16[768,768]{1,0:T(8,128)(2,1)}, u32[]{:S(2)}, u32[]{:S(2)}) collective-permute-start(bf16[768,768]{1,0:T(8,128)(2,1)} %get-tuple-element.149), channel_id=1, source_target_pairs={{0,1},{1,0},{2,3},{3,2},{4,5},{5,4},{6,7},{7,6},{8,9},{9,8},{10,11... | collective-permute-start | bytes 3538952 | tf_op jit(solution)/shard_map/ppermute | solution.py:181
  258.1 13.1 %copy-start.4 = (f32[768,768]{1,0:T(8,128)S(1)}, f32[768,768]{1,0:T(8,128)}, u32[]{:S(2)}) copy-start(f32[768,768]{1,0:T(8,128)} %fusion.27) | copy-start | bytes 7077892
  258.1 13.1 %copy-start.35 = (f32[768]{0:T(1024)S(1)}, f32[768]{0:T(1024)}, u32[]{:S(2)}) copy-start(f32[768]{0:T(1024)} %copy-done.34) | copy-start | bytes 9220
  277.5 7.6 %collective-permute-start.9 = (bf16[4,2,48,1280]{3,2,1,0:T(8,128)(2,1)S(1)}, bf16[4,2,48,1280]{3,2,1,0:T(8,128)(2,1)S(1)}, u32[]{:S(2)}, u32[]{:S(2)}) collective-permute-start(bf16[4,2,48,1280]{3,2,1,0:T(8,128)(2,1)S(1)} %fusion.35), channel_id=1, source_target_pairs={{0,2},{2,0},{4,6},{6,4},{8,10},{10,8},{12,14},{14,12},{16,18},{18,... | collective-permute-start | bytes 2949128 | tf_op jit(solution)/shard_map/ppermute | solution.py:181
  285.5 17.6 %collective-permute-start.10 = (bf16[4,48,1280]{2,1,0:T(8,128)(2,1)S(1)}, bf16[4,48,1280]{2,1,0:T(8,128)(2,1)S(1)}, u32[]{:S(2)}, u32[]{:S(2)}) collective-permute-start(bf16[4,48,1280]{2,1,0:T(8,128)(2,1)S(1)} %fusion.41), channel_id=1, source_target_pairs={{0,4},{2,6},{4,0},{6,2},{8,12},{10,14},{12,8},{14,10},{16,20},{18,... | collective-permute-start | bytes 1474568 | tf_op jit(solution)/shard_map/ppermute | solution.py:181
  286.5 32.4 %copy-start.7 = (f32[768,768]{1,0:T(8,128)S(1)}, f32[768,768]{1,0:T(8,128)}, u32[]{:S(2)}) copy-start(f32[768,768]{1,0:T(8,128)} %get-tuple-element.144) | copy-start | bytes 7077892
  286.5 32.4 %copy-start.8 = (f32[768,768]{1,0:T(8,128)S(1)}, f32[768,768]{1,0:T(8,128)}, u32[]{:S(2)}) copy-start(f32[768,768]{1,0:T(8,128)} %get-tuple-element.145) | copy-start | bytes 7077892
  287.9 31.1 %copy-start.6 = (f32[768,768]{1,0:T(8,128)S(1)}, f32[768,768]{1,0:T(8,128)}, u32[]{:S(2)}) copy-start(f32[768,768]{1,0:T(8,128)} %copy-done.5) | copy-start | bytes 7077892
  287.9 31.1 %slice-start = ((f32[1536]{0:T(1024)}), f32[750]{0:T(1024)S(1)}, s32[]{:S(2)}) async-start(f32[1536]{0:T(1024)} %copy-done.22), calls=%async_computation.6 | async-start | bytes 8192 | tf_op jit(solution)/shard_map/slice | solution.py:378
  303.3 6.9 %collective-permute-start.11 = (bf16[48,1280]{1,0:T(8,128)(2,1)S(1)}, bf16[48,1280]{1,0:T(8,128)(2,1)S(1)}, u32[]{:S(2)}, u32[]{:S(2)}) collective-permute-start(bf16[48,1280]{1,0:T(8,128)(2,1)S(1)} %get-tuple-element.156), channel_id=1, source_target_pairs={{0,8},{2,10},{4,12},{6,14},{8,0},{10,2},{12,4},{14,6},{16,24},{18,... | collective-permute-start | bytes 368648 | tf_op jit(solution)/shard_map/ppermute | solution.py:181
  305.9 6.7 %collective-permute-start.12 = (bf16[48,1280]{1,0:T(8,128)(2,1)S(1)}, bf16[48,1280]{1,0:T(8,128)(2,1)S(1)}, u32[]{:S(2)}, u32[]{:S(2)}) collective-permute-start(bf16[48,1280]{1,0:T(8,128)(2,1)S(1)} %get-tuple-element.158), channel_id=1, source_target_pairs={{0,16},{2,18},{4,20},{6,22},{8,24},{10,26},{12,28},{14,30},{16,0},... | collective-permute-start | bytes 368648 | tf_op jit(solution)/shard_map/ppermute | solution.py:181
  308.8 10.0 %collective-permute-start.13 = (bf16[48,1280]{1,0:T(8,128)(2,1)S(1)}, bf16[48,1280]{1,0:T(8,128)(2,1)S(1)}, u32[]{:S(2)}, u32[]{:S(2)}) collective-permute-start(bf16[48,1280]{1,0:T(8,128)(2,1)S(1)} %get-tuple-element.157), channel_id=1, source_target_pairs={{0,24},{2,26},{4,28},{6,30},{8,16},{10,18},{12,20},{14,22},{16,8},... | collective-permute-start | bytes 368648 | tf_op jit(solution)/shard_map/ppermute | solution.py:181
  318.9 4.9 %collective-permute-start.14 = (bf16[48,1280]{1,0:T(8,128)(2,1)S(1)}, bf16[48,1280]{1,0:T(8,128)(2,1)S(1)}, u32[]{:S(2)}, u32[]{:S(2)}) collective-permute-start(bf16[48,1280]{1,0:T(8,128)(2,1)S(1)} %fusion.44), channel_id=1, source_target_pairs={{0,1},{1,0},{2,3},{3,2},{4,5},{5,4},{6,7},{7,6},{8,9},{9,8},{10,11... | collective-permute-start | bytes 368648 | tf_op jit(solution)/shard_map/ppermute | solution.py:181
  323.9 10.2 %collective-permute-start.16 = (bf16[192,768]{1,0:T(8,128)(2,1)}, bf16[192,768]{1,0:T(8,128)(2,1)S(1)}, u32[]{:S(2)}, u32[]{:S(2)}) collective-permute-start(bf16[192,768]{1,0:T(8,128)(2,1)} %reduce-scatter.5.cloned.1.call-done), channel_id=1, source_target_pairs={{0,1},{1,0},{2,3},{3,2},{4,5},{5,4},{6,7},{7,6},{8,9},{9,8},{10,11... | collective-permute-start | bytes 884744 | tf_op jit(solution)/shard_map/ppermute | solution.py:181
  326.0 13.6 %copy-start.18 = (bf16[48,3840]{1,0:T(8,128)(2,1)S(1)}, bf16[48,3840]{1,0:T(8,128)(2,1)}, u32[]{:S(2)}) copy-start(bf16[48,3840]{1,0:T(8,128)(2,1)} %reduce-scatter.3.cloned.1.call-done) | copy-start | bytes 1105924
  326.0 13.6 %collective-permute-start.15 = (bf16[48,3840]{1,0:T(8,128)(2,1)}, bf16[48,3840]{1,0:T(8,128)(2,1)S(1)}, u32[]{:S(2)}, u32[]{:S(2)}) collective-permute-start(bf16[48,3840]{1,0:T(8,128)(2,1)} %reduce-scatter.3.cloned.1.call-done), channel_id=1, source_target_pairs={{0,1},{1,0},{2,3},{3,2},{4,5},{5,4},{6,7},{7,6},{8,9},{9,8},{10,11... | collective-permute-start | bytes 1105928 | tf_op jit(solution)/shard_map/ppermute | solution.py:181
  (35 other events, 200.4 us)
Sparse Core Ops, SparseCore 0:
  10.9 70.5 all-gather.2
  83.7 52.1 all-gather.4
  139.8 78.1 reduce-scatter.4
  221.8 85.3 reduce-scatter.2

commit v2 on v1

v2 whole, which is shorter than its diff:
```python
import functools
import math

import jax
import jax.numpy as jnp
from jax import lax
from jax.experimental import pallas as pl
from jax.experimental.pallas import tpu as pltpu
from jax.sharding import PartitionSpec as P


EPSILON = 1e-05
BF = jnp.bfloat16
F32 = jnp.float32
MASKED = -1e30


def dot(a, b, ca=1, cb=0):
    return lax.dot_general(a, b, (((ca,), (cb,)), ((), ())), preferred_element_type=F32)


def split3(x):
    high = x.astype(BF).astype(F32)
    rest = x - high
    mid = rest.astype(BF).astype(F32)
    return high, mid, (rest - mid).astype(BF).astype(F32)


def forward_kernel(half, valid, q_ref, k_ref, v_ref, mine_ref, sent_ref, lse_ref, kx_ref, vt_ref):
    rows = k_ref.shape[0]
    wide = q_ref.shape[0]

    kx_ref[:, :128] = k_ref[...]
    row = lax.broadcasted_iota(jnp.int32, (rows, 128), 0)
    lane = lax.broadcasted_iota(jnp.int32, (rows, 128), 1)
    padded = (lax.rem(row, half) >= valid) & (lane == 0)
    kx_ref[:, 128:] = jnp.where(padded, MASKED, 0.0).astype(BF)
    vt = v_ref[...].T
    vt_ref[0:64, :] = vt[0:64, :]
    vt_ref[64:80, :] = jnp.ones((16, rows), BF)
    vt_ref[80:144, :] = vt[64:128, :]
    vt_ref[144:160, :] = jnp.ones((16, rows), BF)

    lane = lax.broadcasted_iota(jnp.int32, (wide, 128), 1)
    q = q_ref[...] * jnp.asarray(0.125, BF)
    one = jnp.where(lane == 0, 1.0, 0.0).astype(BF)
    outs, sums = [], []
    for h in range(2):
        mine = (lane < 64) if h == 0 else (lane >= 64)
        qx = jnp.concatenate([jnp.where(mine, q, jnp.zeros_like(q)), one], axis=1)
        s = dot(kx_ref[...], qx, 1, 1)
        peak = jnp.max(s, axis=0, keepdims=True)
        p = jnp.exp(s - peak).astype(BF)
        o = dot(vt_ref[80 * h : 80 * h + 80, :], p)
        total = o[64:65, :]
        outs.append(o[0:64, :] / total)
        sums.append(peak + jnp.log(total))
    o = jnp.concatenate(outs, axis=0).T.astype(BF)
    mine_ref[...] = o[:half]
    sent_ref[...] = o[half:]
    lse_ref[...] = jnp.concatenate(sums + [jnp.zeros((6, wide), F32)], axis=0)[None]


def attention_forward(qkv, half, valid):
    rows, width = qkv.shape
    pairs = width // 3 // 128
    block = pl.BlockSpec((half, 128), lambda p: (0, p))
    return pl.pallas_call(
        functools.partial(forward_kernel, half, valid),
        grid=(pairs,),
        in_specs=[
            pl.BlockSpec((rows, 128), lambda p: (0, p)),
            pl.BlockSpec((rows, 128), lambda p: (0, pairs + p)),
            pl.BlockSpec((rows, 128), lambda p: (0, 2 * pairs + p)),
        ],
        out_specs=[block, block, pl.BlockSpec((1, 8, rows), lambda p: (p, 0, 0))],
        out_shape=[
            jax.ShapeDtypeStruct((half, pairs * 128), BF),
            jax.ShapeDtypeStruct((half, pairs * 128), BF),
            jax.ShapeDtypeStruct((pairs, 8, rows), F32),
        ],
        scratch_shapes=[pltpu.VMEM((rows, 256), BF), pltpu.VMEM((160, rows), BF)],
        cost_estimate=pl.CostEstimate(
            flops=pairs * 2 * 4 * rows * rows * 256,
            bytes_accessed=rows * width * 2 + rows * width,
            transcendentals=pairs * 2 * rows * rows,
        ),
        name="attention_forward",
    )(qkv, qkv, qkv)


def backward_kernel(
    half, valid, q_ref, k_ref, v_ref, o_mine_ref, o_sent_ref, mine_ref, got_ref, lse_ref, token_ref,
    d_ref, kt_ref, vt_ref, dkt_ref, dvt_ref,
):
    rows = k_ref.shape[0]
    step = pl.program_id(1)

    @pl.when(step == 0)
    def _():
        kt_ref[0:128, :] = k_ref[...].T
        vt_ref[0:128, :] = v_ref[...].T
        row = lax.broadcasted_iota(jnp.int32, (128, rows), 0)
        key = lax.broadcasted_iota(jnp.int32, (128, rows), 1)
        bias = jnp.where(lax.rem(key, half) >= valid, MASKED, 0.0)
        ones = jnp.where((row >= 1) & (row < 4), 1.0, 0.0)
        kt_ref[128:256, :] = jnp.where(row == 0, bias, ones).astype(BF)
        vt_ref[128:256, :] = ones.astype(BF)
        dkt_ref[...] = jnp.zeros_like(dkt_ref)
        dvt_ref[...] = jnp.zeros_like(dvt_ref)

    lane = lax.broadcasted_iota(jnp.int32, (half, 128), 1)
    q = q_ref[...] * jnp.asarray(0.125, BF)
    do = jnp.where(step == 0, mine_ref[...], got_ref[...])
    o = jnp.where(step == 0, o_mine_ref[...], o_sent_ref[...])
    product = do.astype(F32) * o.astype(F32)
    lse = lse_ref[0].T
    qt, dot_t = q.T, do.T

    def extra(x, first):
        a, b, c = split3(-x)
        tail = jnp.where(lane == 2, b, jnp.where(lane == 3, c, 0.0))
        return jnp.where(lane == 0, first, jnp.where(lane == 1, a, tail)).astype(BF)

    dq = []
    for h in range(2):
        mine = (lane < 64) if h == 0 else (lane >= 64)
        delta = jnp.sum(jnp.where(mine, product, 0.0), axis=1, keepdims=True)
        qx = jnp.concatenate(
            [jnp.where(mine, q, jnp.zeros_like(q)), extra(lse[:, h : h + 1], 1.0)], axis=1
        )
        dx = jnp.concatenate([jnp.where(mine, do, jnp.zeros_like(do)), extra(delta, 0.0)], axis=1)
        p = jnp.exp(dot(qx, kt_ref[...]))
        low = p.astype(BF)
        ds = (p * dot(dx, vt_ref[...])).astype(BF)
        dq.append(dot(ds, k_ref[...]))
        part = slice(64 * h, 64 * h + 64)
        dkt_ref[part, :] += dot(qt[part, :], ds)
        dvt_ref[part, :] += dot(dot_t[part, :], low)
    dq = (jnp.where(lane < 64, dq[0], dq[1]) * 0.125).astype(BF)
    d_ref[0, pl.ds(pl.multiple_of(step * half, 128), half), :] = dq

    @pl.when(step == 1)
    def _():
        d_ref[1] = dkt_ref[...].T.astype(BF)
        d_ref[2] = dvt_ref[...].T.astype(BF)


def attention_backward(qkv, o_mine, o_sent, do_mine, do_got, lse, token, half, valid, start, count):
    rows, width = qkv.shape
    pairs = width // 3 // 128

    def whole(part):
        return pl.BlockSpec((rows, 128), lambda p, i: (0, part * pairs + start + p))

    block = pl.BlockSpec((half, 128), lambda p, i: (i, start + p))
    fixed = pl.BlockSpec((half, 128), lambda p, i: (0, start + p))
    return pl.pallas_call(
        functools.partial(backward_kernel, half, valid),
        grid=(count, 2),
        in_specs=[
            block, whole(1), whole(2), fixed, fixed, fixed, fixed,
            pl.BlockSpec((1, 8, half), lambda p, i: (start + p, 0, i)),
            pl.BlockSpec(memory_space=pl.ANY),
        ],
        out_specs=pl.BlockSpec((3, rows, 128), lambda p, i: (0, 0, p)),
        out_shape=jax.ShapeDtypeStruct((3, rows, count * 128), BF),
        scratch_shapes=[
            pltpu.VMEM((256, rows), BF),
            pltpu.VMEM((256, rows), BF),
            pltpu.VMEM((128, rows), F32),
            pltpu.VMEM((128, rows), F32),
        ],
        cost_estimate=pl.CostEstimate(
            flops=count * 2 * 8 * rows * rows * 256,
            bytes_accessed=count * rows * 128 * 16,
            transcendentals=count * 2 * rows * rows,
        ),
        name="attention_backward",
    )(qkv, qkv, qkv, o_mine, o_sent, do_mine, do_got, lse, token)


def prepare_kernel(x_ref, *refs):
    normed_ref, flipped_ref, inverse_ref = refs[-3:]
    valid = x_ref.shape[1]
    x = x_ref[0].astype(F32)
    centered = x - jnp.mean(x, axis=-1, keepdims=True)
    inverse = lax.rsqrt(jnp.mean(centered * centered, axis=-1, keepdims=True) + EPSILON)
    rest = (normed_ref.shape[0] - valid // 8 * 8, normed_ref.shape[1])
    normed_ref[valid // 8 * 8 :, :] = jnp.zeros(rest, F32)
    normed_ref[:valid, :] = centered * inverse
    inverse_ref[...] = jnp.zeros(inverse_ref.shape, F32)
    inverse_ref[:valid, :] = inverse
    wide = normed_ref.shape[1]
    flipped_ref[:wide, :] = normed_ref[...].T.astype(BF)
    flipped_ref[wide:, :] = jnp.ones((16, normed_ref.shape[0]), BF)


def prepare(frames, half, block, filled=()):
    _, valid, wide = frames.shape
    return pl.pallas_call(
        prepare_kernel,
        grid=(1,),
        in_specs=[pl.BlockSpec((1, valid, wide), lambda i: (0, 0, 0))]
        + [pl.BlockSpec(memory_space=pl.ANY)] * len(filled),
        out_specs=[
            pl.BlockSpec((half, wide), lambda i: (block, 0)),
            pl.BlockSpec((wide + 16, half), lambda i: (0, block)),
            pl.BlockSpec((half, 1), lambda i: (0, 0)),
        ],
        out_shape=[
            jax.ShapeDtypeStruct((2 * half, wide), F32),
            jax.ShapeDtypeStruct((wide + 16, 2 * half), BF),
            jax.ShapeDtypeStruct((half, 1), F32),
        ],
        input_output_aliases={1: 0, 2: 1} if filled else {},
        cost_estimate=pl.CostEstimate(
            flops=half * wide * 16, bytes_accessed=half * wide * 8, transcendentals=half
        ),
        name="prepare",
    )(frames, *filled)


def projection_kernel(
    part, group, place_ref, held_ref, x_ref, qkv_ref, w_ref, wt_ref, rows_ref, columns_ref,
    gain_ref, bias_ref,
):
    wide, width = w_ref.shape

    @pl.when(pl.program_id(0) == 0)
    def _():
        blocks, extent, _ = held_ref.shape
        for d in range(blocks):
            block = held_ref[place_ref[d]]
            w_ref[d * extent : (d + 1) * extent, :] = block[:, :width]
            columns_ref[d * extent : (d + 1) * extent, :] = block[:, width:].astype(F32)
        wt_ref[...] = w_ref[...].T
        table = columns_ref[...].T[:16, :]
        rows_ref[...] = table
        gain_ref[...] = table[:8]
        here = place_ref[blocks]
        lane = lax.broadcasted_iota(jnp.int32, (wide, group), 0)
        entry = lax.broadcasted_iota(jnp.int32, (wide, group), 1)
        base = lane + part * (lane // part) - group * here
        low = table.astype(BF)
        for v in range(2):
            total = jnp.zeros((16, group), F32)
            for j in range(2):
                chosen = entry == base + part * j - wide * v
                picked = dot(low, jnp.where(chosen, 1.0, 0.0).astype(BF))
                total = total + picked[2 + j : 3 + j, :]
            bias_ref[:, 2 * v * group : (2 * v + 1) * group] = total[:8]
        bias_ref[:, group : 2 * group] = jnp.zeros((8, group), F32)

    h = (x_ref[...] * gain_ref[0:1, :] + gain_ref[1:2, :]).astype(BF)
    qkv_ref[...] = (dot(h, w_ref[...]) + bias_ref[0:1, :]).astype(BF)


def projection(held, place, normed, part):
    blocks, extent, across = held.shape
    width = across - 128
    rows, wide = normed.shape
    tile = 512

    def fixed(*shape):
        return pl.BlockSpec(shape, lambda i, p: tuple(0 for _ in shape))

    return pl.pallas_call(
        functools.partial(projection_kernel, part, width // 3),
        grid_spec=pltpu.PrefetchScalarGridSpec(
            num_scalar_prefetch=1,
            grid=(rows // tile,),
            in_specs=[fixed(blocks, extent, across), pl.BlockSpec((tile, wide), lambda i, p: (i, 0))],
            out_specs=[
                pl.BlockSpec((tile, width), lambda i, p: (i, 0)),
                fixed(wide, width), fixed(width, wide), fixed(16, wide), fixed(wide, 128),
            ],
            scratch_shapes=[pltpu.VMEM((8, wide), F32), pltpu.VMEM((8, width), F32)],
        ),
        out_shape=[
            jax.ShapeDtypeStruct((rows, width), BF),
            jax.ShapeDtypeStruct((wide, width), BF),
            jax.ShapeDtypeStruct((width, wide), BF),
            jax.ShapeDtypeStruct((16, wide), F32),
            jax.ShapeDtypeStruct((wide, 128), F32),
        ],
        cost_estimate=pl.CostEstimate(
            flops=2 * rows * wide * width, bytes_accessed=rows * wide * 8, transcendentals=0
        ),
        name="projection",
    )(place, held, normed)


def weight_kernel(pieces, xt_ref, w_ref, scale_ref, *refs):
    d_refs, (g_ref, c_ref, s_ref) = refs[:pieces], refs[pieces:]
    d = jnp.concatenate([r[0] for r in d_refs], axis=1)
    m = dot(xt_ref[...], d)
    s = m[w_ref.shape[0] :][:8]
    m = m[: w_ref.shape[0]]
    s_ref[...] = s
    gain, shift = scale_ref[:, 0:1], scale_ref[:, 1:2]
    total = s[0:1, :]
    g_ref[...] = (gain * m + shift * total).astype(BF)
    w = w_ref[...].astype(F32)
    lane = lax.broadcasted_iota(jnp.int32, c_ref.shape, 1)
    first = jnp.sum(w * m, axis=1, keepdims=True)
    second = jnp.sum(w * total, axis=1, keepdims=True)
    now = jnp.where(lane == 0, first, jnp.where(lane == 1, second, 0.0))
    before = jnp.where(pl.program_id(0) == 0, jnp.zeros_like(now), c_ref[...])
    c_ref[...] = before + now


def projection_weight_gradient(xt, w, scale, ds):
    tall, rows = xt.shape
    wide = w.shape[0]
    group = sum(d.shape[2] for d in ds)
    return pl.pallas_call(
        functools.partial(weight_kernel, len(ds)),
        grid=(3,),
        in_specs=[
            pl.BlockSpec((tall, rows), lambda j: (0, 0)),
            pl.BlockSpec((wide, group), lambda j: (0, j)),
            pl.BlockSpec((wide, 128), lambda j: (0, 0)),
        ]
        + [pl.BlockSpec((1, *d.shape[1:]), lambda j: (j, 0, 0)) for d in ds],
        out_specs=[
            pl.BlockSpec((wide, group), lambda j: (0, j)),
            pl.BlockSpec((wide, 128), lambda j: (0, 0)),
            pl.BlockSpec((8, group), lambda j: (0, j)),
        ],
        out_shape=[
            jax.ShapeDtypeStruct((wide, 3 * group), BF),
            jax.ShapeDtypeStruct((wide, 128), F32),
            jax.ShapeDtypeStruct((8, 3 * group), F32),
        ],
        cost_estimate=pl.CostEstimate(
            flops=2 * rows * wide * 3 * group, bytes_accessed=rows * wide * 4, transcendentals=0
        ),
        name="projection_weight_gradient",
    )(xt, w, scale, *ds)


def spread_kernel(
    part, pieces, per, place_ref, token_ref, xt_ref, w_ref, scale_ref, *refs
):
    d_refs, (b_ref, v_ref, keep_ref, give_ref, c_ref, s_ref) = refs[:pieces], refs[pieces:]
    step = pl.program_id(0)
    wide, group = w_ref.shape
    d = jnp.concatenate([r[0] for r in d_refs], axis=1)
    m = dot(xt_ref[...], d)
    s = m[wide : wide + 8]
    m = m[:wide]
    s_ref[step] = s
    gain, shift = scale_ref[:, 0:1], scale_ref[:, 1:2]
    total = s[0:1, :]
    g = (gain * m + shift * total).astype(BF)
    w = w_ref[...].astype(F32)
    lane = lax.broadcasted_iota(jnp.int32, c_ref.shape, 1)
    first = jnp.sum(w * m, axis=1, keepdims=True)
    second = jnp.sum(w * total, axis=1, keepdims=True)
    now = jnp.where(lane == 0, first, jnp.where(lane == 1, second, 0.0))

    @pl.when(step == 0)
    def _():
        c_ref[...] = now

    @pl.when(step > 0)
    def _():
        c_ref[...] += now

    def store(value, columns):
        value = value.reshape(keep_ref.shape[0], 2, part, value.shape[1])

        @pl.when(place_ref[0] == 0)
        def _():
            keep_ref[:, :, columns] = value[:, 0]
            give_ref[:, :, columns] = value[:, 1]

        @pl.when(place_ref[0] == 1)
        def _():
            keep_ref[:, :, columns] = value[:, 1]
            give_ref[:, :, columns] = value[:, 0]

    store(g, pl.ds(pl.multiple_of(step * group, 128), group))

    @pl.when(step == 2)
    def _():
        columns = c_ref[...]
        small = v_ref[...].T
        for i, name in enumerate((4, 5, 6, 7 + per)):
            columns = jnp.where(lane == name, small[:, i : i + 1], columns)
        v = jnp.broadcast_to(b_ref[...], (8, b_ref.shape[1])).T[:, 0:1]
        for j in range(per):
            column = jnp.concatenate(
                [v[(d * per + j) * part :][:part] for d in range(wide // part)], axis=0
            )
            columns = jnp.where(lane == 7 + j, column, columns)
        c_ref[...] = columns
        half = group // 2
        low = lane[:half]
        for side in (0, 2):
            v = s_ref[side].T[:, 0:1]
            at = pl.ds(pl.multiple_of(place_ref[1] * half + side * wide // 4, 64), half)
            block = c_ref[at, :]
            for j in range(2):
                column = jnp.concatenate(
                    [v[(2 * d + j) * part :][:part] for d in range(half // part)], axis=0
                )
                block = jnp.where(low == 2 + j, column, block)
            c_ref[at, :] = block
        store(c_ref[...].astype(BF), pl.ds(3 * group, 128))


def spread_weight_gradient(place, token, xt, w, scale, ds, bias, sums, part):
    _, rows = xt.shape
    wide = w.shape[0]
    group = sum(d.shape[2] for d in ds)
    size = wide // part
    out = pl.BlockSpec((size // 2, part, 3 * group + 128), lambda j, p: (0, 0, 0))

    def fixed(x):
        return pl.BlockSpec(x.shape, lambda j, p: (0, 0))

    return pl.pallas_call(
        functools.partial(spread_kernel, part, len(ds), bias.shape[1] // wide),
        grid_spec=pltpu.PrefetchScalarGridSpec(
            num_scalar_prefetch=1,
            grid=(3,),
            in_specs=[
                pl.BlockSpec(memory_space=pl.ANY),
                fixed(xt),
                pl.BlockSpec((wide, group), lambda j, p: (0, j)),
                fixed(scale),
            ]
            + [pl.BlockSpec((1, *d.shape[1:]), lambda j, p: (j, 0, 0)) for d in ds]
            + [fixed(bias), fixed(sums)],
            out_specs=[out, out],
            scratch_shapes=[pltpu.VMEM((wide, 128), F32), pltpu.VMEM((3, 8, group), F32)],
        ),
        out_shape=[jax.ShapeDtypeStruct((size // 2, part, 3 * group + 128), BF)] * 2,
        cost_estimate=pl.CostEstimate(
            flops=2 * rows * wide * 3 * group, bytes_accessed=rows * wide * 4, transcendentals=0
        ),
        name="spread_weight_gradient",
    )(place, token, xt, w, scale, *ds, bias, sums)


def input_kernel(pieces, token_ref, wt_ref, *refs):
    d_refs, (other_ref, mine_ref) = refs[:pieces], refs[pieces:]
    d = jnp.concatenate([r[j] for j in range(3) for r in d_refs], axis=1)
    value = dot(d, wt_ref[...])
    half = pl.num_programs(0) // 2

    @pl.when(pl.program_id(0) < half)
    def _():
        other_ref[...] = value.astype(BF)

    @pl.when(pl.program_id(0) >= half)
    def _():
        mine_ref[...] = value


def projection_input_gradient(wt, ds, token, half):
    wide = wt.shape[1]
    tile = 384
    tiles = half // tile
    return pl.pallas_call(
        functools.partial(input_kernel, len(ds)),
        grid=(2 * tiles,),
        in_specs=[pl.BlockSpec(memory_space=pl.ANY), pl.BlockSpec(wt.shape, lambda i: (0, 0))]
        + [
            pl.BlockSpec((3, tile, d.shape[2]), lambda i: (0, lax.rem(i + tiles, 2 * tiles), 0))
            for d in ds
        ],
        out_specs=[
            pl.BlockSpec((tile, wide), lambda i: (jnp.minimum(i, tiles - 1), 0)),
            pl.BlockSpec((tile, wide), lambda i: (jnp.maximum(i - tiles, 0), 0)),
        ],
        out_shape=[
            jax.ShapeDtypeStruct((half, wide), BF),
            jax.ShapeDtypeStruct((half, wide), F32),
        ],
        cost_estimate=pl.CostEstimate(
            flops=4 * half * wt.size, bytes_accessed=half * wt.shape[0] * 8, transcendentals=0
        ),
        name="projection_input_gradient",
    )(token, wt, *ds)


def second_kernel(place_ref, token_ref, mine_ref, got_ref, drb_ref, h_ref, du_ref, out_ref, ht_ref):
    group = mine_ref.shape[1]
    step = pl.program_id(0)

    @pl.when(step == 0)
    def _():
        ht_ref[...] = h_ref[...].T
        here = place_ref[0]
        first = pl.multiple_of(here * group, 128)
        other = pl.multiple_of(group - here * group, 128)
        out_ref[pl.ds(first, group), :] = dot(mine_ref[...], drb_ref[...], 0, 0).astype(BF)
        out_ref[pl.ds(other, group), :] = dot(got_ref[...], drb_ref[...], 0, 0).astype(BF)

    @pl.when(step > 0)
    def _():
        out_ref[...] = dot(ht_ref[...], du_ref[...]).astype(BF)


def second_gradient(here, token, o_mine, o_got, drb, hidden, du):
    rows, wide = hidden.shape
    ff = du.shape[1]

    def fixed(x):
        return pl.BlockSpec(x.shape, lambda i, p: (0, 0))

    return pl.pallas_call(
        second_kernel,
        grid_spec=pltpu.PrefetchScalarGridSpec(
            num_scalar_prefetch=1,
            grid=(1 + ff // wide,),
            in_specs=[
                pl.BlockSpec(memory_space=pl.ANY), fixed(o_mine), fixed(o_got), fixed(drb), fixed(hidden),
                pl.BlockSpec((rows, wide), lambda i, p: (0, jnp.maximum(i - 1, 0))),
            ],
            out_specs=pl.BlockSpec((wide, wide), lambda i, p: (0, i)),
            scratch_shapes=[pltpu.VMEM((wide, rows), BF)],
        ),
        out_shape=jax.ShapeDtypeStruct((wide, wide + ff), BF),
        cost_estimate=pl.CostEstimate(
            flops=2 * rows * wide * (wide + ff), bytes_accessed=rows * ff * 4, transcendentals=0
        ),
        name="second_gradient",
    )(here, token, o_mine, o_got, drb, hidden, du)


def fill_rows(ref, x):
    valid = x.shape[0]
    start = valid // 16 * 16
    ref[start:, :] = jnp.zeros((ref.shape[0] - start, ref.shape[1]), ref.dtype)
    ref[:valid, :] = x


def third_kernel(place_ref, z_ref, cot_ref, token_ref, keep_ref, give_ref, padded_ref):
    @pl.when(pl.program_id(0) == 0)
    def _():
        fill_rows(padded_ref, cot_ref[0])

    value = dot(z_ref[...], padded_ref[...], 0, 0).astype(BF)
    owners, extent, wide = keep_ref.shape
    value = value.reshape(owners, 2, extent, wide)

    @pl.when(place_ref[0] == 0)
    def _():
        keep_ref[...] = value[:, 0]
        give_ref[...] = value[:, 1]

    @pl.when(place_ref[0] == 1)
    def _():
        keep_ref[...] = value[:, 1]
        give_ref[...] = value[:, 0]


def third_gradient(parity, activated, cotangent, size, token):
    _, valid, wide = cotangent.shape
    rows, ff = activated.shape
    extent = ff // size
    owners = wide // extent // 2
    out = pl.BlockSpec((owners, extent, wide), lambda i, p: (i, 0, 0))
    return pl.pallas_call(
        third_kernel,
        grid_spec=pltpu.PrefetchScalarGridSpec(
            num_scalar_prefetch=1,
            grid=(ff // wide,),
            in_specs=[
                pl.BlockSpec((rows, wide), lambda i, p: (0, i)),
                pl.BlockSpec((1, valid, wide), lambda i, p: (0, 0, 0)),
                pl.BlockSpec(memory_space=pl.ANY),
            ],
            out_specs=[out, out],
            scratch_shapes=[pltpu.VMEM((rows, wide), BF)],
        ),
        out_shape=[jax.ShapeDtypeStruct((size // 2, extent, wide), BF)] * 2,
        cost_estimate=pl.CostEstimate(
            flops=2 * rows * wide * ff, bytes_accessed=rows * ff * 4, transcendentals=0
        ),
        name="third_gradient",
    )(parity, activated, cotangent, token)


def feed_back_kernel(
    part, place_ref, fc2_ref, fc1_ref, out_ref, slope_ref, cot_ref, residual_ref, gain_ref,
    du_ref, flat_ref, grad_ref, low_ref, mine_ref, sent_ref, bias_ref, sums_ref,
    total_ref, padded_ref,
):
    step = pl.program_id(0)
    rows, wide = total_ref.shape
    group = mine_ref.shape[1]
    per = fc2_ref.shape[1] // wide

    @pl.when(step == 0)
    def _():
        fill_rows(padded_ref, cot_ref[0])
        total_ref[...] = jnp.zeros_like(total_ref)

    if part:
        for d in range(fc2_ref.shape[0] // part):
            for j in range(per):
                block = fc2_ref[d * part : (d + 1) * part, j * wide : (j + 1) * wide]
                flat_ref[(d * per + j) * part : (d * per + j + 1) * part, :] = block
    else:
        flat_ref[...] = fc2_ref[...]
    du = dot(padded_ref[...], flat_ref[...], 1, 1) * slope_ref[...].astype(F32)
    bias_ref[...] = jnp.sum(du, axis=0, keepdims=True)
    du = du.astype(BF)
    du_ref[...] = du
    total_ref[...] += dot(du, fc1_ref[...], 1, 1)

    @pl.when(step == pl.num_programs(0) - 1)
    def _():
        tile = 64

        def body(i, sums):
            at = pl.ds(pl.multiple_of(i * tile, tile), tile)
            r = residual_ref[at, :]
            centered = r - jnp.mean(r, axis=-1, keepdims=True)
            inverse = lax.rsqrt(jnp.mean(centered * centered, axis=-1, keepdims=True) + EPSILON)
            normed = centered * inverse
            dh = total_ref[at, :]
            weighted = dh * gain_ref[...]
            first = jnp.mean(weighted, axis=-1, keepdims=True)
            second = jnp.mean(weighted * normed, axis=-1, keepdims=True)
            g = padded_ref[at, :].astype(F32)
            grad = g + inverse * (weighted - first - normed * second)
            grad_ref[at, :] = grad
            low_ref[at, :] = grad.astype(BF)
            parts = (grad, dh * normed, dh, g)
            return tuple(s + jnp.sum(p, axis=0, keepdims=True) for s, p in zip(sums, parts, strict=True))

        zero = jnp.zeros((1, wide), F32)
        sums = lax.fori_loop(0, rows // tile, body, (zero,) * 4)
        sums_ref[...] = jnp.concatenate(sums + (jnp.zeros((4, wide), F32),), axis=0)
        here = place_ref[0]
        mine = out_ref[pl.ds(pl.multiple_of(here * group, 128), group), :]
        other = out_ref[pl.ds(pl.multiple_of(group - here * group, 128), group), :]
        sent_ref[...] = dot(low_ref[...], other, 1, 1).astype(BF)
        mine_ref[...] = dot(low_ref[...], mine, 1, 1).astype(BF)


def feed_back(here, weights, slope, cotangent, residual, gain, part):
    rows, ff = slope.shape
    _, valid, wide = cotangent.shape
    group = wide // 2
    per = ff // wide
    if part % 16:
        part = 0
        fc2, fc1, out = weights
        fc2_spec = pl.BlockSpec((wide, wide), lambda i, p: (i, 0))
        fc1_spec = pl.BlockSpec((wide, wide), lambda i, p: (0, i))
        out_spec = pl.BlockSpec((wide, wide), lambda i, p: (0, 0))
    else:
        fc2 = fc1 = out = weights
        fc2_spec = pl.BlockSpec((wide // per, ff), lambda i, p: (i, 0))
        fc1_spec = pl.BlockSpec((wide, wide), lambda i, p: (0, per + 1 + i))
        out_spec = pl.BlockSpec((wide, wide), lambda i, p: (0, per))

    def fixed(*shape):
        return pl.BlockSpec(shape, lambda i, p: tuple(0 for _ in shape))

    block = pl.BlockSpec((rows, wide), lambda i, p: (0, i))
    return pl.pallas_call(
        functools.partial(feed_back_kernel, part),
        grid_spec=pltpu.PrefetchScalarGridSpec(
            num_scalar_prefetch=1,
            grid=(per,),
            in_specs=[
                fc2_spec, fc1_spec, out_spec, block, fixed(1, valid, wide), fixed(rows, wide),
                fixed(1, wide),
            ],
            out_specs=[
                block, pl.BlockSpec((wide, wide), lambda i, p: (i, 0)), fixed(rows, wide),
                fixed(rows, wide), fixed(rows, group), fixed(rows, group),
                pl.BlockSpec((1, wide), lambda i, p: (0, i)), fixed(8, wide),
            ],
            scratch_shapes=[pltpu.VMEM((rows, wide), F32), pltpu.VMEM((rows, wide), BF)],
        ),
        out_shape=[
            jax.ShapeDtypeStruct((rows, ff), BF),
            jax.ShapeDtypeStruct((ff, wide), BF),
            jax.ShapeDtypeStruct((rows, wide), F32),
            jax.ShapeDtypeStruct((rows, wide), BF),
            jax.ShapeDtypeStruct((rows, group), BF),
            jax.ShapeDtypeStruct((rows, group), BF),
            jax.ShapeDtypeStruct((1, ff), F32),
            jax.ShapeDtypeStruct((8, wide), F32),
        ],
        cost_estimate=pl.CostEstimate(
            flops=4 * rows * wide * ff, bytes_accessed=ff * wide * 10, transcendentals=rows
        ),
        name="feed_back",
    )(here, fc2, fc1, out, slope, cotangent, residual, gain)


def finish_kernel(spans, place_ref, mine_ref, theirs_ref, w_ref, *refs):
    here = place_ref[0]
    group = w_ref.shape[1] // 6
    mine, theirs = mine_ref[...].astype(F32), theirs_ref[...].astype(F32)
    for j in range(3):
        part = slice(j * group, (j + 1) * group)
        at = (2 * j * group) + here * group
        w_ref[:, pl.ds(pl.multiple_of(at, 128), group)] = mine[:, part]
        at = (2 * j + 1) * group - here * group
        w_ref[:, pl.ds(pl.multiple_of(at, 128), group)] = theirs[:, part]
    rows = (mine[:, 3 * group :] + theirs[:, 3 * group :]).T
    for (start, stop), ref in zip(spans, refs, strict=True):
        ref[...] = jnp.concatenate([rows[i : i + 1] for i in range(start, stop)], axis=1)


def finish(here, mine, theirs, spans):
    part, across = mine.shape
    width = 2 * (across - 128)

    def fixed(*shape):
        return pl.BlockSpec(shape, lambda i, p: (0, 0))

    sizes = [(1, (stop - start) * part) for start, stop in spans]
    return pl.pallas_call(
        functools.partial(finish_kernel, spans),
        grid_spec=pltpu.PrefetchScalarGridSpec(
            num_scalar_prefetch=1,
            grid=(1,),
            in_specs=[fixed(part, across)] * 2,
            out_specs=[fixed(part, width)] + [fixed(*shape) for shape in sizes],
        ),
        out_shape=[jax.ShapeDtypeStruct((part, width), F32)]
        + [jax.ShapeDtypeStruct(shape, F32) for shape in sizes],
        name="finish",
    )(here, mine, theirs)


def join_kernel(mine_ref, theirs_ref, out_ref, first_ref):
    wide = out_ref.shape[1]
    mine, theirs = mine_ref[...].astype(F32), theirs_ref[...].astype(F32)
    out_ref[...] = mine[:, :wide] + theirs[:, :wide]
    first_ref[...] = mine[:, wide:] + theirs[:, wide:]


def join_second(mine, theirs, wide):
    part, across = mine.shape
    return pl.pallas_call(
        join_kernel,
        out_shape=[
            jax.ShapeDtypeStruct((part, wide), F32),
            jax.ShapeDtypeStruct((part, across - wide), F32),
        ],
        name="join_second",
    )(mine, theirs)


def input_end_kernel(mine_ref, got_ref, residual_ref, normed_ref, gain_ref, inverse_ref, out_ref):
    normed = normed_ref[...]
    weighted = (mine_ref[...] + got_ref[...].astype(F32)) * gain_ref[...]
    first = jnp.mean(weighted, axis=-1, keepdims=True)
    second = jnp.mean(weighted * normed, axis=-1, keepdims=True)
    out_ref[:, 0, :] = residual_ref[...] + inverse_ref[...] * (weighted - first - normed * second)


def input_end(mine, got, residual, normed, gain, inverse, valid):
    half, wide = mine.shape
    tile = 128
    block = pl.BlockSpec((tile, wide), lambda i: (i, 0))
    return pl.pallas_call(
        input_end_kernel,
        grid=(half // tile,),
        in_specs=[
            block, block, block, block, pl.BlockSpec((1, wide), lambda i: (0, 0)),
            pl.BlockSpec((tile, 1), lambda i: (i, 0)),
        ],
        out_specs=pl.BlockSpec((tile, 1, wide), lambda i: (i, 0, 0)),
        out_shape=jax.ShapeDtypeStruct((valid, 1, wide), F32),
        cost_estimate=pl.CostEstimate(
            flops=half * wide * 10, bytes_accessed=half * wide * 18, transcendentals=0
        ),
        name="input_end",
    )(mine, got, residual, normed, gain, inverse)


def swap(x, axis, size, bit):
    return lax.ppermute(x, axis, [(i, i ^ bit) for i in range(size)])


def bits_of(size):
    top = size // 4
    return top, [1 << b for b in range(top.bit_length() - 2, -1, -1)]


def gather_blocks(x, size):
    me = lax.axis_index("dp")
    top, bits = bits_of(size)
    held = jnp.stack([x] + [swap(x, "dp", size, j * top) for j in (1, 2, 3)])
    where = [j * top for j in range(4)]
    for bit in bits:
        held = jnp.concatenate([held, swap(held, "dp", size, bit)])
        where = where + [w ^ bit for w in where]
    place = [0] * size
    for i, w in enumerate(where):
        place[w] = i
    return held, jnp.asarray(place, jnp.int32)[me ^ jnp.arange(size)]


def halve(x, axis, bit):
    mine = lax.rem(lax.axis_index("dp") // bit, 2)
    keep = lax.dynamic_index_in_dim(x, mine, axis, keepdims=False)
    give = lax.dynamic_index_in_dim(x, 1 - mine, axis, keepdims=False)
    return keep, give.astype(BF)


def scatter_split(x, size):
    top, _ = bits_of(size)
    mine = lax.axis_index("dp") // top
    gives = [
        lax.dynamic_index_in_dim(x, mine ^ j, 0, keepdims=False).astype(BF) for j in (1, 2, 3)
    ]
    return gives, lax.dynamic_index_in_dim(x, mine, 0, keepdims=False).astype(F32)


def scatter_join(total, gives, size):
    top, _ = bits_of(size)
    for j, give in zip((1, 2, 3), gives, strict=True):
        total = total + swap(give, "dp", size, j * top).astype(F32)
    return total


def after(x, *others):
    return lax.optimization_barrier((x, *others))[0]


def normalize(values):
    center = jnp.mean(values, axis=-1, keepdims=True)
    centered = values - center
    variance = jnp.mean(centered * centered, axis=-1, keepdims=True)
    inverse = lax.rsqrt(variance + EPSILON)
    return centered * inverse, inverse


def gelu_cdf(values):
    return 0.5 * (1.0 + lax.erf(values * (1.0 / math.sqrt(2.0))))


def layer(
    size, frames_in, ln1_gain, ln1_bias, w_qkv, b_qv, w_o, b_o,
    ln2_gain, ln2_bias, w_fc1, b_fc1, w_fc2, b_fc2, cotangent,
):
    clips, valid, wide = frames_in.shape
    assert clips == 1
    ff = w_fc1.shape[1]
    part = w_qkv.shape[0]
    group = wide // 2
    half = -(-valid // 256) * 256
    here = lax.axis_index("seq")

    def pad(block):
        return jnp.pad(block[0], ((0, half - valid), (0, 0)))

    def other(x):
        return swap(x, "seq", 2, 1)

    def pick(x, axis, index):
        return lax.dynamic_index_in_dim(x, index, axis, keepdims=False)

    per = ff // wide
    me = lax.axis_index("dp")
    _, bits = bits_of(size)

    vectors = jnp.concatenate([ln1_gain, ln1_bias, b_qv, b_o, ln2_gain, ln2_bias, b_fc1, b_fc2])
    count = vectors.shape[0] // part
    columns = lax.optimization_barrier(
        jnp.pad(vectors.reshape(count, part).T, ((0, 0), (0, 128 - count)))
    )
    w_mine = [
        lax.dynamic_slice_in_dim(w_qkv, j * wide + here * group, group, axis=1) for j in range(3)
    ]
    held, place = gather_blocks(jnp.concatenate(w_mine + [columns], axis=1), size)
    if part % 16:
        held = jnp.take(held, place, axis=0, mode="clip").reshape(1, wide, 3 * group + 128)
        place = jnp.zeros((1,), jnp.int32)
    place = jnp.concatenate([place, jnp.full((1,), here, jnp.int32)])
    fc2_local = w_fc2.reshape(per, part, wide).transpose(1, 0, 2).reshape(part, ff)
    later = lax.all_gather(
        jnp.concatenate([fc2_local, w_o, w_fc1], axis=1), "dp", axis=0, tiled=True
    )
    out_full, fc1_full = later[:, ff : ff + wide], later[:, ff + wide :]
    weights = later
    if part % 16:
        fc2_full = later[:, :ff].reshape(size, part, per, wide)
        weights = (fc2_full.transpose(0, 2, 1, 3).reshape(ff, wide), fc1_full, out_full)

    prepared = prepare(frames_in, half, 0)
    inverse_one = prepared[2]
    normed_both, normed_t, _ = prepare(other(frames_in), half, 1, prepared[:2])
    qkv, w_full, w_flipped, table, scale = projection(held, place, normed_both, part)

    def vector(start, stop):
        return table[start:stop].reshape(-1, size, part).transpose(1, 0, 2).reshape(-1)

    gain_one, bias_out = table[0], table[4]
    gain_two, shift_two = table[5], table[6]
    bias_fc1, bias_fc2 = vector(7, 7 + per), table[7 + per]
    o_mine, o_sent, lse = attention_forward(qkv, half, valid)
    o_got = other(o_sent)
    out_mine = lax.dynamic_slice_in_dim(out_full, here * group, group, axis=0)
    out_other = lax.dynamic_slice_in_dim(out_full, group - here * group, group, axis=0)
    residual = pad(frames_in).astype(F32) + dot(o_mine, out_mine) + dot(o_got, out_other) + bias_out

    normed_two, _ = normalize(residual)
    hidden_two = (normed_two * gain_two + shift_two).astype(BF)
    pre_act = dot(hidden_two, fc1_full) + bias_fc1
    cdf = gelu_cdf(pre_act)
    density = jnp.exp(-0.5 * pre_act * pre_act) * (1.0 / math.sqrt(2.0 * math.pi))
    activated, slope = lax.optimization_barrier(
        ((pre_act * cdf).astype(BF), (cdf + pre_act * density).astype(BF))
    )
    flag = jnp.full((1,), here, jnp.int32)
    (
        grad_pre_low, fc2_full, grad_residual, grad_residual_low,
        do_mine, do_sent, grad_bias_fc1, grad_sums,
    ) = feed_back(flag, weights, slope, cotangent, residual, gain_two[None], part)
    do_got = other(do_sent)
    parity = jnp.full((1,), lax.rem(me, 2), jnp.int32)
    fc2_keep, fc2_give = third_gradient(parity, activated, cotangent, size, do_sent)
    second_part = second_gradient(
        flag, fc2_give, o_mine, o_got, grad_residual_low, hidden_two, grad_pre_low
    )
    grad_second = lax.psum_scatter(second_part, "dp", scatter_dimension=0, tiled=True)

    def backward(token, start, count):
        return attention_backward(
            qkv, o_mine, o_sent, do_mine, do_got, lse, token, half, valid, start, count
        )

    x = fc2_keep.astype(F32) + swap(fc2_give, "dp", size, 1).astype(F32)
    x = x.reshape(size // 2, 2, -1, wide)
    keep, give = pick(x, 1, here).astype(BF), pick(x, 1, 1 - here).astype(BF)
    got = other(give)
    pairs = group // 128
    ds = [backward(give, 0, pairs - 1)]
    for at in range(len(bits) - 2, -1, -1):
        keep, got = after((keep, got), ds[0])
        x = keep.astype(F32) + got.astype(F32)
        keep, give = halve(x.reshape(-1, 2, *x.shape[1:]), 1, bits[at])
        keep, got = keep.astype(BF), swap(give, "dp", size, bits[at])
    fc2_keep_x, fc2_got_x = keep, got
    ds.append(backward(give, pairs - 1, 1))

    vectors = [(7, grad_bias_fc1)]
    if part % 16:
        grad_qkv, norm_sums, sums = projection_weight_gradient(normed_t, w_full, scale, ds)
        grad_bias_mine = jnp.stack([sums[0, :group], sums[0, 2 * group :]])
        zero = jnp.zeros_like(grad_bias_mine)
        grad_bias_qv = jnp.where(
            here == 0,
            jnp.concatenate([grad_bias_mine, zero], axis=1),
            jnp.concatenate([zero, grad_bias_mine], axis=1),
        )

        def as_columns(start, v):
            v = v.reshape(size, -1, part).transpose(0, 2, 1)
            return jnp.pad(v, ((0, 0), (0, 0), (start, 128 - start - v.shape[2])))

        columns = norm_sums.reshape(size, part, 128) + as_columns(2, grad_bias_qv)
        vectors += [(p, grad_sums[i]) for i, p in enumerate((4, 5, 6, 7 + per))]
        columns = columns + sum(as_columns(start, v) for start, v in vectors)
        x = jnp.concatenate([grad_qkv.reshape(size, part, -1), columns.astype(BF)], axis=2)
        keep, give = halve(x.reshape(size // 2, 2, *x.shape[1:]), 1, 1)
    else:
        sides = jnp.concatenate([parity, jnp.full((1,), here, jnp.int32)])
        keep, give = spread_weight_gradient(
            sides, ds[1], normed_t, w_full, scale, ds, grad_bias_fc1, grad_sums, part
        )
    got = swap(give, "dp", size, 1)
    for at in range(len(bits) - 2, -1, -1):
        x = keep.astype(F32) + got.astype(F32)
        keep, give = halve(x.reshape(-1, 2, *x.shape[1:]), 1, bits[at])
        got = swap(give, "dp", size, bits[at])
    fc2_keep, fc2_got = after((fc2_keep_x, fc2_got_x), give)
    fc2_gives, fc2_stay = scatter_split(fc2_keep.astype(F32) + fc2_got.astype(F32), size)
    grad_other, grad_mine = projection_input_gradient(w_flipped, ds, fc2_gives[2], half)
    grad_got = other(grad_other)
    output = dot(after(activated, *fc2_gives), fc2_full)
    output = residual + output + bias_fc2
    frames_out = output.astype(BF)[:valid][None]
    fc2_part = scatter_join(fc2_stay, fc2_gives, size).astype(BF)
    gives, stay = scatter_split(keep.astype(F32) + got.astype(F32), size)
    grad_input = input_end(
        grad_mine, grad_got, grad_residual, normed_both, gain_one[None], inverse_one, valid
    ).transpose(1, 0, 2)
    mine = scatter_join(stay, gives, size).astype(BF)
    theirs = other(mine)
    spans = ((0, 1), (1, 2), (2, 4), (4, 5), (5, 6), (6, 7), (7, 7 + per), (7 + per, 8 + per))
    grad_w_qkv, *small = finish(flag, mine, theirs, spans)
    small = [v[0] for v in small]
    fc2_got = other(fc2_part)
    fc2_sum = jnp.where(
        here == 0,
        jnp.concatenate([fc2_part, fc2_got], axis=0),
        jnp.concatenate([fc2_got, fc2_part], axis=0),
    ).astype(F32)
    out_sum, first_sum = join_second(grad_second, other(grad_second), wide)
    return (
        frames_out, grad_input, small[0], small[1], grad_w_qkv, small[2], out_sum, small[3],
        small[4], small[5], first_sum, small[6], fc2_sum, small[7],
    )


def solution(mesh):
    frames, rows, vector = P("dp", "seq", None), P("dp", None), P("dp")
    in_specs = (
        frames, vector, vector, rows, vector, rows, vector,
        vector, vector, rows, vector, rows, vector, frames,
    )
    out_specs = (
        frames, frames, vector, vector, rows, vector, rows, vector,
        vector, vector, rows, vector, rows, vector,
    )
    return jax.shard_map(
        functools.partial(layer, mesh.shape["dp"]),
        mesh=mesh, in_specs=in_specs, out_specs=out_specs, check_vma=False,
    )
```

time: 354 us -> 325 us (0.918)
  Pallas kernels: 71.7 us -> 154 us
  matrix products: 82.7 us -> 18.2 us
  local copies, waits for them, and re-layouts: 57.6 us -> 20.4 us
  other arithmetic: 32.8 us -> 14.2 us
  waiting for transfers between devices: 65.9 us -> 71.7 us
  starting transfers between devices: 22.5 us -> 27.1 us
    pallas_call x1 -> x13, Pallas kernels: 42.7 us -> 133 us  [the longest x2 44 us: attention_backward(): pl.pallas_call(functools.partial(backward_kernel, half, valid), grid=(cou...]
    dot_general x13 -> x4, matrix products: 82.7 us -> 18.2 us  [dot(): lax.dot_general(a, b, (((ca,), (cb,)), ((), ())), preferred_element_type=...]
    all_gather x2 -> x1, waiting for transfers between devices: 0.01 us -> 17 us  [layer(): lax.all_gather(jnp.concatenate([fc2_local, w_o, w_fc1], axis=1), 'dp', ax...]
    reduce_sum x6 -> x0, other arithmetic: 13.6 us -> none  [the longest x1 6.83 us: shards(): grad_gain_one = jnp.sum(grad_both * normed_both, axis=0)]
    ppermute x17 -> x23, waiting for transfers between devices: 65.7 us -> 54.6 us  [swap(): return lax.ppermute(x, axis, [(i, i ^ bit) for i in range(size)])]
    reshape x15 -> x5, local copies, waits for them, and re-layouts: 10.7 us -> 1.53 us  [the longest x1 1.23 us: layer(): w_fc2.reshape(per, part, wide).transpose(1, 0, 2).reshape(part, ff)]
    pallas_call x1, Pallas kernels: 29 us -> 20.8 us  [attention_forward(): pl.pallas_call(functools.partial(forward_kernel, half, valid), grid=(pair...]
    slice x18 -> x3, local copies, waits for them, and re-layouts: 8.97 us -> 1.96 us  [the longest x1 1.35 us: layer(): out_full, fc1_full = (later[:, ff:ff + wide], later[:, ff + wide:])]
  transfers between devices with their start and end apart: 21 -> 25, of which waited for: 11 -> 9; matrix products, arithmetic and copies ran while one was open for 47% -> 9% of each run, Pallas kernels for 21% -> 38%
where the time goes in v2:
time: 325 us; the launch traced here: 320 us
  Pallas kernels  154 us (47%)
  waiting for transfers between devices  71.7 us (22%)
  starting transfers between devices  27.1 us (8%)
  local copies, waits for them, and re-layouts  20.4 us (6%)
  matrix products  18.2 us (6%)
  between operations  14.8 us (5%)
  other arithmetic  14.2 us (4%)
    ppermute x23, waiting for transfers between devices, swap(): return lax.ppermute(x, axis, [(i, i ^ bit) for i in range(size)])  54.6 us
    pallas_call x2, Pallas kernels, attention_backward(): pl.pallas_call(functools.partial(backward_kernel, half, valid), grid=(cou...  44 us
    ppermute x23, starting transfers between devices, swap(): return lax.ppermute(x, axis, [(i, i ^ bit) for i in range(size)])  27 us
    pallas_call x1, Pallas kernels, feed_back(): pl.pallas_call(functools.partial(feed_back_kernel, part), grid_spec=pltpu...  21.9 us
    pallas_call x1, Pallas kernels, attention_forward(): pl.pallas_call(functools.partial(forward_kernel, half, valid), grid=(pair...  20.8 us
    dot_general x4, matrix products, dot(): lax.dot_general(a, b, (((ca,), (cb,)), ((), ())), preferred_element_type=...  18.2 us
    all_gather x1, waiting for transfers between devices, layer(): lax.all_gather(jnp.concatenate([fc2_local, w_o, w_fc1], axis=1), 'dp', ax...  17 us
    pallas_call x1, Pallas kernels, spread_weight_gradient(): pl.pallas_call(functools.partial(spread_kernel, part, len(ds), bias.shape...  12.5 us
  transfers between devices with their start and end apart: 25, of which 9 were waited for; matrix products, arithmetic and copies ran while one was open for 9% of the time, Pallas kernels for 38%

profile of v2, /device:TPU:0, one launch (start us, length us, event | category | flops | bytes accessed | tf_op | source)
XLA Modules:
  0.0 320.1 jit_solution(11549282320158183735)
XLA Ops:
  8.6 1.9 pad_maximum_fusion
  11.0 3.1 collective-permute-start
  14.2 2.6 collective-permute-start.1
  19.2 9.2 %collective-permute-done.1 = bf16[48,1280]{1,0:T(8,128)(2,1)S(1)} collective-permute-done((bf16[48,1280]{1,0:T(8,128)(2,1)S(1)}, bf16[48,1280]{1,0:T(8,128)(2,1)S(1)}, u32[]{:S(2)}, u32[]{:S(2)}) %collective-permute-start.1) | collective-permute-done | bytes 122912 | tf_op jit(solution)/shard_map/ppermute | solution.py:787
  32.0 9.8 %collective-permute-done.3 = bf16[4,48,1280]{2,1,0:T(8,128)(2,1)S(1)} collective-permute-done((bf16[4,48,1280]{2,1,0:T(8,128)(2,1)S(1)}, bf16[4,48,1280]{2,1,0:T(8,128)(2,1)S(1)}, u32[]{:S(2)}, u32[]{:S(2)}) %collective-permute-start.3) | collective-permute-done | bytes 491552 | tf_op jit(solution)/shard_map/ppermute | solution.py:787
  44.7 4.1 %prepare.2 = (f32[1536,768]{1,0:T(8,128)}, bf16[784,1536]{1,0:T(8,128)(2,1)}, f32[768,1]{1,0:T(8,128)}) custom-call(bf16[1,750,768]{2,1,0:T(8,128)(2,1)} %x_ref.1), custom_call_target="tpu_custom_call" | custom-call | flops 9437184 | bytes 4718592 | tf_op jit(solution)/shard_map/prepare/pallas_call | solution.py:201
  50.4 4.1 %prepare.3 = (f32[1536,768]{1,0:T(8,128)}, bf16[784,1536]{1,0:T(8,128)(2,1)}, f32[768,1]{1,0:T(8,128)}) custom-call(bf16[1,750,768]{2,1,0:T(8,128)(2,1)} %copy-done.11, f32[1536,768]{1,0:T(8,128)} %get-tuple-element.59.refs_0_, bf16[784,1536]{1,0:T(8,128)(2,1)} %get-tuple-element.60.refs_1_), custom_call_target="tpu_custom_call", output_to_operand_aliasing={{0}: (1, {}), {1}: (2, {})} | custom-call | flops 9437184 | bytes 4718592 | tf_op jit(solution)/shard_map/prepare/pallas_call | solution.py:201
  55.5 9.5 %projection.1 = (bf16[1536,1152]{1,0:T(8,128)(2,1)}, bf16[768,1152]{1,0:T(8,128)(2,1)}, bf16[1152,768]{1,0:T(8,128)(2,1)}, f32[16,768]{1,0:T(8,128)}, f32[768,128]{1,0:T(8,128)}) custom-call(s32[17]{0:T(128)} %pad_add_fusion.place_ref, bf16[16,48,1280]{2,1,0:T(8,128)(2,1)} %constant_dynamic-update-slice_fusion.5.held_ref, ...), custom_call_target="tpu_custom_call" | custom-call | flops 2717908992 | bytes 9437184 | tf_op jit(solution)/shard_map/projection/pallas_call | solution.py:268
  65.0 20.8 %attention_forward.1 = (bf16[768,384]{1,0:T(8,128)(2,1)}, bf16[768,384]{1,0:T(8,128)(2,1)}, f32[3,8,1536]{2,1,0:T(8,128)}) custom-call(bf16[1536,1152]{1,0:T(8,128)(2,1)} %get-tuple-element.62.q_ref.k_ref.v_ref, bf16[1536,1152]{1,0:T(8,128)(2,1)} %get-tuple-element.62.q_ref.k_ref.v_ref, bf16[1536,1152]{1,0:T(8,128)(2,1)} %get-tuple-element.62.q_ref.k_ref.v_ref), custom_call_target="tpu_custom_call" | custom-call | flops 14495514624 | bytes 5308416 | tf_op jit(solution)/shard_map/attention_forward/pallas_call | solution.py:68
  88.1 17.0 %all-gather.2.cloned.1.call-done.fc2_ref.fc1_ref.out_ref = bf16[768,6912]{1,0:T(8,128)(2,1)} async-done(((bf16[48,6912]{1,0:T(8,128)(2,1)}), bf16[768,6912]{1,0:T(8,128)(2,1)}) %all-gather.2.cloned.1.call-update) | async-done | bytes 10616848 | tf_op jit(solution)/shard_map/all_gather | solution.py:887
  110.1 2.5 copy-done.1
  112.6 9.0 %fusion.4 = (bf16[768,3072]{1,0:T(8,128)(2,1)}, bf16[768,3072]{1,0:T(8,128)(2,1)}) fusion(f32[3072]{0:T(1024)S(1)} %add.194, bf16[768,768]{1,0:T(8,128)(2,1)S(1)} %add_convert_fusion.h_ref, bf16[768,6912]{1,0:T(8,128)(2,1)S(1)} %copy-done.1), kind=kOutput, calls=%fused_computation.6 | convolution fusion | flops 3652190208 | bytes 15347712 | tf_op jit(solution)/shard_map/dot_general | solution.py:19
  121.6 21.9 %feed_back.1 = (bf16[768,3072]{1,0:T(8,128)(2,1)}, bf16[3072,768]{1,0:T(8,128)(2,1)}, f32[768,768]{1,0:T(8,128)}, bf16[768,768]{1,0:T(8,128)(2,1)}, bf16[768,384...) custom-call(s32[1]{0:T(128)} %bitcast.2.place_ref, ...), custom_call_target="tpu_custom_call" | custom-call | flops 7247757312 | bytes 23592960 | tf_op jit(solution)/shard_map/feed_back/pallas_call | solution.py:669
  143.5 8.4 %third_gradient.1 = (bf16[8,192,768]{2,1,0:T(8,128)(2,1)}, bf16[8,192,768]{2,1,0:T(8,128)(2,1)}) custom-call(s32[1]{0:T(128)} %bitcast.11.place_ref, bf16[768,3072]{1,0:T(8,128)(2,1)} %get-tuple-element.84.z_ref, bf16[1,750,768]{2,1,0:T(8,128)(2,1)} %cot_ref.3, bf16[768,384]{1,0:T(8,128)(2,1)} %get-tuple-element.68.token_ref), custom_call_target="tpu_custom_call" | custom-call | flops 3623878656 | bytes 9437184 | tf_op jit(solution)/shard_map/third_gradient/pallas_call | solution.py:568
  154.2 10.2 %second_gradient.1 = bf16[768,3840]{1,0:T(8,128)(2,1)} custom-call(s32[1]{0:T(128)} %bitcast.2.place_ref, bf16[8,192,768]{2,1,0:T(8,128)(2,1)} %get-tuple-element.70.token_ref, bf16[768,384]{1,0:T(8,128)(2,1)} %get-tuple-element.63.o_mine_ref.mine_ref, bf16[768,384]{1,0:T(8,128)(2,1)} %copy-done.12, bf16[768,768]{1,0:T(8,128)(2,1)} %get-tuple-element.95.drb_ref, ...), custom_call_target="tpu_custom_call" | custom-call | flops 4529848320 | bytes 9437184 | tf_op jit(solution)/shard_map/second_gradient/pallas_call | solution.py:515
  166.1 2.3 convert_add_fusion
  169.6 28.5 %attention_backward.2.refs_0_ = bf16[3,1536,256]{2,1,0:T(8,128)(2,1)} custom-call(bf16[1536,1152]{1,0:T(8,128)(2,1)} %get-tuple-element.62.q_ref.k_ref.v_ref, bf16[1536,1152]{1,0:T(8,128)(2,1)} %get-tuple-element.62.q_ref.k_ref.v_ref, bf16[1536,1152]{1,0:T(8,128)(2,1)} %get-tuple-element.62.q_ref.k_ref.v_ref, ...), custom_call_target="tpu_custom_call" | custom-call | flops 19327352832 | bytes 6291456 | tf_op jit(solution)/shard_map/attention_backward/pallas_call | solution.py:158
  199.5 15.5 %attention_backward.3.token_ref.refs_1_ = bf16[3,1536,128]{2,1,0:T(8,128)(2,1)} custom-call(bf16[1536,1152]{1,0:T(8,128)(2,1)} %get-tuple-element.62.q_ref.k_ref.v_ref, bf16[1536,1152]{1,0:T(8,128)(2,1)} %get-tuple-element.62.q_ref.k_ref.v_ref, bf16[1536,1152]{1,0:T(8,128)(2,1)} %get-tuple-element.62.q_ref.k_ref.v_ref, ...), custom_call_target="tpu_custom_call" | custom-call | flops 9663676416 | bytes 3145728 | tf_op jit(solution)/shard_map/attention_backward/pallas_call | solution.py:158
  215.0 12.5 %spread_weight_gradient.1 = (bf16[8,48,1280]{2,1,0:T(8,128)(2,1)}, bf16[8,48,1280]{2,1,0:T(8,128)(2,1)}) custom-call(s32[2]{0:T(128)} %pad_add_fusion.1.place_ref, bf16[3,1536,128]{2,1,0:T(8,128)(2,1)} %attention_backward.3.token_ref.refs_1_, bf16[784,1536]{1,0:T(8,128)(2,1)} %get-tuple-element.75.xt_ref, bf16[768,1152]{1,0:T(8,128)(2,1)} %get-tuple-element.76.w_ref, ...), custom_call_target="tpu_custom_call" | custom-call | flops 2717908992 | bytes 4718592 | tf_op jit(solution)/shard_map/spread_weight_gradient/pallas_call | solution.py:424
  228.1 2.2 collective-permute-done.11
  233.1 14.8 %collective-permute-done.10 = bf16[4,96,768]{2,1,0:T(8,128)(2,1)S(1)} collective-permute-done((bf16[4,96,768]{2,1,0:T(8,128)(2,1)}, bf16[4,96,768]{2,1,0:T(8,128)(2,1)S(1)}, u32[]{:S(2)}, u32[]{:S(2)}) %collective-permute-start.10) | collective-permute-done | bytes 589856 | tf_op jit(solution)/shard_map/ppermute | solution.py:787
  251.1 2.1 collective-permute-start.21
  253.3 7.4 %projection_input_gradient.1 = (bf16[768,768]{1,0:T(8,128)(2,1)}, f32[768,768]{1,0:T(8,128)}) custom-call(bf16[96,768]{1,0:T(8,128)(2,1)} %get-tuple-element.112.token_ref, bf16[1152,768]{1,0:T(8,128)(2,1)} %get-tuple-element.86.wt_ref, bf16[3,1536,256]{2,1,0:T(8,128)(2,1)} %attention_backward.2.refs_0_, ...), custom_call_target="tpu_custom_call" | custom-call | flops 2717908992 | bytes 7077888 | tf_op jit(solution)/shard_map/projection_input_gradient/pallas_call | solution.py:467
  261.6 7.4 %fusion.37 = f32[768,768]{1,0:T(8,128)S(1)} fusion(bf16[768,3072]{1,0:T(8,128)(2,1)} %get-tuple-element.84.z_ref, bf16[3072,768]{1,0:T(8,128)(2,1)} %get-tuple-element.85), kind=kOutput, calls=%fused_computation.92 | convolution fusion | flops 3623878656 | bytes 11796480 | tf_op jit(solution)/shard_map/dot_general | solution.py:19
  271.7 2.2 collective-permute-start.15
  273.9 2.2 collective-permute-start.16
  279.7 2.9 collective-permute-done.15
  284.7 8.2 %collective-permute-done.22 = bf16[96,768]{1,0:T(8,128)(2,1)S(1)} collective-permute-done((bf16[96,768]{1,0:T(8,128)(2,1)S(1)}, bf16[96,768]{1,0:T(8,128)(2,1)S(1)}, u32[]{:S(2)}, u32[]{:S(2)}) %collective-permute-start.22) | collective-permute-done | bytes 147488 | tf_op jit(solution)/shard_map/ppermute | solution.py:787
  293.8 7.0 %collective-permute-done.17.theirs_ref = bf16[48,1280]{1,0:T(8,128)(2,1)S(1)} collective-permute-done((bf16[48,1280]{1,0:T(8,128)(2,1)S(1)}, bf16[48,1280]{1,0:T(8,128)(2,1)S(1)}, u32[]{:S(2)}, u32[]{:S(2)}) %collective-permute-start.17) | collective-permute-done | bytes 122912 | tf_op jit(solution)/shard_map/ppermute | solution.py:787
  301.5 1.8 finish.1
  303.3 6.9 %input_end.1 = f32[750,1,768]{2,1,0:T(1,128)} custom-call(f32[768,768]{1,0:T(8,128)} %get-tuple-element.87.mine_ref, bf16[768,768]{1,0:T(8,128)(2,1)} %collective-permute-done.12.got_ref, f32[768,768]{1,0:T(8,128)} %get-tuple-element.89.residual_ref, f32[1536,768]{1,0:T(8,128)} %get-tuple-element.61.x_ref.normed_ref, f32[1,768]{1,0:T(1,128)} %get-tuple-element.135.gain_ref, ...), custom_call_target="tpu_custom_call" | custom-call | flops 5898240 | bytes 10616832 | tf_op jit(solution)/shard_map/input_end/pallas_call | solution.py:770
  311.0 2.0 join_second.1
  (139 shorter events, 44.9 us)
Async XLA Ops:
  7.3 9.5 %copy-start.4 = (bf16[1,750,768]{2,1,0:T(8,128)(2,1)S(1)}, bf16[1,750,768]{2,1,0:T(8,128)(2,1)}, u32[]{:S(2)}) copy-start(bf16[1,750,768]{2,1,0:T(8,128)(2,1)} %x_ref.1) | copy-start | bytes 3456004
  7.3 97.8 %all-gather.2.cloned.1.call-start = ((), (), s32[]{:S(2)}) async-start(), calls=%async_computation.1 | async-start | bytes 11280384 | tf_op jit(solution)/shard_map/all_gather | solution.py:887
  10.5 33.5 %copy-start = (s32[16]{0:T(128)S(1)}, s32[16]{0:T(128)}, u32[]{:S(2)}) copy-start(s32[16]{0:T(128)} %constant.122.clone) | copy-start | bytes 196
  10.5 268.0 %reduce-scatter.2.cloned.1.call-start = ((), (), s32[]{:S(2)}) async-start(), calls=%async_computation.2 | async-start | bytes 6266880 | tf_op jit(solution)/shard_map/reduce_scatter | solution.py:932
  11.0 8.1 %collective-permute-start = (bf16[48,1280]{1,0:T(8,128)(2,1)S(1)}, bf16[48,1280]{1,0:T(8,128)(2,1)S(1)}, u32[]{:S(2)}, u32[]{:S(2)}) collective-permute-start(bf16[48,1280]{1,0:T(8,128)(2,1)S(1)} %get-tuple-element.134), channel_id=1, source_target_pairs={{0,8},{2,10},{4,12},{6,14},{8,0},{10,2},{12,4},{14,6},{16,24},{18,... | collective-permute-start | bytes 368648 | tf_op jit(solution)/shard_map/ppermute | solution.py:787
  14.2 14.2 %collective-permute-start.1 = (bf16[48,1280]{1,0:T(8,128)(2,1)S(1)}, bf16[48,1280]{1,0:T(8,128)(2,1)S(1)}, u32[]{:S(2)}, u32[]{:S(2)}) collective-permute-start(bf16[48,1280]{1,0:T(8,128)(2,1)S(1)} %get-tuple-element.134), channel_id=1, source_target_pairs={{0,16},{2,18},{4,20},{6,22},{8,24},{10,26},{12,28},{14,30},{16,0},... | collective-permute-start | bytes 368648 | tf_op jit(solution)/shard_map/ppermute | solution.py:787
  16.7 11.6 %collective-permute-start.2 = (bf16[48,1280]{1,0:T(8,128)(2,1)S(1)}, bf16[48,1280]{1,0:T(8,128)(2,1)S(1)}, u32[]{:S(2)}, u32[]{:S(2)}) collective-permute-start(bf16[48,1280]{1,0:T(8,128)(2,1)S(1)} %get-tuple-element.134), channel_id=1, source_target_pairs={{0,24},{2,26},{4,28},{6,30},{8,16},{10,18},{12,20},{14,22},{16,8},... | collective-permute-start | bytes 368648 | tf_op jit(solution)/shard_map/ppermute | solution.py:787
  16.7 32.6 %collective-permute-start.5 = (bf16[1,750,768]{2,1,0:T(8,128)(2,1)S(1)}, bf16[1,750,768]{2,1,0:T(8,128)(2,1)S(1)}, u32[]{:S(2)}, u32[]{:S(2)}) collective-permute-start(bf16[1,750,768]{2,1,0:T(8,128)(2,1)S(1)} %copy-done.4), channel_id=1, source_target_pairs={{0,1},{1,0},{2,3},{3,2},{4,5},{5,4},{6,7},{7,6},{8,9},{9,8},{10,11... | collective-permute-start | bytes 3456008 | tf_op jit(solution)/shard_map/ppermute | solution.py:787
  28.4 13.4 %collective-permute-start.3 = (bf16[4,48,1280]{2,1,0:T(8,128)(2,1)S(1)}, bf16[4,48,1280]{2,1,0:T(8,128)(2,1)S(1)}, u32[]{:S(2)}, u32[]{:S(2)}) collective-permute-start(bf16[4,48,1280]{2,1,0:T(8,128)(2,1)S(1)} %pad_maximum_fusion.1), channel_id=1, source_target_pairs={{0,4},{2,6},{4,0},{6,2},{8,12},{10,14},{12,8},{14,10},{16,20},{18,... | collective-permute-start | bytes 1474568 | tf_op jit(solution)/shard_map/ppermute | solution.py:787
  44.0 10.5 %collective-permute-start.4 = (bf16[8,48,1280]{2,1,0:T(8,128)(2,1)}, bf16[8,48,1280]{2,1,0:T(8,128)(2,1)S(1)}, u32[]{:S(2)}, u32[]{:S(2)}) collective-permute-start(bf16[8,48,1280]{2,1,0:T(8,128)(2,1)} %get-tuple-element.120), channel_id=1, source_target_pairs={{0,2},{2,0},{4,6},{6,4},{8,10},{10,8},{12,14},{14,12},{16,18},{18,... | collective-permute-start | bytes 2949128 | tf_op jit(solution)/shard_map/ppermute | solution.py:787
  65.0 22.3 %copy-start.18 = (f32[16,768]{1,0:T(8,128)S(1)}, f32[16,768]{1,0:T(8,128)}, u32[]{:S(2)}) copy-start(f32[16,768]{1,0:T(8,128)} %get-tuple-element.65) | copy-start | bytes 147460
  85.8 20.7 %copy-start.13 = (bf16[768,384]{1,0:T(8,128)(2,1)S(1)}, bf16[768,384]{1,0:T(8,128)(2,1)}, u32[]{:S(2)}) copy-start(bf16[768,384]{1,0:T(8,128)(2,1)} %get-tuple-element.63.o_mine_ref.mine_ref) | copy-start | bytes 1769476
  85.8 21.4 %collective-permute-start.6 = (bf16[768,384]{1,0:T(8,128)(2,1)}, bf16[768,384]{1,0:T(8,128)(2,1)S(1)}, u32[]{:S(2)}, u32[]{:S(2)}) collective-permute-start(bf16[768,384]{1,0:T(8,128)(2,1)} %get-tuple-element.64.o_sent_ref), channel_id=1, source_target_pairs={{0,1},{1,0},{2,3},{3,2},{4,5},{5,4},{6,7},{7,6},{8,9},{9,8},{10,11... | collective-permute-start | bytes 1769480 | tf_op jit(solution)/shard_map/ppermute | solution.py:787
  112.6 9.0 %copy-start.9 = (bf16[768,768]{1,0:T(8,128)(2,1)}, bf16[768,768]{1,0:T(8,128)(2,1)S(1)}, u32[]{:S(2)}) copy-start(bf16[768,768]{1,0:T(8,128)(2,1)S(1)} %add_convert_fusion.h_ref) | copy-start | bytes 3538948
  151.9 12.6 %collective-permute-start.7 = (bf16[8,192,768]{2,1,0:T(8,128)(2,1)}, bf16[8,192,768]{2,1,0:T(8,128)(2,1)}, u32[]{:S(2)}, u32[]{:S(2)}) collective-permute-start(bf16[8,192,768]{2,1,0:T(8,128)(2,1)} %get-tuple-element.70.token_ref), channel_id=1, source_target_pairs={{0,2},{2,0},{4,6},{6,4},{8,10},{10,8},{12,14},{14,12},{16,18},{18,... | collective-permute-start | bytes 7077896 | tf_op jit(solution)/shard_map/ppermute | solution.py:787
  152.7 16.5 %collective-permute-start.9 = (bf16[768,384]{1,0:T(8,128)(2,1)}, bf16[768,384]{1,0:T(8,128)(2,1)}, u32[]{:S(2)}, u32[]{:S(2)}) collective-permute-start(bf16[768,384]{1,0:T(8,128)(2,1)} %get-tuple-element.68.token_ref), channel_id=1, source_target_pairs={{0,1},{1,0},{2,3},{3,2},{4,5},{5,4},{6,7},{7,6},{8,9},{9,8},{10,11... | collective-permute-start | bytes 1769480 | tf_op jit(solution)/shard_map/ppermute | solution.py:787
  168.6 29.5 %collective-permute-start.8 = (bf16[8,96,768]{2,1,0:T(8,128)(2,1)S(1)}, bf16[8,96,768]{2,1,0:T(8,128)(2,1)S(1)}, u32[]{:S(2)}, u32[]{:S(2)}) collective-permute-start(bf16[8,96,768]{2,1,0:T(8,128)(2,1)S(1)} %get-tuple-element.110.token_ref), channel_id=1, source_target_pairs={{0,1},{1,0},{2,3},{3,2},{4,5},{5,4},{6,7},{7,6},{8,9},{9,8},{10,11... | collective-permute-start | bytes 3538952 | tf_op jit(solution)/shard_map/ppermute | solution.py:787
  227.6 2.8 collective-permute-start.11
  227.6 20.4 %collective-permute-start.10 = (bf16[4,96,768]{2,1,0:T(8,128)(2,1)}, bf16[4,96,768]{2,1,0:T(8,128)(2,1)S(1)}, u32[]{:S(2)}, u32[]{:S(2)}) collective-permute-start(bf16[4,96,768]{2,1,0:T(8,128)(2,1)} %get-tuple-element.115.token_ref), channel_id=1, source_target_pairs={{0,4},{2,6},{4,0},{6,2},{8,12},{10,14},{12,8},{14,10},{16,20},{18,... | collective-permute-start | bytes 1769480 | tf_op jit(solution)/shard_map/ppermute | solution.py:787
  230.3 17.6 %copy-start.8 = (bf16[4,96,768]{2,1,0:T(8,128)(2,1)S(1)}, bf16[4,96,768]{2,1,0:T(8,128)(2,1)}, u32[]{:S(2)}) copy-start(bf16[4,96,768]{2,1,0:T(8,128)(2,1)} %get-tuple-element.82) | copy-start | bytes 1769476
  232.7 37.7 %collective-permute-start.13 = (bf16[4,48,1280]{2,1,0:T(8,128)(2,1)}, bf16[4,48,1280]{2,1,0:T(8,128)(2,1)}, u32[]{:S(2)}, u32[]{:S(2)}) collective-permute-start(bf16[4,48,1280]{2,1,0:T(8,128)(2,1)} %fusion.17), channel_id=1, source_target_pairs={{0,4},{2,6},{4,0},{6,2},{8,12},{10,14},{12,8},{14,10},{16,20},{18,... | collective-permute-start | bytes 1474568 | tf_op jit(solution)/shard_map/ppermute | solution.py:787
  248.9 22.8 %collective-permute-start.19 = (bf16[96,768]{1,0:T(8,128)(2,1)}, bf16[96,768]{1,0:T(8,128)(2,1)S(1)}, u32[]{:S(2)}, u32[]{:S(2)}) collective-permute-start(bf16[96,768]{1,0:T(8,128)(2,1)} %get-tuple-element.114), channel_id=1, source_target_pairs={{0,8},{2,10},{4,12},{6,14},{8,0},{10,2},{12,4},{14,6},{16,24},{18,... | collective-permute-start | bytes 442376 | tf_op jit(solution)/shard_map/ppermute | solution.py:787
  249.5 24.4 %collective-permute-start.20 = (bf16[96,768]{1,0:T(8,128)(2,1)}, bf16[96,768]{1,0:T(8,128)(2,1)S(1)}, u32[]{:S(2)}, u32[]{:S(2)}) collective-permute-start(bf16[96,768]{1,0:T(8,128)(2,1)} %get-tuple-element.113), channel_id=1, source_target_pairs={{0,16},{2,18},{4,20},{6,22},{8,24},{10,26},{12,28},{14,30},{16,0},... | collective-permute-start | bytes 442376 | tf_op jit(solution)/shard_map/ppermute | solution.py:787
  251.1 24.9 %collective-permute-start.21 = (bf16[96,768]{1,0:T(8,128)(2,1)}, bf16[96,768]{1,0:T(8,128)(2,1)}, u32[]{:S(2)}, u32[]{:S(2)}) collective-permute-start(bf16[96,768]{1,0:T(8,128)(2,1)} %get-tuple-element.112.token_ref), channel_id=1, source_target_pairs={{0,24},{2,26},{4,28},{6,30},{8,16},{10,18},{12,20},{14,22},{16,8},... | collective-permute-start | bytes 442376 | tf_op jit(solution)/shard_map/ppermute | solution.py:787
  260.7 42.6 %collective-permute-start.12 = (bf16[768,768]{1,0:T(8,128)(2,1)}, bf16[768,768]{1,0:T(8,128)(2,1)}, u32[]{:S(2)}, u32[]{:S(2)}) collective-permute-start(bf16[768,768]{1,0:T(8,128)(2,1)} %get-tuple-element.88), channel_id=1, source_target_pairs={{0,1},{1,0},{2,3},{3,2},{4,5},{5,4},{6,7},{7,6},{8,9},{9,8},{10,11... | collective-permute-start | bytes 3538952 | tf_op jit(solution)/shard_map/ppermute | solution.py:787
  271.6 6.9 %collective-permute-start.14 = (bf16[48,1280]{1,0:T(8,128)(2,1)S(1)}, bf16[48,1280]{1,0:T(8,128)(2,1)S(1)}, u32[]{:S(2)}, u32[]{:S(2)}) collective-permute-start(bf16[48,1280]{1,0:T(8,128)(2,1)S(1)} %get-tuple-element.117), channel_id=1, source_target_pairs={{0,8},{2,10},{4,12},{6,14},{8,0},{10,2},{12,4},{14,6},{16,24},{18,... | collective-permute-start | bytes 368648 | tf_op jit(solution)/shard_map/ppermute | solution.py:787
  271.7 11.0 %collective-permute-start.15 = (bf16[48,1280]{1,0:T(8,128)(2,1)S(1)}, bf16[48,1280]{1,0:T(8,128)(2,1)S(1)}, u32[]{:S(2)}, u32[]{:S(2)}) collective-permute-start(bf16[48,1280]{1,0:T(8,128)(2,1)S(1)} %get-tuple-element.119), channel_id=1, source_target_pairs={{0,16},{2,18},{4,20},{6,22},{8,24},{10,26},{12,28},{14,30},{16,0},... | collective-permute-start | bytes 368648 | tf_op jit(solution)/shard_map/ppermute | solution.py:787
  273.9 8.8 %collective-permute-start.16 = (bf16[48,1280]{1,0:T(8,128)(2,1)S(1)}, bf16[48,1280]{1,0:T(8,128)(2,1)S(1)}, u32[]{:S(2)}, u32[]{:S(2)}) collective-permute-start(bf16[48,1280]{1,0:T(8,128)(2,1)S(1)} %get-tuple-element.118), channel_id=1, source_target_pairs={{0,24},{2,26},{4,28},{6,30},{8,16},{10,18},{12,20},{14,22},{16,8},... | collective-permute-start | bytes 368648 | tf_op jit(solution)/shard_map/ppermute | solution.py:787
  277.1 15.8 %collective-permute-start.22 = (bf16[96,768]{1,0:T(8,128)(2,1)S(1)}, bf16[96,768]{1,0:T(8,128)(2,1)S(1)}, u32[]{:S(2)}, u32[]{:S(2)}) collective-permute-start(bf16[96,768]{1,0:T(8,128)(2,1)S(1)} %fusion.21), channel_id=1, source_target_pairs={{0,1},{1,0},{2,3},{3,2},{4,5},{5,4},{6,7},{7,6},{8,9},{9,8},{10,11... | collective-permute-start | bytes 442376 | tf_op jit(solution)/shard_map/ppermute | solution.py:787
  278.5 31.7 %collective-permute-start.18 = (bf16[48,3840]{1,0:T(8,128)(2,1)}, bf16[48,3840]{1,0:T(8,128)(2,1)S(1)}, u32[]{:S(2)}, u32[]{:S(2)}) collective-permute-start(bf16[48,3840]{1,0:T(8,128)(2,1)} %reduce-scatter.2.cloned.1.call-done.mine_ref), channel_id=1, source_target_pairs={{0,1},{1,0},{2,3},{3,2},{4,5},{5,4},{6,7},{7,6},{8,9},{9,8},{10,11... | collective-permute-start | bytes 1105928 | tf_op jit(solution)/shard_map/ppermute | solution.py:787
  283.7 17.1 %copy-start.14 = (bf16[48,1280]{1,0:T(8,128)(2,1)}, bf16[48,1280]{1,0:T(8,128)(2,1)S(1)}, u32[]{:S(2)}) copy-start(bf16[48,1280]{1,0:T(8,128)(2,1)S(1)} %fusion.24.mine_ref) | copy-start | bytes 368644
  283.7 17.1 %collective-permute-start.17 = (bf16[48,1280]{1,0:T(8,128)(2,1)S(1)}, bf16[48,1280]{1,0:T(8,128)(2,1)S(1)}, u32[]{:S(2)}, u32[]{:S(2)}) collective-permute-start(bf16[48,1280]{1,0:T(8,128)(2,1)S(1)} %fusion.24.mine_ref), channel_id=1, source_target_pairs={{0,1},{1,0},{2,3},{3,2},{4,5},{5,4},{6,7},{7,6},{8,9},{9,8},{10,11... | collective-permute-start | bytes 368648 | tf_op jit(solution)/shard_map/ppermute | solution.py:787
  (21 other events, 59.2 us)
Sparse Core Ops, SparseCore 0:
  10.6 94.3 all-gather.1
  164.5 85.0 reduce-scatter.1

commit v3 on v2

--- a/solution.py
+++ b/solution.py
@@ -109,10 +109,12 @@
         dkt_ref[...] = jnp.zeros_like(dkt_ref)
         dvt_ref[...] = jnp.zeros_like(dvt_ref)
 
-    lane = lax.broadcasted_iota(jnp.int32, (half, 128), 1)
+    tile = q_ref.shape[0]
+    first = step < half // tile
+    lane = lax.broadcasted_iota(jnp.int32, (tile, 128), 1)
     q = q_ref[...] * jnp.asarray(0.125, BF)
-    do = jnp.where(step == 0, mine_ref[...], got_ref[...])
-    o = jnp.where(step == 0, o_mine_ref[...], o_sent_ref[...])
+    do = jnp.where(first, mine_ref[...], got_ref[...])
+    o = jnp.where(first, o_mine_ref[...], o_sent_ref[...])
     product = do.astype(F32) * o.astype(F32)
     lse = lse_ref[0].T
     qt, dot_t = q.T, do.T
@@ -138,9 +140,9 @@
         dkt_ref[part, :] += dot(qt[part, :], ds)
         dvt_ref[part, :] += dot(dot_t[part, :], low)
     dq = (jnp.where(lane < 64, dq[0], dq[1]) * 0.125).astype(BF)
-    d_ref[0, pl.ds(pl.multiple_of(step * half, 128), half), :] = dq
-
-    @pl.when(step == 1)
+    d_ref[0, pl.ds(pl.multiple_of(step * tile, 128), tile), :] = dq
+
+    @pl.when(step == pl.num_programs(1) - 1)
     def _():
         d_ref[1] = dkt_ref[...].T.astype(BF)
         d_ref[2] = dvt_ref[...].T.astype(BF)
@@ -153,14 +155,16 @@
     def whole(part):
         return pl.BlockSpec((rows, 128), lambda p, i: (0, part * pairs + start + p))
 
-    block = pl.BlockSpec((half, 128), lambda p, i: (i, start + p))
-    fixed = pl.BlockSpec((half, 128), lambda p, i: (0, start + p))
+    tile = 256
+    per_half = half // tile
+    block = pl.BlockSpec((tile, 128), lambda p, i: (i, start + p))
+    fixed = pl.BlockSpec((tile, 128), lambda p, i: (lax.rem(i, per_half), start + p))
     return pl.pallas_call(
         functools.partial(backward_kernel, half, valid),
-        grid=(count, 2),
+        grid=(count, 2 * per_half),
         in_specs=[
             block, whole(1), whole(2), fixed, fixed, fixed, fixed,
-            pl.BlockSpec((1, 8, half), lambda p, i: (start + p, 0, i)),
+            pl.BlockSpec((1, 8, tile), lambda p, i: (start + p, 0, i)),
             pl.BlockSpec(memory_space=pl.ANY),
         ],
         out_specs=pl.BlockSpec((3, rows, 128), lambda p, i: (0, 0, p)),
@@ -180,38 +184,42 @@
     )(qkv, qkv, qkv, o_mine, o_sent, do_mine, do_got, lse, token)
 
 
-def prepare_kernel(x_ref, *refs):
+def rows_below(x, start, valid):
+    row = start + lax.broadcasted_iota(jnp.int32, x.shape, 0)
+    return jnp.where(row < valid, x, jnp.zeros_like(x))
+
+
+def prepare_kernel(valid, x_ref, *refs):
     normed_ref, flipped_ref, inverse_ref = refs[-3:]
-    valid = x_ref.shape[1]
-    x = x_ref[0].astype(F32)
+    tile, wide = normed_ref.shape
+    x = rows_below(x_ref[0].astype(F32), pl.program_id(0) * tile, valid)
     centered = x - jnp.mean(x, axis=-1, keepdims=True)
     inverse = lax.rsqrt(jnp.mean(centered * centered, axis=-1, keepdims=True) + EPSILON)
-    rest = (normed_ref.shape[0] - valid // 8 * 8, normed_ref.shape[1])
-    normed_ref[valid // 8 * 8 :, :] = jnp.zeros(rest, F32)
-    normed_ref[:valid, :] = centered * inverse
-    inverse_ref[...] = jnp.zeros(inverse_ref.shape, F32)
-    inverse_ref[:valid, :] = inverse
-    wide = normed_ref.shape[1]
-    flipped_ref[:wide, :] = normed_ref[...].T.astype(BF)
-    flipped_ref[wide:, :] = jnp.ones((16, normed_ref.shape[0]), BF)
+    normed = centered * inverse
+    normed_ref[...] = normed
+    inverse_ref[...] = jnp.broadcast_to(inverse, inverse_ref.shape)
+    flipped_ref[:wide, :] = normed.T.astype(BF)
+    flipped_ref[wide:, :] = jnp.ones((16, tile), BF)
 
 
 def prepare(frames, half, block, filled=()):
     _, valid, wide = frames.shape
-    return pl.pallas_call(
-        prepare_kernel,
-        grid=(1,),
-        in_specs=[pl.BlockSpec((1, valid, wide), lambda i: (0, 0, 0))]
+    tile = 384
+    first = block * (half // tile)
+    return pl.pallas_call(
+        functools.partial(prepare_kernel, valid),
+        grid=(half // tile,),
+        in_specs=[pl.BlockSpec((1, tile, wide), lambda i: (0, i, 0))]
         + [pl.BlockSpec(memory_space=pl.ANY)] * len(filled),
         out_specs=[
-            pl.BlockSpec((half, wide), lambda i: (block, 0)),
-            pl.BlockSpec((wide + 16, half), lambda i: (0, block)),
-            pl.BlockSpec((half, 1), lambda i: (0, 0)),
+            pl.BlockSpec((tile, wide), lambda i: (first + i, 0)),
+            pl.BlockSpec((wide + 16, tile), lambda i: (0, first + i)),
+            pl.BlockSpec((tile, 128), lambda i: (i, 0)),
         ],
         out_shape=[
             jax.ShapeDtypeStruct((2 * half, wide), F32),
             jax.ShapeDtypeStruct((wide + 16, 2 * half), BF),
-            jax.ShapeDtypeStruct((half, 1), F32),
+            jax.ShapeDtypeStruct((half, 128), F32),
         ],
         input_output_aliases={1: 0, 2: 1} if filled else {},
         cost_estimate=pl.CostEstimate(
@@ -221,9 +229,53 @@
     )(frames, *filled)
 
 
+def attend_kernel(valid, place_ref, x_ref, mine_ref, got_ref, w_ref, rows_ref, sum_ref, h_ref):
+    tile = sum_ref.shape[0]
+    group = mine_ref.shape[1]
+    here = place_ref[0]
+    first = w_ref[pl.ds(pl.multiple_of(here * group, 128), group), :]
+    other = w_ref[pl.ds(pl.multiple_of(group - here * group, 128), group), :]
+    total = dot(mine_ref[...], first) + dot(got_ref[...], other)
+    x = rows_below(x_ref[0].astype(F32), pl.program_id(0) * tile, valid)
+    total = x + total + rows_ref[4:5, :]
+    sum_ref[...] = total
+    centered = total - jnp.mean(total, axis=-1, keepdims=True)
+    inverse = lax.rsqrt(jnp.mean(centered * centered, axis=-1, keepdims=True) + EPSILON)
+    h_ref[...] = (centered * inverse * rows_ref[5:6, :] + rows_ref[6:7, :]).astype(BF)
+
+
+def attend(here, frames, mine, got, w, column, table):
+    _, valid, wide = frames.shape
+    half, group = mine.shape
+    tile = 128
+    block = pl.BlockSpec((tile, group), lambda i, p: (i, 0))
+    out = pl.BlockSpec((tile, wide), lambda i, p: (i, 0))
+    return pl.pallas_call(
+        functools.partial(attend_kernel, valid),
+        grid_spec=pltpu.PrefetchScalarGridSpec(
+            num_scalar_prefetch=1,
+            grid=(half // tile,),
+            in_specs=[
+                pl.BlockSpec((1, tile, wide), lambda i, p: (0, i, 0)), block, block,
+                pl.BlockSpec((wide, wide), lambda i, p: (0, column)),
+                pl.BlockSpec((16, wide), lambda i, p: (0, 0)),
+            ],
+            out_specs=[out, out],
+        ),
+        out_shape=[
+            jax.ShapeDtypeStruct((half, wide), F32),
+            jax.ShapeDtypeStruct((half, wide), BF),
+        ],
+        cost_estimate=pl.CostEstimate(
+            flops=4 * half * wide * group, bytes_accessed=half * wide * 10, transcendentals=half
+        ),
+        name="attend",
+    )(here, frames, mine, got, w, table)
+
+
 def projection_kernel(
-    part, group, place_ref, held_ref, x_ref, qkv_ref, w_ref, wt_ref, rows_ref, columns_ref,
-    gain_ref, bias_ref,
+    part, group, place_ref, held_ref, x_ref, qkv_ref, w_ref, wt_ref, rows_ref, scale_ref,
+    gain_ref, bias_ref, columns_ref,
 ):
     wide, width = w_ref.shape
 
@@ -237,6 +289,8 @@
         wt_ref[...] = w_ref[...].T
         table = columns_ref[...].T[:16, :]
         rows_ref[...] = table
+        scale_ref[:, :128] = jnp.broadcast_to(columns_ref[:, 0:1], (wide, 128))
+        scale_ref[:, 128:] = jnp.broadcast_to(columns_ref[:, 1:2], (wide, 128))
         gain_ref[...] = table[:8]
         here = place_ref[blocks]
         lane = lax.broadcasted_iota(jnp.int32, (wide, group), 0)
@@ -260,7 +314,7 @@
     blocks, extent, across = held.shape
     width = across - 128
     rows, wide = normed.shape
-    tile = 512
+    tile = 384
 
     def fixed(*shape):
         return pl.BlockSpec(shape, lambda i, p: tuple(0 for _ in shape))
@@ -273,16 +327,20 @@
             in_specs=[fixed(blocks, extent, across), pl.BlockSpec((tile, wide), lambda i, p: (i, 0))],
             out_specs=[
                 pl.BlockSpec((tile, width), lambda i, p: (i, 0)),
-                fixed(wide, width), fixed(width, wide), fixed(16, wide), fixed(wide, 128),
+                fixed(wide, width), fixed(width, wide), fixed(16, wide), fixed(wide, 256),
             ],
-            scratch_shapes=[pltpu.VMEM((8, wide), F32), pltpu.VMEM((8, width), F32)],
+            scratch_shapes=[
+                pltpu.VMEM((8, wide), F32),
+                pltpu.VMEM((8, width), F32),
+                pltpu.VMEM((wide, 128), F32),
+            ],
         ),
         out_shape=[
             jax.ShapeDtypeStruct((rows, width), BF),
             jax.ShapeDtypeStruct((wide, width), BF),
             jax.ShapeDtypeStruct((width, wide), BF),
             jax.ShapeDtypeStruct((16, wide), F32),
-            jax.ShapeDtypeStruct((wide, 128), F32),
+            jax.ShapeDtypeStruct((wide, 256), F32),
         ],
         cost_estimate=pl.CostEstimate(
             flops=2 * rows * wide * width, bytes_accessed=rows * wide * 8, transcendentals=0
@@ -298,7 +356,7 @@
     s = m[w_ref.shape[0] :][:8]
     m = m[: w_ref.shape[0]]
     s_ref[...] = s
-    gain, shift = scale_ref[:, 0:1], scale_ref[:, 1:2]
+    gain, shift = scale_ref[:, 0:1], scale_ref[:, 128:129]
     total = s[0:1, :]
     g_ref[...] = (gain * m + shift * total).astype(BF)
     w = w_ref[...].astype(F32)
@@ -320,7 +378,7 @@
         in_specs=[
             pl.BlockSpec((tall, rows), lambda j: (0, 0)),
             pl.BlockSpec((wide, group), lambda j: (0, j)),
-            pl.BlockSpec((wide, 128), lambda j: (0, 0)),
+            pl.BlockSpec((wide, 256), lambda j: (0, 0)),
         ]
         + [pl.BlockSpec((1, *d.shape[1:]), lambda j: (j, 0, 0)) for d in ds],
         out_specs=[
@@ -343,49 +401,37 @@
 def spread_kernel(
     part, pieces, per, place_ref, token_ref, xt_ref, w_ref, scale_ref, *refs
 ):
-    d_refs, (b_ref, v_ref, keep_ref, give_ref, c_ref, s_ref) = refs[:pieces], refs[pieces:]
+    d_refs, refs = refs[:pieces], refs[pieces:]
+    b_ref, v_ref, keep_ref, give_ref, c_ref, s_ref, first_ref, second_ref = refs
     step = pl.program_id(0)
     wide, group = w_ref.shape
     d = jnp.concatenate([r[0] for r in d_refs], axis=1)
     m = dot(xt_ref[...], d)
     s = m[wide : wide + 8]
-    m = m[:wide]
     s_ref[step] = s
-    gain, shift = scale_ref[:, 0:1], scale_ref[:, 1:2]
-    total = s[0:1, :]
-    g = (gain * m + shift * total).astype(BF)
-    w = w_ref[...].astype(F32)
-    lane = lax.broadcasted_iota(jnp.int32, c_ref.shape, 1)
-    first = jnp.sum(w * m, axis=1, keepdims=True)
-    second = jnp.sum(w * total, axis=1, keepdims=True)
-    now = jnp.where(lane == 0, first, jnp.where(lane == 1, second, 0.0))
 
     @pl.when(step == 0)
     def _():
-        c_ref[...] = now
-
-    @pl.when(step > 0)
-    def _():
-        c_ref[...] += now
-
-    def store(value, columns):
-        value = value.reshape(keep_ref.shape[0], 2, part, value.shape[1])
-
-        @pl.when(place_ref[0] == 0)
-        def _():
-            keep_ref[:, :, columns] = value[:, 0]
-            give_ref[:, :, columns] = value[:, 1]
-
-        @pl.when(place_ref[0] == 1)
-        def _():
-            keep_ref[:, :, columns] = value[:, 1]
-            give_ref[:, :, columns] = value[:, 0]
-
-    store(g, pl.ds(pl.multiple_of(step * group, 128), group))
+        first_ref[...] = jnp.zeros_like(first_ref)
+        second_ref[...] = jnp.zeros_like(second_ref)
+
+    gain, shift = scale_ref[:, :128], scale_ref[:, 128:]
+    one, two, gs = first_ref[...], second_ref[...], []
+    for i in range(group // 128):
+        columns = slice(128 * i, 128 * (i + 1))
+        piece, w, total = m[:wide, columns], w_ref[:, columns].astype(F32), s[0:1, columns]
+        one, two = one + w * piece, two + w * total
+        gs.append((gain * piece + shift * total).astype(BF))
+    first_ref[...], second_ref[...] = one, two
+    at = pl.ds(pl.multiple_of(step * group, 128), group)
+    spread_store(part, place_ref, keep_ref, give_ref, jnp.concatenate(gs, axis=1), at)
 
     @pl.when(step == 2)
     def _():
-        columns = c_ref[...]
+        lane = lax.broadcasted_iota(jnp.int32, c_ref.shape, 1)
+        second = jnp.sum(second_ref[...], axis=1, keepdims=True)
+        first = jnp.sum(first_ref[...], axis=1, keepdims=True)
+        columns = jnp.where(lane == 0, first, jnp.where(lane == 1, second, 0.0))
         small = v_ref[...].T
         for i, name in enumerate((4, 5, 6, 7 + per)):
             columns = jnp.where(lane == name, small[:, i : i + 1], columns)
@@ -408,7 +454,16 @@
                 )
                 block = jnp.where(low == 2 + j, column, block)
             c_ref[at, :] = block
-        store(c_ref[...].astype(BF), pl.ds(3 * group, 128))
+        g = c_ref[...].astype(BF)
+        spread_store(part, place_ref, keep_ref, give_ref, g, pl.ds(3 * group, 128))
+
+
+def spread_store(part, place_ref, keep_ref, give_ref, value, columns):
+    value = value.reshape(keep_ref.shape[0], 2, part, value.shape[1])
+    even, odd = value[:, 0], value[:, 1]
+    low = place_ref[0] == 0
+    keep_ref[:, :, columns] = jnp.where(low, even, odd)
+    give_ref[:, :, columns] = jnp.where(low, odd, even)
 
 
 def spread_weight_gradient(place, token, xt, w, scale, ds, bias, sums, part):
@@ -435,7 +490,12 @@
             + [pl.BlockSpec((1, *d.shape[1:]), lambda j, p: (j, 0, 0)) for d in ds]
             + [fixed(bias), fixed(sums)],
             out_specs=[out, out],
-            scratch_shapes=[pltpu.VMEM((wide, 128), F32), pltpu.VMEM((3, 8, group), F32)],
+            scratch_shapes=[
+                pltpu.VMEM((wide, 128), F32),
+                pltpu.VMEM((3, 8, group), F32),
+                pltpu.VMEM((wide, 128), F32),
+                pltpu.VMEM((wide, 128), F32),
+            ],
         ),
         out_shape=[jax.ShapeDtypeStruct((size // 2, part, 3 * group + 128), BF)] * 2,
         cost_estimate=pl.CostEstimate(
@@ -446,42 +506,24 @@
 
 
 def input_kernel(pieces, token_ref, wt_ref, *refs):
-    d_refs, (other_ref, mine_ref) = refs[:pieces], refs[pieces:]
+    d_refs, out_ref = refs[:pieces], refs[pieces]
     d = jnp.concatenate([r[j] for j in range(3) for r in d_refs], axis=1)
-    value = dot(d, wt_ref[...])
-    half = pl.num_programs(0) // 2
-
-    @pl.when(pl.program_id(0) < half)
-    def _():
-        other_ref[...] = value.astype(BF)
-
-    @pl.when(pl.program_id(0) >= half)
-    def _():
-        mine_ref[...] = value
-
-
-def projection_input_gradient(wt, ds, token, half):
+    out_ref[...] = dot(d, wt_ref[...]).astype(out_ref.dtype)
+
+
+def projection_input_gradient(wt, ds, token, half, block, kind):
     wide = wt.shape[1]
-    tile = 384
-    tiles = half // tile
+    tile = 256
+    start = block * (half // tile)
     return pl.pallas_call(
         functools.partial(input_kernel, len(ds)),
-        grid=(2 * tiles,),
+        grid=(half // tile,),
         in_specs=[pl.BlockSpec(memory_space=pl.ANY), pl.BlockSpec(wt.shape, lambda i: (0, 0))]
-        + [
-            pl.BlockSpec((3, tile, d.shape[2]), lambda i: (0, lax.rem(i + tiles, 2 * tiles), 0))
-            for d in ds
-        ],
-        out_specs=[
-            pl.BlockSpec((tile, wide), lambda i: (jnp.minimum(i, tiles - 1), 0)),
-            pl.BlockSpec((tile, wide), lambda i: (jnp.maximum(i - tiles, 0), 0)),
-        ],
-        out_shape=[
-            jax.ShapeDtypeStruct((half, wide), BF),
-            jax.ShapeDtypeStruct((half, wide), F32),
-        ],
-        cost_estimate=pl.CostEstimate(
-            flops=4 * half * wt.size, bytes_accessed=half * wt.shape[0] * 8, transcendentals=0
+        + [pl.BlockSpec((3, tile, d.shape[2]), lambda i: (0, start + i, 0)) for d in ds],
+        out_specs=pl.BlockSpec((tile, wide), lambda i: (i, 0)),
+        out_shape=jax.ShapeDtypeStruct((half, wide), kind),
+        cost_estimate=pl.CostEstimate(
+            flops=2 * half * wt.size, bytes_accessed=half * wt.shape[0] * 4, transcendentals=0
         ),
         name="projection_input_gradient",
     )(token, wt, *ds)
@@ -736,6 +778,43 @@
     )(here, mine, theirs)
 
 
+def output_kernel(token_ref, z_ref, w_ref, residual_ref, rows_ref, out_ref, total_ref):
+    step = pl.program_id(0)
+
+    @pl.when(step == 0)
+    def _():
+        total_ref[...] = residual_ref[...] + rows_ref[-1:, :]
+
+    total_ref[...] += dot(z_ref[...], w_ref[...])
+
+    @pl.when(step == pl.num_programs(0) - 1)
+    def _():
+        out_ref[0] = total_ref[: out_ref.shape[1], :].astype(BF)
+
+
+def output_end(token, activated, w, residual, bias, valid):
+    rows, ff = activated.shape
+    wide = w.shape[1]
+    return pl.pallas_call(
+        output_kernel,
+        grid=(ff // wide,),
+        in_specs=[
+            pl.BlockSpec(memory_space=pl.ANY),
+            pl.BlockSpec((rows, wide), lambda i: (0, i)),
+            pl.BlockSpec((wide, wide), lambda i: (i, 0)),
+            pl.BlockSpec((rows, wide), lambda i: (0, 0)),
+            pl.BlockSpec((1, wide), lambda i: (0, 0)),
+        ],
+        out_specs=pl.BlockSpec((1, valid, wide), lambda i: (0, 0, 0)),
+        out_shape=jax.ShapeDtypeStruct((1, valid, wide), BF),
+        scratch_shapes=[pltpu.VMEM((rows, wide), F32)],
+        cost_estimate=pl.CostEstimate(
+            flops=2 * rows * wide * ff, bytes_accessed=rows * ff * 4, transcendentals=0
+        ),
+        name="output_end",
+    )(token, activated, w, residual, bias)
+
+
 def join_kernel(mine_ref, theirs_ref, out_ref, first_ref):
     wide = out_ref.shape[1]
     mine, theirs = mine_ref[...].astype(F32), theirs_ref[...].astype(F32)
@@ -760,19 +839,19 @@
     weighted = (mine_ref[...] + got_ref[...].astype(F32)) * gain_ref[...]
     first = jnp.mean(weighted, axis=-1, keepdims=True)
     second = jnp.mean(weighted * normed, axis=-1, keepdims=True)
-    out_ref[:, 0, :] = residual_ref[...] + inverse_ref[...] * (weighted - first - normed * second)
+    out_ref[:, 0, :] = residual_ref[...] + inverse_ref[:, 0:1] * (weighted - first - normed * second)
 
 
 def input_end(mine, got, residual, normed, gain, inverse, valid):
     half, wide = mine.shape
-    tile = 128
+    tile = 256
     block = pl.BlockSpec((tile, wide), lambda i: (i, 0))
     return pl.pallas_call(
         input_end_kernel,
         grid=(half // tile,),
         in_specs=[
             block, block, block, block, pl.BlockSpec((1, wide), lambda i: (0, 0)),
-            pl.BlockSpec((tile, 1), lambda i: (i, 0)),
+            pl.BlockSpec((tile, 128), lambda i: (i, 0)),
         ],
         out_specs=pl.BlockSpec((tile, 1, wide), lambda i: (i, 0, 0)),
         out_shape=jax.ShapeDtypeStruct((valid, 1, wide), F32),
@@ -833,14 +912,6 @@
     return lax.optimization_barrier((x, *others))[0]
 
 
-def normalize(values):
-    center = jnp.mean(values, axis=-1, keepdims=True)
-    centered = values - center
-    variance = jnp.mean(centered * centered, axis=-1, keepdims=True)
-    inverse = lax.rsqrt(variance + EPSILON)
-    return centered * inverse, inverse
-
-
 def gelu_cdf(values):
     return 0.5 * (1.0 + lax.erf(values * (1.0 / math.sqrt(2.0))))
 
@@ -856,9 +927,6 @@
     group = wide // 2
     half = -(-valid // 256) * 256
     here = lax.axis_index("seq")
-
-    def pad(block):
-        return jnp.pad(block[0], ((0, half - valid), (0, 0)))
 
     def other(x):
         return swap(x, "seq", 2, 1)
@@ -901,24 +969,22 @@
     def vector(start, stop):
         return table[start:stop].reshape(-1, size, part).transpose(1, 0, 2).reshape(-1)
 
-    gain_one, bias_out = table[0], table[4]
-    gain_two, shift_two = table[5], table[6]
+    gain_one, gain_two = table[0], table[5]
     bias_fc1, bias_fc2 = vector(7, 7 + per), table[7 + per]
     o_mine, o_sent, lse = attention_forward(qkv, half, valid)
     o_got = other(o_sent)
-    out_mine = lax.dynamic_slice_in_dim(out_full, here * group, group, axis=0)
-    out_other = lax.dynamic_slice_in_dim(out_full, group - here * group, group, axis=0)
-    residual = pad(frames_in).astype(F32) + dot(o_mine, out_mine) + dot(o_got, out_other) + bias_out
-
-    normed_two, _ = normalize(residual)
-    hidden_two = (normed_two * gain_two + shift_two).astype(BF)
+    flag = jnp.full((1,), here, jnp.int32)
+    if part % 16:
+        residual, hidden_two = attend(flag, frames_in, o_mine, o_got, out_full, 0, table)
+    else:
+        residual, hidden_two = attend(flag, frames_in, o_mine, o_got, later, per, table)
+
     pre_act = dot(hidden_two, fc1_full) + bias_fc1
     cdf = gelu_cdf(pre_act)
     density = jnp.exp(-0.5 * pre_act * pre_act) * (1.0 / math.sqrt(2.0 * math.pi))
     activated, slope = lax.optimization_barrier(
         ((pre_act * cdf).astype(BF), (cdf + pre_act * density).astype(BF))
     )
-    flag = jnp.full((1,), here, jnp.int32)
     (
         grad_pre_low, fc2_full, grad_residual, grad_residual_low,
         do_mine, do_sent, grad_bias_fc1, grad_sums,
@@ -940,15 +1006,14 @@
     x = x.reshape(size // 2, 2, -1, wide)
     keep, give = pick(x, 1, here).astype(BF), pick(x, 1, 1 - here).astype(BF)
     got = other(give)
-    pairs = group // 128
-    ds = [backward(give, 0, pairs - 1)]
+    ds = [backward(give, 0, group // 128)]
+    grad_other = projection_input_gradient(w_flipped, ds, ds[0], half, 1, BF)
+    grad_got = other(grad_other)
     for at in range(len(bits) - 2, -1, -1):
-        keep, got = after((keep, got), ds[0])
-        x = keep.astype(F32) + got.astype(F32)
+        x = after(keep, grad_other).astype(F32) + got.astype(F32)
         keep, give = halve(x.reshape(-1, 2, *x.shape[1:]), 1, bits[at])
         keep, got = keep.astype(BF), swap(give, "dp", size, bits[at])
     fc2_keep_x, fc2_got_x = keep, got
-    ds.append(backward(give, pairs - 1, 1))
 
     vectors = [(7, grad_bias_fc1)]
     if part % 16:
@@ -973,7 +1038,7 @@
     else:
         sides = jnp.concatenate([parity, jnp.full((1,), here, jnp.int32)])
         keep, give = spread_weight_gradient(
-            sides, ds[1], normed_t, w_full, scale, ds, grad_bias_fc1, grad_sums, part
+            sides, give, normed_t, w_full, scale, ds, grad_bias_fc1, grad_sums, part
         )
     got = swap(give, "dp", size, 1)
     for at in range(len(bits) - 2, -1, -1):
@@ -982,11 +1047,10 @@
         got = swap(give, "dp", size, bits[at])
     fc2_keep, fc2_got = after((fc2_keep_x, fc2_got_x), give)
     fc2_gives, fc2_stay = scatter_split(fc2_keep.astype(F32) + fc2_got.astype(F32), size)
-    grad_other, grad_mine = projection_input_gradient(w_flipped, ds, fc2_gives[2], half)
-    grad_got = other(grad_other)
-    output = dot(after(activated, *fc2_gives), fc2_full)
-    output = residual + output + bias_fc2
-    frames_out = output.astype(BF)[:valid][None]
+    grad_mine = projection_input_gradient(w_flipped, ds, fc2_gives[2], half, 0, F32)
+    frames_out = output_end(
+        fc2_gives[2], activated, fc2_full, residual, bias_fc2[None], valid
+    )
     fc2_part = scatter_join(fc2_stay, fc2_gives, size).astype(BF)
     gives, stay = scatter_split(keep.astype(F32) + got.astype(F32), size)
     grad_input = input_end(

time: 325 us -> 323 us (level); the launches traced: 320 us -> 322 us
  Pallas kernels: 154 us -> 171 us
  matrix products: 18.2 us -> 10.9 us
  local copies, waits for them, and re-layouts: 20.4 us -> 15.2 us
    pallas_call x3 -> x6, Pallas kernels: 15.6 us -> 32.7 us  [the longest x2 10.4 us: projection_input_gradient(): pl.pallas_call(functools.partial(input_kernel, len(ds)), grid=(half // ti...]
    all_gather x1, waiting for transfers between devices: 17 us -> 3.95 us  [layer(): lax.all_gather(jnp.concatenate([fc2_local, w_o, w_fc1], axis=1), 'dp', ax...]
    ppermute x23, waiting for transfers between devices: 54.6 us -> 64.7 us  [swap(): return lax.ppermute(x, axis, [(i, i ^ bit) for i in range(size)])]
    dot_general x4 -> x1, matrix products: 18.2 us -> 10.9 us  [dot(): lax.dot_general(a, b, (((ca,), (cb,)), ((), ())), preferred_element_type=...]
    unnamed x60 -> x48, local copies, waits for them, and re-layouts: 11.2 us -> 5.77 us
    pallas_call x2 -> x1, Pallas kernels: 44 us -> 43.6 us  [attention_backward(): pl.pallas_call(functools.partial(backward_kernel, half, valid), grid=(cou...]
  transfers between devices with their start and end apart: 25 -> 25, of which waited for: 9 -> 9; matrix products, arithmetic and copies ran while one was open for 9% -> 6% of each run, Pallas kernels for 38% -> 41%
where the time goes in v3:
time: 323 us; the launch traced here: 322 us
  Pallas kernels  171 us (53%)
  waiting for transfers between devices  68.7 us (21%)
  starting transfers between devices  30.3 us (9%)
  local copies, waits for them, and re-layouts  15.2 us (5%)
  between operations  14.4 us (4%)
  other arithmetic  12 us (4%)
  matrix products  10.9 us (3%)
    ppermute x23, waiting for transfers between devices, swap(): return lax.ppermute(x, axis, [(i, i ^ bit) for i in range(size)])  64.7 us
    pallas_call x1, Pallas kernels, attention_backward(): pl.pallas_call(functools.partial(backward_kernel, half, valid), grid=(cou...  43.6 us
    ppermute x23, starting transfers between devices, swap(): return lax.ppermute(x, axis, [(i, i ^ bit) for i in range(size)])  30.2 us
    pallas_call x1, Pallas kernels, feed_back(): pl.pallas_call(functools.partial(feed_back_kernel, part), grid_spec=pltpu...  21.9 us
    pallas_call x1, Pallas kernels, attention_forward(): pl.pallas_call(functools.partial(forward_kernel, half, valid), grid=(pair...  20.8 us
    pallas_call x1, Pallas kernels, spread_weight_gradient(): pl.pallas_call(functools.partial(spread_kernel, part, len(ds), bias.shape...  12.5 us
    dot_general x1, matrix products, dot(): lax.dot_general(a, b, (((ca,), (cb,)), ((), ())), preferred_element_type=...  10.9 us
    pallas_call x1, Pallas kernels, projection(): pl.pallas_call(functools.partial(projection_kernel, part, width // 3), gr...  10.4 us
  transfers between devices with their start and end apart: 25, of which 9 were waited for; matrix products, arithmetic and copies ran while one was open for 6% of the time, Pallas kernels for 41%

profile of v3, /device:TPU:0, one launch (start us, length us, event | category | flops | bytes accessed | tf_op | source)
XLA Modules:
  0.0 322.1 jit_solution(6095488277554190213)
XLA Ops:
  8.6 1.9 pad_maximum_fusion
  11.1 3.1 collective-permute-start
  14.2 2.6 collective-permute-start.1
  19.2 9.2 %collective-permute-done.1 = bf16[48,1280]{1,0:T(8,128)(2,1)S(1)} collective-permute-done((bf16[48,1280]{1,0:T(8,128)(2,1)S(1)}, bf16[48,1280]{1,0:T(8,128)(2,1)S(1)}, u32[]{:S(2)}, u32[]{:S(2)}) %collective-permute-start.1) | collective-permute-done | bytes 122912 | tf_op jit(solution)/shard_map/ppermute | solution.py:866
  32.1 9.8 %collective-permute-done.3 = bf16[4,48,1280]{2,1,0:T(8,128)(2,1)S(1)} collective-permute-done((bf16[4,48,1280]{2,1,0:T(8,128)(2,1)S(1)}, bf16[4,48,1280]{2,1,0:T(8,128)(2,1)S(1)}, u32[]{:S(2)}, u32[]{:S(2)}) %collective-permute-start.3) | collective-permute-done | bytes 491552 | tf_op jit(solution)/shard_map/ppermute | solution.py:866
  44.7 3.5 %prepare.2 = (f32[1536,768]{1,0:T(8,128)}, bf16[784,1536]{1,0:T(8,128)(2,1)}, f32[768,128]{1,0:T(8,128)}) custom-call(bf16[1,750,768]{2,1,0:T(8,128)(2,1)} %x_ref.3), custom_call_target="tpu_custom_call" | custom-call | flops 9437184 | bytes 4718592 | tf_op jit(solution)/shard_map/prepare/pallas_call | solution.py:209
  49.8 3.4 %prepare.3 = (f32[1536,768]{1,0:T(8,128)}, bf16[784,1536]{1,0:T(8,128)(2,1)}, f32[768,128]{1,0:T(8,128)}) custom-call(bf16[1,750,768]{2,1,0:T(8,128)(2,1)} %copy-done.6, f32[1536,768]{1,0:T(8,128)} %get-tuple-element.57.refs_0_, bf16[784,1536]{1,0:T(8,128)(2,1)} %get-tuple-element.58.refs_1_), custom_call_target="tpu_custom_call", output_to_operand_aliasing={{0}: (1, {}), {1}: (2, {})} | custom-call | flops 9437184 | bytes 4718592 | tf_op jit(solution)/shard_map/prepare/pallas_call | solution.py:209
  54.2 10.4 %projection.1 = (bf16[1536,1152]{1,0:T(8,128)(2,1)}, bf16[768,1152]{1,0:T(8,128)(2,1)}, bf16[1152,768]{1,0:T(8,128)(2,1)}, f32[16,768]{1,0:T(8,128)}, f32[768,256]{1,0:T(8,128)}) custom-call(s32[17]{0:T(128)} %pad_add_fusion.place_ref, bf16[16,48,1280]{2,1,0:T(8,128)(2,1)} %constant_dynamic-update-slice_fusion.5.held_ref, ...), custom_call_target="tpu_custom_call" | custom-call | flops 2717908992 | bytes 9437184 | tf_op jit(solution)/shard_map/projection/pallas_call | solution.py:322
  64.6 20.8 %attention_forward.1 = (bf16[768,384]{1,0:T(8,128)(2,1)}, bf16[768,384]{1,0:T(8,128)(2,1)}, f32[3,8,1536]{2,1,0:T(8,128)}) custom-call(bf16[1536,1152]{1,0:T(8,128)(2,1)} %get-tuple-element.60.q_ref.k_ref.v_ref, bf16[1536,1152]{1,0:T(8,128)(2,1)} %get-tuple-element.60.q_ref.k_ref.v_ref, bf16[1536,1152]{1,0:T(8,128)(2,1)} %get-tuple-element.60.q_ref.k_ref.v_ref), custom_call_target="tpu_custom_call" | custom-call | flops 14495514624 | bytes 5308416 | tf_op jit(solution)/shard_map/attention_forward/pallas_call | solution.py:68
  89.6 11.6 %collective-permute-done.6.got_ref = bf16[768,384]{1,0:T(8,128)(2,1)S(1)} collective-permute-done((bf16[768,384]{1,0:T(8,128)(2,1)}, bf16[768,384]{1,0:T(8,128)(2,1)S(1)}, u32[]{:S(2)}, u32[]{:S(2)}) %collective-permute-start.6) | collective-permute-done | bytes 589856 | tf_op jit(solution)/shard_map/ppermute | solution.py:866
  101.1 4.0 %all-gather.2.cloned.1.call-done.w_ref.fc2_ref.fc1_ref.out_ref = bf16[768,6912]{1,0:T(8,128)(2,1)} async-done(((bf16[48,6912]{1,0:T(8,128)(2,1)}), bf16[768,6912]{1,0:T(8,128)(2,1)}) %all-gather.2.cloned.1.call-update) | async-done | bytes 10616848 | tf_op jit(solution)/shard_map/all_gather | solution.py:955
  105.1 6.8 %attend.1 = (f32[768,768]{1,0:T(8,128)}, bf16[768,768]{1,0:T(8,128)(2,1)}) custom-call(s32[1]{0:T(128)} %bitcast.1.place_ref, bf16[1,750,768]{2,1,0:T(8,128)(2,1)} %x_ref.3, bf16[768,384]{1,0:T(8,128)(2,1)} %get-tuple-element.61.mine_ref.o_mine_ref, bf16[768,384]{1,0:T(8,128)(2,1)} %copy-done.7, ...), custom_call_target="tpu_custom_call" | custom-call | flops 905969664 | bytes 5898240 | tf_op jit(solution)/shard_map/attend/pallas_call | solution.py:253
  111.9 10.9 %fusion.4 = (bf16[768,3072]{1,0:T(8,128)(2,1)}, bf16[768,3072]{1,0:T(8,128)(2,1)}) fusion(f32[3072]{0:T(1024)S(1)} %add.122, bf16[768,768]{1,0:T(8,128)(2,1)} %get-tuple-element.64.h_ref, bf16[768,6912]{1,0:T(8,128)(2,1)} %all-gather.2.cloned.1.call-done.w_ref.fc2_ref.fc1_ref.out_ref), kind=kOutput, calls=%fused_computation.6 | convolution fusion | flops 3652190208 | bytes 15347712 | tf_op jit(solution)/shard_map/dot_general | solution.py:19
  122.7 21.9 %feed_back.1 = (bf16[768,3072]{1,0:T(8,128)(2,1)}, bf16[3072,768]{1,0:T(8,128)(2,1)}, f32[768,768]{1,0:T(8,128)}, bf16[768,768]{1,0:T(8,128)(2,1)}, bf16[768,384...) custom-call(s32[1]{0:T(128)} %bitcast.1.place_ref, ...), custom_call_target="tpu_custom_call" | custom-call | flops 7247757312 | bytes 23592960 | tf_op jit(solution)/shard_map/feed_back/pallas_call | solution.py:711
  144.6 8.3 %third_gradient.1 = (bf16[8,192,768]{2,1,0:T(8,128)(2,1)}, bf16[8,192,768]{2,1,0:T(8,128)(2,1)}) custom-call(s32[1]{0:T(128)} %bitcast.place_ref, bf16[768,3072]{1,0:T(8,128)(2,1)} %get-tuple-element.65.z_ref, bf16[1,750,768]{2,1,0:T(8,128)(2,1)} %cot_ref.3, bf16[768,384]{1,0:T(8,128)(2,1)} %get-tuple-element.68.token_ref), custom_call_target="tpu_custom_call" | custom-call | flops 3623878656 | bytes 9437184 | tf_op jit(solution)/shard_map/third_gradient/pallas_call | solution.py:610
  153.2 10.2 %second_gradient.1 = bf16[768,3840]{1,0:T(8,128)(2,1)} custom-call(s32[1]{0:T(128)} %bitcast.1.place_ref, bf16[8,192,768]{2,1,0:T(8,128)(2,1)} %get-tuple-element.70.token_ref, bf16[768,384]{1,0:T(8,128)(2,1)} %get-tuple-element.61.mine_ref.o_mine_ref, bf16[768,384]{1,0:T(8,128)(2,1)} %copy-done.7, bf16[768,768]{1,0:T(8,128)(2,1)} %get-tuple-element.91.drb_ref, ...), custom_call_target="tpu_custom_call" | custom-call | flops 4529848320 | bytes 9437184 | tf_op jit(solution)/shard_map/second_gradient/pallas_call | solution.py:557
  165.8 2.2 convert_add_fusion
  169.2 10.8 %collective-permute-done.8.got_ref = bf16[768,384]{1,0:T(8,128)(2,1)} collective-permute-done((bf16[768,384]{1,0:T(8,128)(2,1)}, bf16[768,384]{1,0:T(8,128)(2,1)}, u32[]{:S(2)}, u32[]{:S(2)}) %collective-permute-start.8) | collective-permute-done | bytes 589856 | tf_op jit(solution)/shard_map/ppermute | solution.py:866
  180.0 43.6 %attention_backward.1.token_ref.refs_0_ = bf16[3,1536,384]{2,1,0:T(8,128)(2,1)} custom-call(bf16[1536,1152]{1,0:T(8,128)(2,1)} %get-tuple-element.60.q_ref.k_ref.v_ref, bf16[1536,1152]{1,0:T(8,128)(2,1)} %get-tuple-element.60.q_ref.k_ref.v_ref, bf16[1536,1152]{1,0:T(8,128)(2,1)} %get-tuple-element.60.q_ref.k_ref.v_ref, ...), custom_call_target="tpu_custom_call" | custom-call | flops 28991029248 | bytes 9437184 | tf_op jit(solution)/shard_map/attention_backward/pallas_call | solution.py:162
  223.6 5.0 %projection_input_gradient.2 = bf16[768,768]{1,0:T(8,128)(2,1)} custom-call(bf16[3,1536,384]{2,1,0:T(8,128)(2,1)} %attention_backward.1.token_ref.refs_0_, bf16[1152,768]{1,0:T(8,128)(2,1)} %get-tuple-element.73.wt_ref, bf16[3,1536,384]{2,1,0:T(8,128)(2,1)} %attention_backward.1.token_ref.refs_0_), custom_call_target="tpu_custom_call" | custom-call | flops 1358954496 | bytes 3538944 | tf_op jit(solution)/shard_map/projection_input_gradient/pallas_call | solution.py:518
  230.1 12.5 %spread_weight_gradient.1 = (bf16[8,48,1280]{2,1,0:T(8,128)(2,1)}, bf16[8,48,1280]{2,1,0:T(8,128)(2,1)}) custom-call(s32[2]{0:T(128)} %pad_add_fusion.1.place_ref, bf16[4,96,768]{2,1,0:T(8,128)(2,1)} %get-tuple-element.107.token_ref, bf16[784,1536]{1,0:T(8,128)(2,1)} %get-tuple-element.75.xt_ref, bf16[768,1152]{1,0:T(8,128)(2,1)} %get-tuple-element.76.w_ref, ...), custom_call_target="tpu_custom_call" | custom-call | flops 2717908992 | bytes 4718592 | tf_op jit(solution)/shard_map/spread_weight_gradient/pallas_call | solution.py:479
  248.6 12.0 %collective-permute-done.10 = bf16[4,96,768]{2,1,0:T(8,128)(2,1)S(1)} collective-permute-done((bf16[4,96,768]{2,1,0:T(8,128)(2,1)}, bf16[4,96,768]{2,1,0:T(8,128)(2,1)S(1)}, u32[]{:S(2)}, u32[]{:S(2)}) %collective-permute-start.10) | collective-permute-done | bytes 589856 | tf_op jit(solution)/shard_map/ppermute | solution.py:866
  261.5 1.9 collective-permute-start.19
  263.4 2.1 collective-permute-start.20
  267.0 5.3 %projection_input_gradient.3.mine_ref = f32[768,768]{1,0:T(8,128)} custom-call(bf16[96,768]{1,0:T(8,128)(2,1)} %copy-done.8, bf16[1152,768]{1,0:T(8,128)(2,1)} %get-tuple-element.73.wt_ref, bf16[3,1536,384]{2,1,0:T(8,128)(2,1)} %attention_backward.1.token_ref.refs_0_), custom_call_target="tpu_custom_call" | custom-call | flops 1358954496 | bytes 3538944 | tf_op jit(solution)/shard_map/projection_input_gradient/pallas_call | solution.py:518
  272.3 6.4 %input_end.1 = f32[750,1,768]{2,1,0:T(1,128)} custom-call(f32[768,768]{1,0:T(8,128)} %projection_input_gradient.3.mine_ref, bf16[768,768]{1,0:T(8,128)(2,1)} %collective-permute-done.12.got_ref, f32[768,768]{1,0:T(8,128)} %get-tuple-element.85.residual_ref, f32[1536,768]{1,0:T(8,128)} %get-tuple-element.59.x_ref.normed_ref, ...), custom_call_target="tpu_custom_call" | custom-call | flops 5898240 | bytes 10616832 | tf_op jit(solution)/shard_map/input_end/pallas_call | solution.py:849
  278.7 8.7 %output_end.1 = bf16[1,750,768]{2,1,0:T(8,128)(2,1)} custom-call(bf16[96,768]{1,0:T(8,128)(2,1)} %copy-done.8, bf16[768,3072]{1,0:T(8,128)(2,1)} %get-tuple-element.65.z_ref, bf16[3072,768]{1,0:T(8,128)(2,1)} %get-tuple-element.84.w_ref, f32[768,768]{1,0:T(8,128)} %get-tuple-element.67.residual_ref, f32[1,768]{1,0:T(1,128)} %get-tuple-element.128.rows_ref), custom_call_target="tpu_custom_call" | custom-call | flops 3623878656 | bytes 9437184 | tf_op jit(solution)/shard_map/output_end/pallas_call | solution.py:798
  290.2 2.0 collective-permute-start.15
  296.7 5.4 %collective-permute-done.15 = bf16[48,1280]{1,0:T(8,128)(2,1)S(1)} collective-permute-done((bf16[48,1280]{1,0:T(8,128)(2,1)S(1)}, bf16[48,1280]{1,0:T(8,128)(2,1)S(1)}, u32[]{:S(2)}, u32[]{:S(2)}) %collective-permute-start.15) | collective-permute-done | bytes 122912 | tf_op jit(solution)/shard_map/ppermute | solution.py:866
  304.9 5.1 %collective-permute-done.17.theirs_ref = bf16[48,1280]{1,0:T(8,128)(2,1)S(1)} collective-permute-done((bf16[48,1280]{1,0:T(8,128)(2,1)S(1)}, bf16[48,1280]{1,0:T(8,128)(2,1)S(1)}, u32[]{:S(2)}, u32[]{:S(2)}) %collective-permute-start.17) | collective-permute-done | bytes 122912 | tf_op jit(solution)/shard_map/ppermute | solution.py:866
  310.7 1.8 finish.1
  313.3 2.0 join_second.1
  (120 shorter events, 42.5 us)
Async XLA Ops:
  7.3 9.5 %copy-start.1 = (bf16[1,750,768]{2,1,0:T(8,128)(2,1)S(1)}, bf16[1,750,768]{2,1,0:T(8,128)(2,1)}, u32[]{:S(2)}) copy-start(bf16[1,750,768]{2,1,0:T(8,128)(2,1)} %x_ref.3) | copy-start | bytes 3456004
  7.3 97.8 %all-gather.2.cloned.1.call-start = ((), (), s32[]{:S(2)}) async-start(), calls=%async_computation.1 | async-start | bytes 11280384 | tf_op jit(solution)/shard_map/all_gather | solution.py:955
  10.5 285.4 %reduce-scatter.2.cloned.1.call-start = ((), (), s32[]{:S(2)}) async-start(), calls=%async_computation.2 | async-start | bytes 6266880 | tf_op jit(solution)/shard_map/reduce_scatter | solution.py:998
  11.0 33.0 %copy-start = (s32[16]{0:T(128)S(1)}, s32[16]{0:T(128)}, u32[]{:S(2)}) copy-start(s32[16]{0:T(128)} %constant.112.clone) | copy-start | bytes 196
  11.1 8.1 %collective-permute-start = (bf16[48,1280]{1,0:T(8,128)(2,1)S(1)}, bf16[48,1280]{1,0:T(8,128)(2,1)S(1)}, u32[]{:S(2)}, u32[]{:S(2)}) collective-permute-start(bf16[48,1280]{1,0:T(8,128)(2,1)S(1)} %get-tuple-element.126), channel_id=1, source_target_pairs={{0,8},{2,10},{4,12},{6,14},{8,0},{10,2},{12,4},{14,6},{16,24},{18,... | collective-permute-start | bytes 368648 | tf_op jit(solution)/shard_map/ppermute | solution.py:866
  14.2 14.2 %collective-permute-start.1 = (bf16[48,1280]{1,0:T(8,128)(2,1)S(1)}, bf16[48,1280]{1,0:T(8,128)(2,1)S(1)}, u32[]{:S(2)}, u32[]{:S(2)}) collective-permute-start(bf16[48,1280]{1,0:T(8,128)(2,1)S(1)} %get-tuple-element.126), channel_id=1, source_target_pairs={{0,16},{2,18},{4,20},{6,22},{8,24},{10,26},{12,28},{14,30},{16,0},... | collective-permute-start | bytes 368648 | tf_op jit(solution)/shard_map/ppermute | solution.py:866
  16.8 11.6 %collective-permute-start.2 = (bf16[48,1280]{1,0:T(8,128)(2,1)S(1)}, bf16[48,1280]{1,0:T(8,128)(2,1)S(1)}, u32[]{:S(2)}, u32[]{:S(2)}) collective-permute-start(bf16[48,1280]{1,0:T(8,128)(2,1)S(1)} %get-tuple-element.126), channel_id=1, source_target_pairs={{0,24},{2,26},{4,28},{6,30},{8,16},{10,18},{12,20},{14,22},{16,8},... | collective-permute-start | bytes 368648 | tf_op jit(solution)/shard_map/ppermute | solution.py:866
  16.8 32.0 %collective-permute-start.5 = (bf16[1,750,768]{2,1,0:T(8,128)(2,1)S(1)}, bf16[1,750,768]{2,1,0:T(8,128)(2,1)S(1)}, u32[]{:S(2)}, u32[]{:S(2)}) collective-permute-start(bf16[1,750,768]{2,1,0:T(8,128)(2,1)S(1)} %copy-done.1), channel_id=1, source_target_pairs={{0,1},{1,0},{2,3},{3,2},{4,5},{5,4},{6,7},{7,6},{8,9},{9,8},{10,11... | collective-permute-start | bytes 3456008 | tf_op jit(solution)/shard_map/ppermute | solution.py:866
  28.5 13.4 %collective-permute-start.3 = (bf16[4,48,1280]{2,1,0:T(8,128)(2,1)S(1)}, bf16[4,48,1280]{2,1,0:T(8,128)(2,1)S(1)}, u32[]{:S(2)}, u32[]{:S(2)}) collective-permute-start(bf16[4,48,1280]{2,1,0:T(8,128)(2,1)S(1)} %pad_maximum_fusion.1), channel_id=1, source_target_pairs={{0,4},{2,6},{4,0},{6,2},{8,12},{10,14},{12,8},{14,10},{16,20},{18,... | collective-permute-start | bytes 1474568 | tf_op jit(solution)/shard_map/ppermute | solution.py:866
  44.0 9.2 %collective-permute-start.4 = (bf16[8,48,1280]{2,1,0:T(8,128)(2,1)}, bf16[8,48,1280]{2,1,0:T(8,128)(2,1)S(1)}, u32[]{:S(2)}, u32[]{:S(2)}) collective-permute-start(bf16[8,48,1280]{2,1,0:T(8,128)(2,1)} %get-tuple-element.112), channel_id=1, source_target_pairs={{0,2},{2,0},{4,6},{6,4},{8,10},{10,8},{12,14},{14,12},{16,18},{18,... | collective-permute-start | bytes 2949128 | tf_op jit(solution)/shard_map/ppermute | solution.py:866
  85.3 15.8 %collective-permute-start.6 = (bf16[768,384]{1,0:T(8,128)(2,1)}, bf16[768,384]{1,0:T(8,128)(2,1)S(1)}, u32[]{:S(2)}, u32[]{:S(2)}) collective-permute-start(bf16[768,384]{1,0:T(8,128)(2,1)} %get-tuple-element.62.o_sent_ref), channel_id=1, source_target_pairs={{0,1},{1,0},{2,3},{3,2},{4,5},{5,4},{6,7},{7,6},{8,9},{9,8},{10,11... | collective-permute-start | bytes 1769480 | tf_op jit(solution)/shard_map/ppermute | solution.py:866
  153.0 12.8 %collective-permute-start.7 = (bf16[8,192,768]{2,1,0:T(8,128)(2,1)}, bf16[8,192,768]{2,1,0:T(8,128)(2,1)}, u32[]{:S(2)}, u32[]{:S(2)}) collective-permute-start(bf16[8,192,768]{2,1,0:T(8,128)(2,1)} %get-tuple-element.70.token_ref), channel_id=1, source_target_pairs={{0,2},{2,0},{4,6},{6,4},{8,10},{10,8},{12,14},{14,12},{16,18},{18,... | collective-permute-start | bytes 7077896 | tf_op jit(solution)/shard_map/ppermute | solution.py:866
  163.5 16.6 %collective-permute-start.8 = (bf16[768,384]{1,0:T(8,128)(2,1)}, bf16[768,384]{1,0:T(8,128)(2,1)}, u32[]{:S(2)}, u32[]{:S(2)}) collective-permute-start(bf16[768,384]{1,0:T(8,128)(2,1)} %get-tuple-element.68.token_ref), channel_id=1, source_target_pairs={{0,1},{1,0},{2,3},{3,2},{4,5},{5,4},{6,7},{7,6},{8,9},{9,8},{10,11... | collective-permute-start | bytes 1769480 | tf_op jit(solution)/shard_map/ppermute | solution.py:866
  168.2 11.9 %copy-start.5 = (bf16[8,96,768]{2,1,0:T(8,128)(2,1)}, bf16[8,96,768]{2,1,0:T(8,128)(2,1)S(1)}, u32[]{:S(2)}) copy-start(bf16[8,96,768]{2,1,0:T(8,128)(2,1)S(1)} %get-tuple-element.103.token_ref) | copy-start | bytes 3538948
  168.2 60.5 %collective-permute-start.9 = (bf16[8,96,768]{2,1,0:T(8,128)(2,1)S(1)}, bf16[8,96,768]{2,1,0:T(8,128)(2,1)S(1)}, u32[]{:S(2)}, u32[]{:S(2)}) collective-permute-start(bf16[8,96,768]{2,1,0:T(8,128)(2,1)S(1)} %get-tuple-element.103.token_ref), channel_id=1, source_target_pairs={{0,1},{1,0},{2,3},{3,2},{4,5},{5,4},{6,7},{7,6},{8,9},{9,8},{10,11... | collective-permute-start | bytes 3538952 | tf_op jit(solution)/shard_map/ppermute | solution.py:866
  242.5 2.8 collective-permute-start.11
  242.5 29.7 %collective-permute-start.12 = (bf16[768,768]{1,0:T(8,128)(2,1)}, bf16[768,768]{1,0:T(8,128)(2,1)}, u32[]{:S(2)}, u32[]{:S(2)}) collective-permute-start(bf16[768,768]{1,0:T(8,128)(2,1)} %projection_input_gradient.2), channel_id=1, source_target_pairs={{0,1},{1,0},{2,3},{3,2},{4,5},{5,4},{6,7},{7,6},{8,9},{9,8},{10,11... | collective-permute-start | bytes 3538952 | tf_op jit(solution)/shard_map/ppermute | solution.py:866
  244.2 16.4 %collective-permute-start.10 = (bf16[4,96,768]{2,1,0:T(8,128)(2,1)}, bf16[4,96,768]{2,1,0:T(8,128)(2,1)S(1)}, u32[]{:S(2)}, u32[]{:S(2)}) collective-permute-start(bf16[4,96,768]{2,1,0:T(8,128)(2,1)} %get-tuple-element.107.token_ref), channel_id=1, source_target_pairs={{0,4},{2,6},{4,0},{6,2},{8,12},{10,14},{12,8},{14,10},{16,20},{18,... | collective-permute-start | bytes 1769480 | tf_op jit(solution)/shard_map/ppermute | solution.py:866
  245.3 15.3 %copy-start.4 = (bf16[4,96,768]{2,1,0:T(8,128)(2,1)S(1)}, bf16[4,96,768]{2,1,0:T(8,128)(2,1)}, u32[]{:S(2)}) copy-start(bf16[4,96,768]{2,1,0:T(8,128)(2,1)} %get-tuple-element.82) | copy-start | bytes 1769476
  247.7 39.8 %collective-permute-start.13 = (bf16[4,48,1280]{2,1,0:T(8,128)(2,1)}, bf16[4,48,1280]{2,1,0:T(8,128)(2,1)}, u32[]{:S(2)}, u32[]{:S(2)}) collective-permute-start(bf16[4,48,1280]{2,1,0:T(8,128)(2,1)} %fusion.11), channel_id=1, source_target_pairs={{0,4},{2,6},{4,0},{6,2},{8,12},{10,14},{12,8},{14,10},{16,20},{18,... | collective-permute-start | bytes 1474568 | tf_op jit(solution)/shard_map/ppermute | solution.py:866
  261.5 5.5 %copy-start.8 = (bf16[96,768]{1,0:T(8,128)(2,1)}, bf16[96,768]{1,0:T(8,128)(2,1)S(1)}, u32[]{:S(2)}) copy-start(bf16[96,768]{1,0:T(8,128)(2,1)S(1)} %get-tuple-element.106.token_ref) | copy-start | bytes 442372
  261.5 30.6 %collective-permute-start.19 = (bf16[96,768]{1,0:T(8,128)(2,1)}, bf16[96,768]{1,0:T(8,128)(2,1)S(1)}, u32[]{:S(2)}, u32[]{:S(2)}) collective-permute-start(bf16[96,768]{1,0:T(8,128)(2,1)} %get-tuple-element.104), channel_id=1, source_target_pairs={{0,8},{2,10},{4,12},{6,14},{8,0},{10,2},{12,4},{14,6},{16,24},{18,... | collective-permute-start | bytes 442376 | tf_op jit(solution)/shard_map/ppermute | solution.py:866
  263.4 30.1 %collective-permute-start.20 = (bf16[96,768]{1,0:T(8,128)(2,1)}, bf16[96,768]{1,0:T(8,128)(2,1)}, u32[]{:S(2)}, u32[]{:S(2)}) collective-permute-start(bf16[96,768]{1,0:T(8,128)(2,1)} %get-tuple-element.105), channel_id=1, source_target_pairs={{0,16},{2,18},{4,20},{6,22},{8,24},{10,26},{12,28},{14,30},{16,0},... | collective-permute-start | bytes 442376 | tf_op jit(solution)/shard_map/ppermute | solution.py:866
  265.5 28.0 %collective-permute-start.21 = (bf16[96,768]{1,0:T(8,128)(2,1)S(1)}, bf16[96,768]{1,0:T(8,128)(2,1)}, u32[]{:S(2)}, u32[]{:S(2)}) collective-permute-start(bf16[96,768]{1,0:T(8,128)(2,1)S(1)} %get-tuple-element.106.token_ref), channel_id=1, source_target_pairs={{0,24},{2,26},{4,28},{6,30},{8,16},{10,18},{12,20},{14,22},{16,8},... | collective-permute-start | bytes 442376 | tf_op jit(solution)/shard_map/ppermute | solution.py:866
  288.6 6.0 %copy-start.2 = (f32[4,48,1280]{2,1,0:T(8,128)}, f32[4,48,1280]{2,1,0:T(8,128)S(1)}, u32[]{:S(2)}) copy-start(f32[4,48,1280]{2,1,0:T(8,128)S(1)} %bitcast_add_fusion) | copy-start | bytes 2949124
  288.6 8.0 %collective-permute-start.14 = (bf16[48,1280]{1,0:T(8,128)(2,1)S(1)}, bf16[48,1280]{1,0:T(8,128)(2,1)S(1)}, u32[]{:S(2)}, u32[]{:S(2)}) collective-permute-start(bf16[48,1280]{1,0:T(8,128)(2,1)S(1)} %get-tuple-element.109), channel_id=1, source_target_pairs={{0,8},{2,10},{4,12},{6,14},{8,0},{10,2},{12,4},{14,6},{16,24},{18,... | collective-permute-start | bytes 368648 | tf_op jit(solution)/shard_map/ppermute | solution.py:866
  290.2 11.9 %collective-permute-start.15 = (bf16[48,1280]{1,0:T(8,128)(2,1)S(1)}, bf16[48,1280]{1,0:T(8,128)(2,1)S(1)}, u32[]{:S(2)}, u32[]{:S(2)}) collective-permute-start(bf16[48,1280]{1,0:T(8,128)(2,1)S(1)} %get-tuple-element.111), channel_id=1, source_target_pairs={{0,16},{2,18},{4,20},{6,22},{8,24},{10,26},{12,28},{14,30},{16,0},... | collective-permute-start | bytes 368648 | tf_op jit(solution)/shard_map/ppermute | solution.py:866
  292.1 9.9 %collective-permute-start.16 = (bf16[48,1280]{1,0:T(8,128)(2,1)S(1)}, bf16[48,1280]{1,0:T(8,128)(2,1)S(1)}, u32[]{:S(2)}, u32[]{:S(2)}) collective-permute-start(bf16[48,1280]{1,0:T(8,128)(2,1)S(1)} %get-tuple-element.110), channel_id=1, source_target_pairs={{0,24},{2,26},{4,28},{6,30},{8,16},{10,18},{12,20},{14,22},{16,8},... | collective-permute-start | bytes 368648 | tf_op jit(solution)/shard_map/ppermute | solution.py:866
  294.6 9.5 %collective-permute-start.22 = (bf16[96,768]{1,0:T(8,128)(2,1)S(1)}, bf16[96,768]{1,0:T(8,128)(2,1)S(1)}, u32[]{:S(2)}, u32[]{:S(2)}) collective-permute-start(bf16[96,768]{1,0:T(8,128)(2,1)S(1)} %fusion.15), channel_id=1, source_target_pairs={{0,1},{1,0},{2,3},{3,2},{4,5},{5,4},{6,7},{7,6},{8,9},{9,8},{10,11... | collective-permute-start | bytes 442376 | tf_op jit(solution)/shard_map/ppermute | solution.py:866
  295.9 16.6 %collective-permute-start.18 = (bf16[48,3840]{1,0:T(8,128)(2,1)}, bf16[48,3840]{1,0:T(8,128)(2,1)S(1)}, u32[]{:S(2)}, u32[]{:S(2)}) collective-permute-start(bf16[48,3840]{1,0:T(8,128)(2,1)} %reduce-scatter.2.cloned.1.call-done.mine_ref), channel_id=1, source_target_pairs={{0,1},{1,0},{2,3},{3,2},{4,5},{5,4},{6,7},{7,6},{8,9},{9,8},{10,11... | collective-permute-start | bytes 1105928 | tf_op jit(solution)/shard_map/ppermute | solution.py:866
  303.1 7.0 %copy-start.9 = (bf16[48,1280]{1,0:T(8,128)(2,1)}, bf16[48,1280]{1,0:T(8,128)(2,1)S(1)}, u32[]{:S(2)}) copy-start(bf16[48,1280]{1,0:T(8,128)(2,1)S(1)} %fusion.18.mine_ref) | copy-start | bytes 368644
  303.1 7.0 %collective-permute-start.17 = (bf16[48,1280]{1,0:T(8,128)(2,1)S(1)}, bf16[48,1280]{1,0:T(8,128)(2,1)S(1)}, u32[]{:S(2)}, u32[]{:S(2)}) collective-permute-start(bf16[48,1280]{1,0:T(8,128)(2,1)S(1)} %fusion.18.mine_ref), channel_id=1, source_target_pairs={{0,1},{1,0},{2,3},{3,2},{4,5},{5,4},{6,7},{7,6},{8,9},{9,8},{10,11... | collective-permute-start | bytes 368648 | tf_op jit(solution)/shard_map/ppermute | solution.py:866
  (15 other events, 41.0 us)
Sparse Core Ops, SparseCore 0:
  10.7 94.3 all-gather.1
  163.6 84.6 reduce-scatter.1

commit v4 on v3

--- a/solution.py
+++ b/solution.py
@@ -155,7 +155,7 @@
     def whole(part):
         return pl.BlockSpec((rows, 128), lambda p, i: (0, part * pairs + start + p))
 
-    tile = 256
+    tile = 384
     per_half = half // tile
     block = pl.BlockSpec((tile, 128), lambda p, i: (i, start + p))
     fixed = pl.BlockSpec((tile, 128), lambda p, i: (lax.rem(i, per_half), start + p))
@@ -247,7 +247,7 @@
 def attend(here, frames, mine, got, w, column, table):
     _, valid, wide = frames.shape
     half, group = mine.shape
-    tile = 128
+    tile = 256
     block = pl.BlockSpec((tile, group), lambda i, p: (i, 0))
     out = pl.BlockSpec((tile, wide), lambda i, p: (i, 0))
     return pl.pallas_call(
@@ -293,14 +293,16 @@
         scale_ref[:, 128:] = jnp.broadcast_to(columns_ref[:, 1:2], (wide, 128))
         gain_ref[...] = table[:8]
         here = place_ref[blocks]
-        lane = lax.broadcasted_iota(jnp.int32, (wide, group), 0)
-        entry = lax.broadcasted_iota(jnp.int32, (wide, group), 1)
-        base = lane + part * (lane // part) - group * here
-        low = table.astype(BF)
+        few = group // 2
+        row = lax.broadcasted_iota(jnp.int32, (few, group), 0)
+        entry = lax.broadcasted_iota(jnp.int32, (few, group), 1)
+        base = row + part * (row // part)
         for v in range(2):
+            at = pl.multiple_of(v * (wide // 2) + here * few, 64)
+            low = columns_ref[pl.ds(at, few), :].T[:16].astype(BF)
             total = jnp.zeros((16, group), F32)
             for j in range(2):
-                chosen = entry == base + part * j - wide * v
+                chosen = entry == base + part * j
                 picked = dot(low, jnp.where(chosen, 1.0, 0.0).astype(BF))
                 total = total + picked[2 + j : 3 + j, :]
             bias_ref[:, 2 * v * group : (2 * v + 1) * group] = total[:8]
@@ -513,7 +515,7 @@
 
 def projection_input_gradient(wt, ds, token, half, block, kind):
     wide = wt.shape[1]
-    tile = 256
+    tile = 384
     start = block * (half // tile)
     return pl.pallas_call(
         functools.partial(input_kernel, len(ds)),
@@ -572,6 +574,23 @@
         ),
         name="second_gradient",
     )(here, token, o_mine, o_got, drb, hidden, du)
+
+
+def pack_kernel(fc2_ref, out_ref, fc1_ref, packed_ref):
+    part, wide = out_ref.shape
+    per = fc2_ref.shape[0] // part
+    for j in range(per):
+        packed_ref[:, j * wide : (j + 1) * wide] = fc2_ref[j * part : (j + 1) * part, :]
+    packed_ref[:, per * wide : (per + 1) * wide] = out_ref[...]
+    packed_ref[:, (per + 1) * wide :] = fc1_ref[...]
+
+
+def pack(w_fc2, w_o, w_fc1):
+    part, wide = w_o.shape
+    across = wide + 2 * w_fc1.shape[1]
+    return pl.pallas_call(
+        pack_kernel, out_shape=jax.ShapeDtypeStruct((part, across), BF), name="pack"
+    )(w_fc2, w_o, w_fc1)
 
 
 def fill_rows(ref, x):
@@ -629,17 +648,25 @@
 
 
 def feed_back_kernel(
-    part, place_ref, fc2_ref, fc1_ref, out_ref, slope_ref, cot_ref, residual_ref, gain_ref,
-    du_ref, flat_ref, grad_ref, low_ref, mine_ref, sent_ref, bias_ref, sums_ref,
-    total_ref, padded_ref,
+    part, place_ref, fc2_ref, fc1_ref, late_out_ref, slope_ref, cot_ref, late_ref, gain_ref,
+    du_ref, flat_ref, low_ref, mine_ref, sent_ref, bias_ref, sums_ref,
+    total_ref, padded_ref, out_ref, residual_ref, sem_ref,
 ):
     step = pl.program_id(0)
     rows, wide = total_ref.shape
     group = mine_ref.shape[1]
     per = fc2_ref.shape[1] // wide
 
+    first = per * wide if part else 0
+    copies = (
+        pltpu.make_async_copy(late_out_ref.at[:, first : first + wide], out_ref, sem_ref.at[0]),
+        pltpu.make_async_copy(late_ref, residual_ref, sem_ref.at[1]),
+    )
+
     @pl.when(step == 0)
     def _():
+        for copy in copies:
+            copy.start()
         fill_rows(padded_ref, cot_ref[0])
         total_ref[...] = jnp.zeros_like(total_ref)
 
@@ -658,6 +685,8 @@
 
     @pl.when(step == pl.num_programs(0) - 1)
     def _():
+        for copy in copies:
+            copy.wait()
         tile = 64
 
         def body(i, sums):
@@ -672,7 +701,6 @@
             second = jnp.mean(weighted * normed, axis=-1, keepdims=True)
             g = padded_ref[at, :].astype(F32)
             grad = g + inverse * (weighted - first - normed * second)
-            grad_ref[at, :] = grad
             low_ref[at, :] = grad.astype(BF)
             parts = (grad, dh * normed, dh, g)
             return tuple(s + jnp.sum(p, axis=0, keepdims=True) for s, p in zip(sums, parts, strict=True))
@@ -697,12 +725,10 @@
         fc2, fc1, out = weights
         fc2_spec = pl.BlockSpec((wide, wide), lambda i, p: (i, 0))
         fc1_spec = pl.BlockSpec((wide, wide), lambda i, p: (0, i))
-        out_spec = pl.BlockSpec((wide, wide), lambda i, p: (0, 0))
     else:
         fc2 = fc1 = out = weights
         fc2_spec = pl.BlockSpec((wide // per, ff), lambda i, p: (i, 0))
         fc1_spec = pl.BlockSpec((wide, wide), lambda i, p: (0, per + 1 + i))
-        out_spec = pl.BlockSpec((wide, wide), lambda i, p: (0, per))
 
     def fixed(*shape):
         return pl.BlockSpec(shape, lambda i, p: tuple(0 for _ in shape))
@@ -714,20 +740,25 @@
             num_scalar_prefetch=1,
             grid=(per,),
             in_specs=[
-                fc2_spec, fc1_spec, out_spec, block, fixed(1, valid, wide), fixed(rows, wide),
-                fixed(1, wide),
+                fc2_spec, fc1_spec, pl.BlockSpec(memory_space=pl.ANY), block,
+                fixed(1, valid, wide), pl.BlockSpec(memory_space=pl.ANY), fixed(1, wide),
             ],
             out_specs=[
-                block, pl.BlockSpec((wide, wide), lambda i, p: (i, 0)), fixed(rows, wide),
+                block, pl.BlockSpec((wide, wide), lambda i, p: (i, 0)),
                 fixed(rows, wide), fixed(rows, group), fixed(rows, group),
                 pl.BlockSpec((1, wide), lambda i, p: (0, i)), fixed(8, wide),
             ],
-            scratch_shapes=[pltpu.VMEM((rows, wide), F32), pltpu.VMEM((rows, wide), BF)],
+            scratch_shapes=[
+                pltpu.VMEM((rows, wide), F32),
+                pltpu.VMEM((rows, wide), BF),
+                pltpu.VMEM((wide, wide), BF),
+                pltpu.VMEM((rows, wide), F32),
+                pltpu.SemaphoreType.DMA((2,)),
+            ],
         ),
         out_shape=[
             jax.ShapeDtypeStruct((rows, ff), BF),
             jax.ShapeDtypeStruct((ff, wide), BF),
-            jax.ShapeDtypeStruct((rows, wide), F32),
             jax.ShapeDtypeStruct((rows, wide), BF),
             jax.ShapeDtypeStruct((rows, group), BF),
             jax.ShapeDtypeStruct((rows, group), BF),
@@ -836,15 +867,15 @@
 
 def input_end_kernel(mine_ref, got_ref, residual_ref, normed_ref, gain_ref, inverse_ref, out_ref):
     normed = normed_ref[...]
-    weighted = (mine_ref[...] + got_ref[...].astype(F32)) * gain_ref[...]
+    weighted = (mine_ref[...].astype(F32) + got_ref[...].astype(F32)) * gain_ref[...]
     first = jnp.mean(weighted, axis=-1, keepdims=True)
     second = jnp.mean(weighted * normed, axis=-1, keepdims=True)
-    out_ref[:, 0, :] = residual_ref[...] + inverse_ref[:, 0:1] * (weighted - first - normed * second)
+    out_ref[:, 0, :] = residual_ref[...].astype(F32) + inverse_ref[:, 0:1] * (weighted - first - normed * second)
 
 
 def input_end(mine, got, residual, normed, gain, inverse, valid):
     half, wide = mine.shape
-    tile = 256
+    tile = 384
     block = pl.BlockSpec((tile, wide), lambda i: (i, 0))
     return pl.pallas_call(
         input_end_kernel,
@@ -951,10 +982,12 @@
         held = jnp.take(held, place, axis=0, mode="clip").reshape(1, wide, 3 * group + 128)
         place = jnp.zeros((1,), jnp.int32)
     place = jnp.concatenate([place, jnp.full((1,), here, jnp.int32)])
-    fc2_local = w_fc2.reshape(per, part, wide).transpose(1, 0, 2).reshape(part, ff)
-    later = lax.all_gather(
-        jnp.concatenate([fc2_local, w_o, w_fc1], axis=1), "dp", axis=0, tiled=True
-    )
+    if part % 16:
+        fc2_local = w_fc2.reshape(per, part, wide).transpose(1, 0, 2).reshape(part, ff)
+        packed = jnp.concatenate([fc2_local, w_o, w_fc1], axis=1)
+    else:
+        packed = pack(w_fc2, w_o, w_fc1)
+    later = lax.all_gather(packed, "dp", axis=0, tiled=True)
     out_full, fc1_full = later[:, ff : ff + wide], later[:, ff + wide :]
     weights = later
     if part % 16:
@@ -986,7 +1019,7 @@
         ((pre_act * cdf).astype(BF), (cdf + pre_act * density).astype(BF))
     )
     (
-        grad_pre_low, fc2_full, grad_residual, grad_residual_low,
+        grad_pre_low, fc2_full, grad_residual_low,
         do_mine, do_sent, grad_bias_fc1, grad_sums,
     ) = feed_back(flag, weights, slope, cotangent, residual, gain_two[None], part)
     do_got = other(do_sent)
@@ -1047,14 +1080,14 @@
         got = swap(give, "dp", size, bits[at])
     fc2_keep, fc2_got = after((fc2_keep_x, fc2_got_x), give)
     fc2_gives, fc2_stay = scatter_split(fc2_keep.astype(F32) + fc2_got.astype(F32), size)
-    grad_mine = projection_input_gradient(w_flipped, ds, fc2_gives[2], half, 0, F32)
+    grad_mine = projection_input_gradient(w_flipped, ds, fc2_gives[2], half, 0, BF)
     frames_out = output_end(
         fc2_gives[2], activated, fc2_full, residual, bias_fc2[None], valid
     )
     fc2_part = scatter_join(fc2_stay, fc2_gives, size).astype(BF)
     gives, stay = scatter_split(keep.astype(F32) + got.astype(F32), size)
     grad_input = input_end(
-        grad_mine, grad_got, grad_residual, normed_both, gain_one[None], inverse_one, valid
+        grad_mine, grad_got, grad_residual_low, normed_both, gain_one[None], inverse_one, valid
     ).transpose(1, 0, 2)
     mine = scatter_join(stay, gives, size).astype(BF)
     theirs = other(mine)

time: 323 us -> 314 us (0.972)
  Pallas kernels: 171 us -> 165 us
  transfers between devices with their start and end apart: 25 -> 25, of which waited for: 9 -> 10; matrix products, arithmetic and copies ran while one was open for 6% -> 6% of each run, Pallas kernels for 41% -> 41%
where the time goes in v4:
time: 314 us; the launch traced here: 313 us
  Pallas kernels  165 us (53%)
  waiting for transfers between devices  70.6 us (22%)
  starting transfers between devices  28.4 us (9%)
  between operations  14.4 us (5%)
  local copies, waits for them, and re-layouts  13.9 us (4%)
  matrix products  10.9 us (3%)
  other arithmetic  10 us (3%)
    ppermute x23, waiting for transfers between devices, swap(): return lax.ppermute(x, axis, [(i, i ^ bit) for i in range(size)])  66.7 us
    pallas_call x1, Pallas kernels, attention_backward(): pl.pallas_call(functools.partial(backward_kernel, half, valid), grid=(cou...  42.8 us
    ppermute x23, starting transfers between devices, swap(): return lax.ppermute(x, axis, [(i, i ^ bit) for i in range(size)])  28.3 us
    pallas_call x1, Pallas kernels, attention_forward(): pl.pallas_call(functools.partial(forward_kernel, half, valid), grid=(pair...  20.7 us
    pallas_call x1, Pallas kernels, feed_back(): pl.pallas_call(functools.partial(feed_back_kernel, part), grid_spec=pltpu...  20.1 us
    pallas_call x1, Pallas kernels, spread_weight_gradient(): pl.pallas_call(functools.partial(spread_kernel, part, len(ds), bias.shape...  12.5 us
    dot_general x1, matrix products, dot(): lax.dot_general(a, b, (((ca,), (cb,)), ((), ())), preferred_element_type=...  10.9 us
    pallas_call x1, Pallas kernels, second_gradient(): pl.pallas_call(second_kernel, grid_spec=pltpu.PrefetchScalarGridSpec(num_...  10.2 us
  transfers between devices with their start and end apart: 25, of which 10 were waited for; matrix products, arithmetic and copies ran while one was open for 6% of the time, Pallas kernels for 41%

profile of v4, /device:TPU:0, one launch (start us, length us, event | category | flops | bytes accessed | tf_op | source)
XLA Modules:
  0.0 313.3 jit_solution(7388736386921282472)
XLA Ops:
  7.3 2.1 pack.1
  10.0 3.1 collective-permute-start
  13.1 2.6 collective-permute-start.1
  18.1 7.3 %collective-permute-done.1 = bf16[48,1280]{1,0:T(8,128)(2,1)S(1)} collective-permute-done((bf16[48,1280]{1,0:T(8,128)(2,1)S(1)}, bf16[48,1280]{1,0:T(8,128)(2,1)S(1)}, u32[]{:S(2)}, u32[]{:S(2)}) %collective-permute-start.1) | collective-permute-done | bytes 122912 | tf_op jit(solution)/shard_map/ppermute | solution.py:897
  29.1 12.5 %collective-permute-done.3 = bf16[4,48,1280]{2,1,0:T(8,128)(2,1)S(1)} collective-permute-done((bf16[4,48,1280]{2,1,0:T(8,128)(2,1)S(1)}, bf16[4,48,1280]{2,1,0:T(8,128)(2,1)S(1)}, u32[]{:S(2)}, u32[]{:S(2)}) %collective-permute-start.3) | collective-permute-done | bytes 491552 | tf_op jit(solution)/shard_map/ppermute | solution.py:897
  44.4 3.5 %prepare.2 = (f32[1536,768]{1,0:T(8,128)}, bf16[784,1536]{1,0:T(8,128)(2,1)}, f32[768,128]{1,0:T(8,128)}) custom-call(bf16[1,750,768]{2,1,0:T(8,128)(2,1)} %x_ref.3), custom_call_target="tpu_custom_call" | custom-call | flops 9437184 | bytes 4718592 | tf_op jit(solution)/shard_map/prepare/pallas_call | solution.py:209
  49.5 3.4 %prepare.3 = (f32[1536,768]{1,0:T(8,128)}, bf16[784,1536]{1,0:T(8,128)(2,1)}, f32[768,128]{1,0:T(8,128)}) custom-call(bf16[1,750,768]{2,1,0:T(8,128)(2,1)} %copy-done.6, f32[1536,768]{1,0:T(8,128)} %get-tuple-element.56.refs_0_, bf16[784,1536]{1,0:T(8,128)(2,1)} %get-tuple-element.57.refs_1_), custom_call_target="tpu_custom_call", output_to_operand_aliasing={{0}: (1, {}), {1}: (2, {})} | custom-call | flops 9437184 | bytes 4718592 | tf_op jit(solution)/shard_map/prepare/pallas_call | solution.py:209
  53.9 9.5 %projection.1 = (bf16[1536,1152]{1,0:T(8,128)(2,1)}, bf16[768,1152]{1,0:T(8,128)(2,1)}, bf16[1152,768]{1,0:T(8,128)(2,1)}, f32[16,768]{1,0:T(8,128)}, f32[768,256]{1,0:T(8,128)}) custom-call(s32[17]{0:T(128)} %pad_add_fusion.place_ref, bf16[16,48,1280]{2,1,0:T(8,128)(2,1)} %constant_dynamic-update-slice_fusion.5.held_ref, ...), custom_call_target="tpu_custom_call" | custom-call | flops 2717908992 | bytes 9437184 | tf_op jit(solution)/shard_map/projection/pallas_call | solution.py:324
  63.4 20.7 %attention_forward.1 = (bf16[768,384]{1,0:T(8,128)(2,1)}, bf16[768,384]{1,0:T(8,128)(2,1)}, f32[3,8,1536]{2,1,0:T(8,128)}) custom-call(bf16[1536,1152]{1,0:T(8,128)(2,1)} %get-tuple-element.59.q_ref.k_ref.v_ref, bf16[1536,1152]{1,0:T(8,128)(2,1)} %get-tuple-element.59.q_ref.k_ref.v_ref, bf16[1536,1152]{1,0:T(8,128)(2,1)} %get-tuple-element.59.q_ref.k_ref.v_ref), custom_call_target="tpu_custom_call" | custom-call | flops 14495514624 | bytes 5308416 | tf_op jit(solution)/shard_map/attention_forward/pallas_call | solution.py:68
  88.2 11.9 %collective-permute-done.6.got_ref = bf16[768,384]{1,0:T(8,128)(2,1)S(1)} collective-permute-done((bf16[768,384]{1,0:T(8,128)(2,1)}, bf16[768,384]{1,0:T(8,128)(2,1)S(1)}, u32[]{:S(2)}, u32[]{:S(2)}) %collective-permute-start.6) | collective-permute-done | bytes 589856 | tf_op jit(solution)/shard_map/ppermute | solution.py:897
  100.2 3.9 %all-gather.2.cloned.1.call-done.w_ref.fc2_ref.fc1_ref.late_out_ref = bf16[768,6912]{1,0:T(8,128)(2,1)} async-done(((bf16[48,6912]{1,0:T(8,128)(2,1)}), bf16[768,6912]{1,0:T(8,128)(2,1)}) %all-gather.2.cloned.1.call-update) | async-done | bytes 10616848 | tf_op jit(solution)/shard_map/all_gather | solution.py:990
  104.0 5.3 %attend.1 = (f32[768,768]{1,0:T(8,128)}, bf16[768,768]{1,0:T(8,128)(2,1)}) custom-call(s32[1]{0:T(128)} %bitcast.1.place_ref, bf16[1,750,768]{2,1,0:T(8,128)(2,1)} %x_ref.3, bf16[768,384]{1,0:T(8,128)(2,1)} %get-tuple-element.60.mine_ref.o_mine_ref, bf16[768,384]{1,0:T(8,128)(2,1)} %copy-done.7, ...), custom_call_target="tpu_custom_call" | custom-call | flops 905969664 | bytes 5898240 | tf_op jit(solution)/shard_map/attend/pallas_call | solution.py:253
  109.3 10.9 %fusion.4 = (bf16[768,3072]{1,0:T(8,128)(2,1)}, bf16[768,3072]{1,0:T(8,128)(2,1)}) fusion(f32[3072]{0:T(1024)S(1)} %add.122, bf16[768,768]{1,0:T(8,128)(2,1)} %get-tuple-element.63.h_ref, bf16[768,6912]{1,0:T(8,128)(2,1)} %all-gather.2.cloned.1.call-done.w_ref.fc2_ref.fc1_ref.late_out_ref), kind=kOutput, calls=%fused_computation.6 | convolution fusion | flops 3652190208 | bytes 15347712 | tf_op jit(solution)/shard_map/dot_general | solution.py:19
  120.2 20.1 %feed_back.1 = (bf16[768,3072]{1,0:T(8,128)(2,1)}, bf16[3072,768]{1,0:T(8,128)(2,1)}, bf16[768,768]{1,0:T(8,128)(2,1)}, bf16[768,384]{1,0:T(8,128)(2,1)}, bf16[7...) custom-call(s32[1]{0:T(128)} %bitcast.1.place_ref, ...), custom_call_target="tpu_custom_call" | custom-call | flops 7247757312 | bytes 23592960 | tf_op jit(solution)/shard_map/feed_back/pallas_call | solution.py:737
  140.3 8.3 %third_gradient.1 = (bf16[8,192,768]{2,1,0:T(8,128)(2,1)}, bf16[8,192,768]{2,1,0:T(8,128)(2,1)}) custom-call(s32[1]{0:T(128)} %bitcast.place_ref, bf16[768,3072]{1,0:T(8,128)(2,1)} %get-tuple-element.64.z_ref, bf16[1,750,768]{2,1,0:T(8,128)(2,1)} %cot_ref.3, bf16[768,384]{1,0:T(8,128)(2,1)} %get-tuple-element.67.token_ref), custom_call_target="tpu_custom_call" | custom-call | flops 3623878656 | bytes 9437184 | tf_op jit(solution)/shard_map/third_gradient/pallas_call | solution.py:629
  148.9 10.2 %second_gradient.1 = bf16[768,3840]{1,0:T(8,128)(2,1)} custom-call(s32[1]{0:T(128)} %bitcast.1.place_ref, bf16[8,192,768]{2,1,0:T(8,128)(2,1)} %get-tuple-element.69.token_ref, bf16[768,384]{1,0:T(8,128)(2,1)} %get-tuple-element.60.mine_ref.o_mine_ref, bf16[768,384]{1,0:T(8,128)(2,1)} %copy-done.7, bf16[768,768]{1,0:T(8,128)(2,1)} %get-tuple-element.84.residual_ref.drb_ref, ...), custom_call_target="tpu_custom_call" | custom-call | flops 4529848320 | bytes 9437184 | tf_op jit(solution)/shard_map/second_gradient/pallas_call | solution.py:559
  161.2 2.2 convert_add_fusion
  164.7 11.0 %collective-permute-done.8.got_ref = bf16[768,384]{1,0:T(8,128)(2,1)} collective-permute-done((bf16[768,384]{1,0:T(8,128)(2,1)}, bf16[768,384]{1,0:T(8,128)(2,1)}, u32[]{:S(2)}, u32[]{:S(2)}) %collective-permute-start.8) | collective-permute-done | bytes 589856 | tf_op jit(solution)/shard_map/ppermute | solution.py:897
  175.7 42.8 %attention_backward.1.token_ref.refs_0_ = bf16[3,1536,384]{2,1,0:T(8,128)(2,1)} custom-call(bf16[1536,1152]{1,0:T(8,128)(2,1)} %get-tuple-element.59.q_ref.k_ref.v_ref, bf16[1536,1152]{1,0:T(8,128)(2,1)} %get-tuple-element.59.q_ref.k_ref.v_ref, bf16[1536,1152]{1,0:T(8,128)(2,1)} %get-tuple-element.59.q_ref.k_ref.v_ref, ...), custom_call_target="tpu_custom_call" | custom-call | flops 28991029248 | bytes 9437184 | tf_op jit(solution)/shard_map/attention_backward/pallas_call | solution.py:162
  218.5 4.5 %projection_input_gradient.2 = bf16[768,768]{1,0:T(8,128)(2,1)} custom-call(bf16[3,1536,384]{2,1,0:T(8,128)(2,1)} %attention_backward.1.token_ref.refs_0_, bf16[1152,768]{1,0:T(8,128)(2,1)} %get-tuple-element.72.wt_ref, bf16[3,1536,384]{2,1,0:T(8,128)(2,1)} %attention_backward.1.token_ref.refs_0_), custom_call_target="tpu_custom_call" | custom-call | flops 1358954496 | bytes 3538944 | tf_op jit(solution)/shard_map/projection_input_gradient/pallas_call | solution.py:520
  224.3 12.5 %spread_weight_gradient.1 = (bf16[8,48,1280]{2,1,0:T(8,128)(2,1)}, bf16[8,48,1280]{2,1,0:T(8,128)(2,1)}) custom-call(s32[2]{0:T(128)} %pad_add_fusion.1.place_ref, bf16[4,96,768]{2,1,0:T(8,128)(2,1)} %get-tuple-element.105.token_ref, bf16[784,1536]{1,0:T(8,128)(2,1)} %get-tuple-element.74.xt_ref, bf16[768,1152]{1,0:T(8,128)(2,1)} %get-tuple-element.75.w_ref, ...), custom_call_target="tpu_custom_call" | custom-call | flops 2717908992 | bytes 4718592 | tf_op jit(solution)/shard_map/spread_weight_gradient/pallas_call | solution.py:481
  242.6 12.1 %collective-permute-done.10 = bf16[4,96,768]{2,1,0:T(8,128)(2,1)S(1)} collective-permute-done((bf16[4,96,768]{2,1,0:T(8,128)(2,1)}, bf16[4,96,768]{2,1,0:T(8,128)(2,1)S(1)}, u32[]{:S(2)}, u32[]{:S(2)}) %collective-permute-start.10) | collective-permute-done | bytes 589856 | tf_op jit(solution)/shard_map/ppermute | solution.py:897
  256.2 2.0 collective-permute-start.20
  260.0 4.5 %projection_input_gradient.3.mine_ref = bf16[768,768]{1,0:T(8,128)(2,1)} custom-call(bf16[96,768]{1,0:T(8,128)(2,1)} %copy-done.8, bf16[1152,768]{1,0:T(8,128)(2,1)} %get-tuple-element.72.wt_ref, bf16[3,1536,384]{2,1,0:T(8,128)(2,1)} %attention_backward.1.token_ref.refs_0_), custom_call_target="tpu_custom_call" | custom-call | flops 1358954496 | bytes 3538944 | tf_op jit(solution)/shard_map/projection_input_gradient/pallas_call | solution.py:520
  265.5 5.1 %input_end.1 = f32[750,1,768]{2,1,0:T(1,128)} custom-call(bf16[768,768]{1,0:T(8,128)(2,1)} %projection_input_gradient.3.mine_ref, bf16[768,768]{1,0:T(8,128)(2,1)} %collective-permute-done.12.got_ref, bf16[768,768]{1,0:T(8,128)(2,1)} %get-tuple-element.84.residual_ref.drb_ref, f32[1536,768]{1,0:T(8,128)} %get-tuple-element.58.x_ref.normed_ref, ...), custom_call_target="tpu_custom_call" | custom-call | flops 5898240 | bytes 10616832 | tf_op jit(solution)/shard_map/input_end/pallas_call | solution.py:880
  270.7 8.7 %output_end.1 = bf16[1,750,768]{2,1,0:T(8,128)(2,1)} custom-call(bf16[96,768]{1,0:T(8,128)(2,1)} %copy-done.8, bf16[768,3072]{1,0:T(8,128)(2,1)} %get-tuple-element.64.z_ref, bf16[3072,768]{1,0:T(8,128)(2,1)} %get-tuple-element.83.w_ref, f32[768,768]{1,0:T(8,128)} %get-tuple-element.66.late_ref.residual_ref, f32[1,768]{1,0:T(1,128)} %get-tuple-element.126.rows_ref), custom_call_target="tpu_custom_call" | custom-call | flops 3623878656 | bytes 9437184 | tf_op jit(solution)/shard_map/output_end/pallas_call | solution.py:829
  281.2 1.9 collective-permute-start.15
  283.1 2.0 collective-permute-start.16
  288.2 4.9 %collective-permute-done.15 = bf16[48,1280]{1,0:T(8,128)(2,1)S(1)} collective-permute-done((bf16[48,1280]{1,0:T(8,128)(2,1)S(1)}, bf16[48,1280]{1,0:T(8,128)(2,1)S(1)}, u32[]{:S(2)}, u32[]{:S(2)}) %collective-permute-start.15) | collective-permute-done | bytes 122912 | tf_op jit(solution)/shard_map/ppermute | solution.py:897
  296.4 4.8 %collective-permute-done.17.theirs_ref = bf16[48,1280]{1,0:T(8,128)(2,1)S(1)} collective-permute-done((bf16[48,1280]{1,0:T(8,128)(2,1)S(1)}, bf16[48,1280]{1,0:T(8,128)(2,1)S(1)}, u32[]{:S(2)}, u32[]{:S(2)}) %collective-permute-start.17) | collective-permute-done | bytes 122912 | tf_op jit(solution)/shard_map/ppermute | solution.py:897
  301.9 1.8 finish.1
  304.5 2.0 join_second.1
  (118 shorter events, 40.7 us)
Async XLA Ops:
  7.3 8.4 %copy-start.1 = (bf16[1,750,768]{2,1,0:T(8,128)(2,1)S(1)}, bf16[1,750,768]{2,1,0:T(8,128)(2,1)}, u32[]{:S(2)}) copy-start(bf16[1,750,768]{2,1,0:T(8,128)(2,1)} %x_ref.3) | copy-start | bytes 3456004
  7.3 96.7 %all-gather.2.cloned.1.call-start = ((), (), s32[]{:S(2)}) async-start(), calls=%async_computation.1 | async-start | bytes 11280384 | tf_op jit(solution)/shard_map/all_gather | solution.py:990
  9.5 278.1 %reduce-scatter.2.cloned.1.call-start = ((), (), s32[]{:S(2)}) async-start(), calls=%async_computation.2 | async-start | bytes 6266880 | tf_op jit(solution)/shard_map/reduce_scatter | solution.py:1031
  10.0 33.8 %copy-start = (s32[16]{0:T(128)S(1)}, s32[16]{0:T(128)}, u32[]{:S(2)}) copy-start(s32[16]{0:T(128)} %constant.112.clone) | copy-start | bytes 196
  10.0 8.1 %collective-permute-start = (bf16[48,1280]{1,0:T(8,128)(2,1)S(1)}, bf16[48,1280]{1,0:T(8,128)(2,1)S(1)}, u32[]{:S(2)}, u32[]{:S(2)}) collective-permute-start(bf16[48,1280]{1,0:T(8,128)(2,1)S(1)} %get-tuple-element.124), channel_id=1, source_target_pairs={{0,8},{2,10},{4,12},{6,14},{8,0},{10,2},{12,4},{14,6},{16,24},{18,... | collective-permute-start | bytes 368648 | tf_op jit(solution)/shard_map/ppermute | solution.py:897
  13.1 12.3 %collective-permute-start.1 = (bf16[48,1280]{1,0:T(8,128)(2,1)S(1)}, bf16[48,1280]{1,0:T(8,128)(2,1)S(1)}, u32[]{:S(2)}, u32[]{:S(2)}) collective-permute-start(bf16[48,1280]{1,0:T(8,128)(2,1)S(1)} %get-tuple-element.124), channel_id=1, source_target_pairs={{0,16},{2,18},{4,20},{6,22},{8,24},{10,26},{12,28},{14,30},{16,0},... | collective-permute-start | bytes 368648 | tf_op jit(solution)/shard_map/ppermute | solution.py:897
  15.7 9.7 %collective-permute-start.2 = (bf16[48,1280]{1,0:T(8,128)(2,1)S(1)}, bf16[48,1280]{1,0:T(8,128)(2,1)S(1)}, u32[]{:S(2)}, u32[]{:S(2)}) collective-permute-start(bf16[48,1280]{1,0:T(8,128)(2,1)S(1)} %get-tuple-element.124), channel_id=1, source_target_pairs={{0,24},{2,26},{4,28},{6,30},{8,16},{10,18},{12,20},{14,22},{16,8},... | collective-permute-start | bytes 368648 | tf_op jit(solution)/shard_map/ppermute | solution.py:897
  15.7 32.7 %collective-permute-start.5 = (bf16[1,750,768]{2,1,0:T(8,128)(2,1)S(1)}, bf16[1,750,768]{2,1,0:T(8,128)(2,1)S(1)}, u32[]{:S(2)}, u32[]{:S(2)}) collective-permute-start(bf16[1,750,768]{2,1,0:T(8,128)(2,1)S(1)} %copy-done.1), channel_id=1, source_target_pairs={{0,1},{1,0},{2,3},{3,2},{4,5},{5,4},{6,7},{7,6},{8,9},{9,8},{10,11... | collective-permute-start | bytes 3456008 | tf_op jit(solution)/shard_map/ppermute | solution.py:897
  25.5 16.1 %collective-permute-start.3 = (bf16[4,48,1280]{2,1,0:T(8,128)(2,1)S(1)}, bf16[4,48,1280]{2,1,0:T(8,128)(2,1)S(1)}, u32[]{:S(2)}, u32[]{:S(2)}) collective-permute-start(bf16[4,48,1280]{2,1,0:T(8,128)(2,1)S(1)} %pad_maximum_fusion), channel_id=1, source_target_pairs={{0,4},{2,6},{4,0},{6,2},{8,12},{10,14},{12,8},{14,10},{16,20},{18,... | collective-permute-start | bytes 1474568 | tf_op jit(solution)/shard_map/ppermute | solution.py:897
  43.7 9.2 %collective-permute-start.4 = (bf16[8,48,1280]{2,1,0:T(8,128)(2,1)}, bf16[8,48,1280]{2,1,0:T(8,128)(2,1)S(1)}, u32[]{:S(2)}, u32[]{:S(2)}) collective-permute-start(bf16[8,48,1280]{2,1,0:T(8,128)(2,1)} %get-tuple-element.110), channel_id=1, source_target_pairs={{0,2},{2,0},{4,6},{6,4},{8,10},{10,8},{12,14},{14,12},{16,18},{18,... | collective-permute-start | bytes 2949128 | tf_op jit(solution)/shard_map/ppermute | solution.py:897
  84.2 16.0 %collective-permute-start.6 = (bf16[768,384]{1,0:T(8,128)(2,1)}, bf16[768,384]{1,0:T(8,128)(2,1)S(1)}, u32[]{:S(2)}, u32[]{:S(2)}) collective-permute-start(bf16[768,384]{1,0:T(8,128)(2,1)} %get-tuple-element.61.o_sent_ref), channel_id=1, source_target_pairs={{0,1},{1,0},{2,3},{3,2},{4,5},{5,4},{6,7},{7,6},{8,9},{9,8},{10,11... | collective-permute-start | bytes 1769480 | tf_op jit(solution)/shard_map/ppermute | solution.py:897
  148.6 12.6 %collective-permute-start.7 = (bf16[8,192,768]{2,1,0:T(8,128)(2,1)}, bf16[8,192,768]{2,1,0:T(8,128)(2,1)}, u32[]{:S(2)}, u32[]{:S(2)}) collective-permute-start(bf16[8,192,768]{2,1,0:T(8,128)(2,1)} %get-tuple-element.69.token_ref), channel_id=1, source_target_pairs={{0,2},{2,0},{4,6},{6,4},{8,10},{10,8},{12,14},{14,12},{16,18},{18,... | collective-permute-start | bytes 7077896 | tf_op jit(solution)/shard_map/ppermute | solution.py:897
  159.1 16.6 %collective-permute-start.8 = (bf16[768,384]{1,0:T(8,128)(2,1)}, bf16[768,384]{1,0:T(8,128)(2,1)}, u32[]{:S(2)}, u32[]{:S(2)}) collective-permute-start(bf16[768,384]{1,0:T(8,128)(2,1)} %get-tuple-element.67.token_ref), channel_id=1, source_target_pairs={{0,1},{1,0},{2,3},{3,2},{4,5},{5,4},{6,7},{7,6},{8,9},{9,8},{10,11... | collective-permute-start | bytes 1769480 | tf_op jit(solution)/shard_map/ppermute | solution.py:897
  163.7 12.0 %copy-start.5 = (bf16[8,96,768]{2,1,0:T(8,128)(2,1)}, bf16[8,96,768]{2,1,0:T(8,128)(2,1)S(1)}, u32[]{:S(2)}) copy-start(bf16[8,96,768]{2,1,0:T(8,128)(2,1)S(1)} %get-tuple-element.101.token_ref) | copy-start | bytes 3538948
  163.7 59.3 %collective-permute-start.9 = (bf16[8,96,768]{2,1,0:T(8,128)(2,1)S(1)}, bf16[8,96,768]{2,1,0:T(8,128)(2,1)S(1)}, u32[]{:S(2)}, u32[]{:S(2)}) collective-permute-start(bf16[8,96,768]{2,1,0:T(8,128)(2,1)S(1)} %get-tuple-element.101.token_ref), channel_id=1, source_target_pairs={{0,1},{1,0},{2,3},{3,2},{4,5},{5,4},{6,7},{7,6},{8,9},{9,8},{10,11... | collective-permute-start | bytes 3538952 | tf_op jit(solution)/shard_map/ppermute | solution.py:897
  236.8 2.8 collective-permute-start.11
  236.8 28.7 %collective-permute-start.12 = (bf16[768,768]{1,0:T(8,128)(2,1)}, bf16[768,768]{1,0:T(8,128)(2,1)}, u32[]{:S(2)}, u32[]{:S(2)}) collective-permute-start(bf16[768,768]{1,0:T(8,128)(2,1)} %projection_input_gradient.2), channel_id=1, source_target_pairs={{0,1},{1,0},{2,3},{3,2},{4,5},{5,4},{6,7},{7,6},{8,9},{9,8},{10,11... | collective-permute-start | bytes 3538952 | tf_op jit(solution)/shard_map/ppermute | solution.py:897
  238.3 16.4 %collective-permute-start.10 = (bf16[4,96,768]{2,1,0:T(8,128)(2,1)}, bf16[4,96,768]{2,1,0:T(8,128)(2,1)S(1)}, u32[]{:S(2)}, u32[]{:S(2)}) collective-permute-start(bf16[4,96,768]{2,1,0:T(8,128)(2,1)} %get-tuple-element.105.token_ref), channel_id=1, source_target_pairs={{0,4},{2,6},{4,0},{6,2},{8,12},{10,14},{12,8},{14,10},{16,20},{18,... | collective-permute-start | bytes 1769480 | tf_op jit(solution)/shard_map/ppermute | solution.py:897
  239.6 15.1 %copy-start.4 = (bf16[4,96,768]{2,1,0:T(8,128)(2,1)S(1)}, bf16[4,96,768]{2,1,0:T(8,128)(2,1)}, u32[]{:S(2)}) copy-start(bf16[4,96,768]{2,1,0:T(8,128)(2,1)} %get-tuple-element.81) | copy-start | bytes 1769476
  241.9 37.4 %collective-permute-start.13 = (bf16[4,48,1280]{2,1,0:T(8,128)(2,1)}, bf16[4,48,1280]{2,1,0:T(8,128)(2,1)}, u32[]{:S(2)}, u32[]{:S(2)}) collective-permute-start(bf16[4,48,1280]{2,1,0:T(8,128)(2,1)} %fusion.11), channel_id=1, source_target_pairs={{0,4},{2,6},{4,0},{6,2},{8,12},{10,14},{12,8},{14,10},{16,20},{18,... | collective-permute-start | bytes 1474568 | tf_op jit(solution)/shard_map/ppermute | solution.py:897
  255.6 4.4 %copy-start.8 = (bf16[96,768]{1,0:T(8,128)(2,1)}, bf16[96,768]{1,0:T(8,128)(2,1)S(1)}, u32[]{:S(2)}) copy-start(bf16[96,768]{1,0:T(8,128)(2,1)S(1)} %get-tuple-element.104.token_ref) | copy-start | bytes 442372
  255.6 27.5 %collective-permute-start.19 = (bf16[96,768]{1,0:T(8,128)(2,1)}, bf16[96,768]{1,0:T(8,128)(2,1)S(1)}, u32[]{:S(2)}, u32[]{:S(2)}) collective-permute-start(bf16[96,768]{1,0:T(8,128)(2,1)} %get-tuple-element.102), channel_id=1, source_target_pairs={{0,8},{2,10},{4,12},{6,14},{8,0},{10,2},{12,4},{14,6},{16,24},{18,... | collective-permute-start | bytes 442376 | tf_op jit(solution)/shard_map/ppermute | solution.py:897
  256.2 28.8 %collective-permute-start.20 = (bf16[96,768]{1,0:T(8,128)(2,1)}, bf16[96,768]{1,0:T(8,128)(2,1)}, u32[]{:S(2)}, u32[]{:S(2)}) collective-permute-start(bf16[96,768]{1,0:T(8,128)(2,1)} %get-tuple-element.103), channel_id=1, source_target_pairs={{0,16},{2,18},{4,20},{6,22},{8,24},{10,26},{12,28},{14,30},{16,0},... | collective-permute-start | bytes 442376 | tf_op jit(solution)/shard_map/ppermute | solution.py:897
  258.2 26.8 %collective-permute-start.21 = (bf16[96,768]{1,0:T(8,128)(2,1)S(1)}, bf16[96,768]{1,0:T(8,128)(2,1)}, u32[]{:S(2)}, u32[]{:S(2)}) collective-permute-start(bf16[96,768]{1,0:T(8,128)(2,1)S(1)} %get-tuple-element.104.token_ref), channel_id=1, source_target_pairs={{0,24},{2,26},{4,28},{6,30},{8,16},{10,18},{12,20},{14,22},{16,8},... | collective-permute-start | bytes 442376 | tf_op jit(solution)/shard_map/ppermute | solution.py:897
  280.5 5.6 %copy-start.2 = (f32[4,48,1280]{2,1,0:T(8,128)}, f32[4,48,1280]{2,1,0:T(8,128)S(1)}, u32[]{:S(2)}) copy-start(f32[4,48,1280]{2,1,0:T(8,128)S(1)} %bitcast_add_fusion) | copy-start | bytes 2949124
  280.6 7.6 %collective-permute-start.14 = (bf16[48,1280]{1,0:T(8,128)(2,1)S(1)}, bf16[48,1280]{1,0:T(8,128)(2,1)S(1)}, u32[]{:S(2)}, u32[]{:S(2)}) collective-permute-start(bf16[48,1280]{1,0:T(8,128)(2,1)S(1)} %get-tuple-element.107), channel_id=1, source_target_pairs={{0,8},{2,10},{4,12},{6,14},{8,0},{10,2},{12,4},{14,6},{16,24},{18,... | collective-permute-start | bytes 368648 | tf_op jit(solution)/shard_map/ppermute | solution.py:897
  281.2 11.9 %collective-permute-start.15 = (bf16[48,1280]{1,0:T(8,128)(2,1)S(1)}, bf16[48,1280]{1,0:T(8,128)(2,1)S(1)}, u32[]{:S(2)}, u32[]{:S(2)}) collective-permute-start(bf16[48,1280]{1,0:T(8,128)(2,1)S(1)} %get-tuple-element.109), channel_id=1, source_target_pairs={{0,16},{2,18},{4,20},{6,22},{8,24},{10,26},{12,28},{14,30},{16,0},... | collective-permute-start | bytes 368648 | tf_op jit(solution)/shard_map/ppermute | solution.py:897
  283.1 10.0 %collective-permute-start.16 = (bf16[48,1280]{1,0:T(8,128)(2,1)S(1)}, bf16[48,1280]{1,0:T(8,128)(2,1)S(1)}, u32[]{:S(2)}, u32[]{:S(2)}) collective-permute-start(bf16[48,1280]{1,0:T(8,128)(2,1)S(1)} %get-tuple-element.108), channel_id=1, source_target_pairs={{0,24},{2,26},{4,28},{6,30},{8,16},{10,18},{12,20},{14,22},{16,8},... | collective-permute-start | bytes 368648 | tf_op jit(solution)/shard_map/ppermute | solution.py:897
  286.1 9.5 %collective-permute-start.22 = (bf16[96,768]{1,0:T(8,128)(2,1)S(1)}, bf16[96,768]{1,0:T(8,128)(2,1)S(1)}, u32[]{:S(2)}, u32[]{:S(2)}) collective-permute-start(bf16[96,768]{1,0:T(8,128)(2,1)S(1)} %fusion.15), channel_id=1, source_target_pairs={{0,1},{1,0},{2,3},{3,2},{4,5},{5,4},{6,7},{7,6},{8,9},{9,8},{10,11... | collective-permute-start | bytes 442376 | tf_op jit(solution)/shard_map/ppermute | solution.py:897
  287.6 16.1 %collective-permute-start.18 = (bf16[48,3840]{1,0:T(8,128)(2,1)}, bf16[48,3840]{1,0:T(8,128)(2,1)S(1)}, u32[]{:S(2)}, u32[]{:S(2)}) collective-permute-start(bf16[48,3840]{1,0:T(8,128)(2,1)} %reduce-scatter.2.cloned.1.call-done.mine_ref), channel_id=1, source_target_pairs={{0,1},{1,0},{2,3},{3,2},{4,5},{5,4},{6,7},{7,6},{8,9},{9,8},{10,11... | collective-permute-start | bytes 1105928 | tf_op jit(solution)/shard_map/ppermute | solution.py:897
  294.1 7.1 %copy-start.9 = (bf16[48,1280]{1,0:T(8,128)(2,1)}, bf16[48,1280]{1,0:T(8,128)(2,1)S(1)}, u32[]{:S(2)}) copy-start(bf16[48,1280]{1,0:T(8,128)(2,1)S(1)} %fusion.18.mine_ref) | copy-start | bytes 368644
  294.1 7.1 %collective-permute-start.17 = (bf16[48,1280]{1,0:T(8,128)(2,1)S(1)}, bf16[48,1280]{1,0:T(8,128)(2,1)S(1)}, u32[]{:S(2)}, u32[]{:S(2)}) collective-permute-start(bf16[48,1280]{1,0:T(8,128)(2,1)S(1)} %fusion.18.mine_ref), channel_id=1, source_target_pairs={{0,1},{1,0},{2,3},{3,2},{4,5},{5,4},{6,7},{7,6},{8,9},{9,8},{10,11... | collective-permute-start | bytes 368648 | tf_op jit(solution)/shard_map/ppermute | solution.py:897
  (15 other events, 31.2 us)
Sparse Core Ops, SparseCore 0:
  10.4 93.6 all-gather.1
  159.2 83.3 reduce-scatter.1

commit v5 on v4

--- a/solution.py
+++ b/solution.py
@@ -283,7 +283,7 @@
     def _():
         blocks, extent, _ = held_ref.shape
         for d in range(blocks):
-            block = held_ref[place_ref[d]]
+            block = held_ref[place_ref[2 + d]]
             w_ref[d * extent : (d + 1) * extent, :] = block[:, :width]
             columns_ref[d * extent : (d + 1) * extent, :] = block[:, width:].astype(F32)
         wt_ref[...] = w_ref[...].T
@@ -292,7 +292,7 @@
         scale_ref[:, :128] = jnp.broadcast_to(columns_ref[:, 0:1], (wide, 128))
         scale_ref[:, 128:] = jnp.broadcast_to(columns_ref[:, 1:2], (wide, 128))
         gain_ref[...] = table[:8]
-        here = place_ref[blocks]
+        here = place_ref[0]
         few = group // 2
         row = lax.broadcasted_iota(jnp.int32, (few, group), 0)
         entry = lax.broadcasted_iota(jnp.int32, (few, group), 1)
@@ -448,7 +448,7 @@
         low = lane[:half]
         for side in (0, 2):
             v = s_ref[side].T[:, 0:1]
-            at = pl.ds(pl.multiple_of(place_ref[1] * half + side * wide // 4, 64), half)
+            at = pl.ds(pl.multiple_of(place_ref[0] * half + side * wide // 4, 64), half)
             block = c_ref[at, :]
             for j in range(2):
                 column = jnp.concatenate(
@@ -463,7 +463,7 @@
 def spread_store(part, place_ref, keep_ref, give_ref, value, columns):
     value = value.reshape(keep_ref.shape[0], 2, part, value.shape[1])
     even, odd = value[:, 0], value[:, 1]
-    low = place_ref[0] == 0
+    low = place_ref[1] == 0
     keep_ref[:, :, columns] = jnp.where(low, even, odd)
     give_ref[:, :, columns] = jnp.where(low, odd, even)
 
@@ -609,18 +609,18 @@
     owners, extent, wide = keep_ref.shape
     value = value.reshape(owners, 2, extent, wide)
 
-    @pl.when(place_ref[0] == 0)
+    @pl.when(place_ref[1] == 0)
     def _():
         keep_ref[...] = value[:, 0]
         give_ref[...] = value[:, 1]
 
-    @pl.when(place_ref[0] == 1)
+    @pl.when(place_ref[1] == 1)
     def _():
         keep_ref[...] = value[:, 1]
         give_ref[...] = value[:, 0]
 
 
-def third_gradient(parity, activated, cotangent, size, token):
+def third_gradient(flag, activated, cotangent, size, token):
     _, valid, wide = cotangent.shape
     rows, ff = activated.shape
     extent = ff // size
@@ -644,7 +644,7 @@
             flops=2 * rows * wide * ff, bytes_accessed=rows * ff * 4, transcendentals=0
         ),
         name="third_gradient",
-    )(parity, activated, cotangent, token)
+    )(flag, activated, cotangent, token)
 
 
 def feed_back_kernel(
@@ -809,18 +809,24 @@
     )(here, mine, theirs)
 
 
-def output_kernel(token_ref, z_ref, w_ref, residual_ref, rows_ref, out_ref, total_ref):
+def output_kernel(
+    token_ref, z_ref, w_ref, late_ref, rows_ref, out_ref, total_ref, residual_ref, sem_ref
+):
     step = pl.program_id(0)
+    copy = pltpu.make_async_copy(late_ref, residual_ref, sem_ref)
 
     @pl.when(step == 0)
     def _():
-        total_ref[...] = residual_ref[...] + rows_ref[-1:, :]
+        copy.start()
+        total_ref[...] = jnp.zeros_like(total_ref)
 
     total_ref[...] += dot(z_ref[...], w_ref[...])
 
     @pl.when(step == pl.num_programs(0) - 1)
     def _():
-        out_ref[0] = total_ref[: out_ref.shape[1], :].astype(BF)
+        copy.wait()
+        total = total_ref[...] + residual_ref[...] + rows_ref[-1:, :]
+        out_ref[0] = total[: out_ref.shape[1], :].astype(BF)
 
 
 def output_end(token, activated, w, residual, bias, valid):
@@ -833,12 +839,16 @@
             pl.BlockSpec(memory_space=pl.ANY),
             pl.BlockSpec((rows, wide), lambda i: (0, i)),
             pl.BlockSpec((wide, wide), lambda i: (i, 0)),
-            pl.BlockSpec((rows, wide), lambda i: (0, 0)),
+            pl.BlockSpec(memory_space=pl.ANY),
             pl.BlockSpec((1, wide), lambda i: (0, 0)),
         ],
         out_specs=pl.BlockSpec((1, valid, wide), lambda i: (0, 0, 0)),
         out_shape=jax.ShapeDtypeStruct((1, valid, wide), BF),
-        scratch_shapes=[pltpu.VMEM((rows, wide), F32)],
+        scratch_shapes=[
+            pltpu.VMEM((rows, wide), F32),
+            pltpu.VMEM((rows, wide), F32),
+            pltpu.SemaphoreType.DMA,
+        ],
         cost_estimate=pl.CostEstimate(
             flops=2 * rows * wide * ff, bytes_accessed=rows * ff * 4, transcendentals=0
         ),
@@ -981,7 +991,7 @@
     if part % 16:
         held = jnp.take(held, place, axis=0, mode="clip").reshape(1, wide, 3 * group + 128)
         place = jnp.zeros((1,), jnp.int32)
-    place = jnp.concatenate([place, jnp.full((1,), here, jnp.int32)])
+    flag = jnp.concatenate([jnp.stack([here, lax.rem(me, 2)]).astype(jnp.int32), place])
     if part % 16:
         fc2_local = w_fc2.reshape(per, part, wide).transpose(1, 0, 2).reshape(part, ff)
         packed = jnp.concatenate([fc2_local, w_o, w_fc1], axis=1)
@@ -997,7 +1007,7 @@
     prepared = prepare(frames_in, half, 0)
     inverse_one = prepared[2]
     normed_both, normed_t, _ = prepare(other(frames_in), half, 1, prepared[:2])
-    qkv, w_full, w_flipped, table, scale = projection(held, place, normed_both, part)
+    qkv, w_full, w_flipped, table, scale = projection(held, flag, normed_both, part)
 
     def vector(start, stop):
         return table[start:stop].reshape(-1, size, part).transpose(1, 0, 2).reshape(-1)
@@ -1006,7 +1016,6 @@
     bias_fc1, bias_fc2 = vector(7, 7 + per), table[7 + per]
     o_mine, o_sent, lse = attention_forward(qkv, half, valid)
     o_got = other(o_sent)
-    flag = jnp.full((1,), here, jnp.int32)
     if part % 16:
         residual, hidden_two = attend(flag, frames_in, o_mine, o_got, out_full, 0, table)
     else:
@@ -1023,8 +1032,7 @@
         do_mine, do_sent, grad_bias_fc1, grad_sums,
     ) = feed_back(flag, weights, slope, cotangent, residual, gain_two[None], part)
     do_got = other(do_sent)
-    parity = jnp.full((1,), lax.rem(me, 2), jnp.int32)
-    fc2_keep, fc2_give = third_gradient(parity, activated, cotangent, size, do_sent)
+    fc2_keep, fc2_give = third_gradient(flag, activated, cotangent, size, do_sent)
     second_part = second_gradient(
         flag, fc2_give, o_mine, o_got, grad_residual_low, hidden_two, grad_pre_low
     )
@@ -1069,9 +1077,8 @@
         x = jnp.concatenate([grad_qkv.reshape(size, part, -1), columns.astype(BF)], axis=2)
         keep, give = halve(x.reshape(size // 2, 2, *x.shape[1:]), 1, 1)
     else:
-        sides = jnp.concatenate([parity, jnp.full((1,), here, jnp.int32)])
         keep, give = spread_weight_gradient(
-            sides, give, normed_t, w_full, scale, ds, grad_bias_fc1, grad_sums, part
+            flag, give, normed_t, w_full, scale, ds, grad_bias_fc1, grad_sums, part
         )
     got = swap(give, "dp", size, 1)
     for at in range(len(bits) - 2, -1, -1):

time: 314 us -> 317 us (level)
  transfers between devices with their start and end apart: 25 -> 25, of which waited for: 10 -> 11; matrix products, arithmetic and copies ran while one was open for 6% -> 6% of each run, Pallas kernels for 41% -> 40%
where the time goes in v5:
time: 317 us; the launch traced here: 316 us
  Pallas kernels  168 us (53%)
  waiting for transfers between devices  70.4 us (22%)
  starting transfers between devices  29.1 us (9%)
  between operations  14.4 us (5%)
  local copies, waits for them, and re-layouts  14 us (4%)
  matrix products  10.9 us (3%)
  other arithmetic  9.44 us (3%)
    ppermute x23, waiting for transfers between devices, swap(): return lax.ppermute(x, axis, [(i, i ^ bit) for i in range(size)])  66.4 us
    pallas_call x1, Pallas kernels, attention_backward(): pl.pallas_call(functools.partial(backward_kernel, half, valid), grid=(cou...  42.8 us
    ppermute x23, starting transfers between devices, swap(): return lax.ppermute(x, axis, [(i, i ^ bit) for i in range(size)])  29.1 us
    pallas_call x1, Pallas kernels, feed_back(): pl.pallas_call(functools.partial(feed_back_kernel, part), grid_spec=pltpu...  20.8 us
    pallas_call x1, Pallas kernels, attention_forward(): pl.pallas_call(functools.partial(forward_kernel, half, valid), grid=(pair...  20.7 us
    pallas_call x1, Pallas kernels, spread_weight_gradient(): pl.pallas_call(functools.partial(spread_kernel, part, len(ds), bias.shape...  12.5 us
    pallas_call x1, Pallas kernels, second_gradient(): pl.pallas_call(second_kernel, grid_spec=pltpu.PrefetchScalarGridSpec(num_...  10.9 us
    dot_general x1, matrix products, dot(): lax.dot_general(a, b, (((ca,), (cb,)), ((), ())), preferred_element_type=...  10.9 us
  transfers between devices with their start and end apart: 25, of which 11 were waited for; matrix products, arithmetic and copies ran while one was open for 6% of the time, Pallas kernels for 40%

profile of v5, /device:TPU:0, one launch (start us, length us, event | category | flops | bytes accessed | tf_op | source)
XLA Modules:
  0.0 316.1 jit_solution(15458573479194017010)
XLA Ops:
  7.3 2.1 pack.1
  10.0 3.1 collective-permute-start
  13.1 2.6 collective-permute-start.1
  15.7 1.7 collective-permute-start.5
  18.1 7.3 %collective-permute-done.1 = bf16[48,1280]{1,0:T(8,128)(2,1)S(1)} collective-permute-done((bf16[48,1280]{1,0:T(8,128)(2,1)S(1)}, bf16[48,1280]{1,0:T(8,128)(2,1)S(1)}, u32[]{:S(2)}, u32[]{:S(2)}) %collective-permute-start.1) | collective-permute-done | bytes 122912 | tf_op jit(solution)/shard_map/ppermute | solution.py:907
  29.1 12.5 %collective-permute-done.3 = bf16[4,48,1280]{2,1,0:T(8,128)(2,1)S(1)} collective-permute-done((bf16[4,48,1280]{2,1,0:T(8,128)(2,1)S(1)}, bf16[4,48,1280]{2,1,0:T(8,128)(2,1)S(1)}, u32[]{:S(2)}, u32[]{:S(2)}) %collective-permute-start.3) | collective-permute-done | bytes 491552 | tf_op jit(solution)/shard_map/ppermute | solution.py:907
  44.4 3.5 %prepare.2 = (f32[1536,768]{1,0:T(8,128)}, bf16[784,1536]{1,0:T(8,128)(2,1)}, f32[768,128]{1,0:T(8,128)}) custom-call(bf16[1,750,768]{2,1,0:T(8,128)(2,1)} %x_ref.3), custom_call_target="tpu_custom_call" | custom-call | flops 9437184 | bytes 4718592 | tf_op jit(solution)/shard_map/prepare/pallas_call | solution.py:209
  49.4 3.4 %prepare.3 = (f32[1536,768]{1,0:T(8,128)}, bf16[784,1536]{1,0:T(8,128)(2,1)}, f32[768,128]{1,0:T(8,128)}) custom-call(bf16[1,750,768]{2,1,0:T(8,128)(2,1)} %copy-done.6, f32[1536,768]{1,0:T(8,128)} %get-tuple-element.56.refs_0_, bf16[784,1536]{1,0:T(8,128)(2,1)} %get-tuple-element.57.refs_1_), custom_call_target="tpu_custom_call", output_to_operand_aliasing={{0}: (1, {}), {1}: (2, {})} | custom-call | flops 9437184 | bytes 4718592 | tf_op jit(solution)/shard_map/prepare/pallas_call | solution.py:209
  53.9 9.5 %projection.1 = (bf16[1536,1152]{1,0:T(8,128)(2,1)}, bf16[768,1152]{1,0:T(8,128)(2,1)}, bf16[1152,768]{1,0:T(8,128)(2,1)}, f32[16,768]{1,0:T(8,128)}, f32[768,256]{1,0:T(8,128)}) custom-call(s32[18]{0:T(128)} %pad_add_fusion.place_ref, bf16[16,48,1280]{2,1,0:T(8,128)(2,1)} %constant_dynamic-update-slice_fusion.5.held_ref, ...), custom_call_target="tpu_custom_call" | custom-call | flops 2717908992 | bytes 9437184 | tf_op jit(solution)/shard_map/projection/pallas_call | solution.py:324
  63.4 20.7 %attention_forward.1 = (bf16[768,384]{1,0:T(8,128)(2,1)}, bf16[768,384]{1,0:T(8,128)(2,1)}, f32[3,8,1536]{2,1,0:T(8,128)}) custom-call(bf16[1536,1152]{1,0:T(8,128)(2,1)} %get-tuple-element.59.q_ref.k_ref.v_ref, bf16[1536,1152]{1,0:T(8,128)(2,1)} %get-tuple-element.59.q_ref.k_ref.v_ref, bf16[1536,1152]{1,0:T(8,128)(2,1)} %get-tuple-element.59.q_ref.k_ref.v_ref), custom_call_target="tpu_custom_call" | custom-call | flops 14495514624 | bytes 5308416 | tf_op jit(solution)/shard_map/attention_forward/pallas_call | solution.py:68
  88.2 11.9 %collective-permute-done.6.got_ref = bf16[768,384]{1,0:T(8,128)(2,1)S(1)} collective-permute-done((bf16[768,384]{1,0:T(8,128)(2,1)}, bf16[768,384]{1,0:T(8,128)(2,1)S(1)}, u32[]{:S(2)}, u32[]{:S(2)}) %collective-permute-start.6) | collective-permute-done | bytes 589856 | tf_op jit(solution)/shard_map/ppermute | solution.py:907
  100.1 3.9 %all-gather.2.cloned.1.call-done.w_ref.fc2_ref.fc1_ref.late_out_ref = bf16[768,6912]{1,0:T(8,128)(2,1)} async-done(((bf16[48,6912]{1,0:T(8,128)(2,1)}), bf16[768,6912]{1,0:T(8,128)(2,1)}) %all-gather.2.cloned.1.call-update) | async-done | bytes 10616848 | tf_op jit(solution)/shard_map/all_gather | solution.py:1000
  104.0 6.0 %attend.1 = (f32[768,768]{1,0:T(8,128)}, bf16[768,768]{1,0:T(8,128)(2,1)}) custom-call(s32[18]{0:T(128)} %pad_add_fusion.place_ref, bf16[1,750,768]{2,1,0:T(8,128)(2,1)} %x_ref.3, bf16[768,384]{1,0:T(8,128)(2,1)} %get-tuple-element.60.mine_ref.o_mine_ref, bf16[768,384]{1,0:T(8,128)(2,1)} %copy-done.7, ...), custom_call_target="tpu_custom_call" | custom-call | flops 905969664 | bytes 5898240 | tf_op jit(solution)/shard_map/attend/pallas_call | solution.py:253
  110.0 10.9 %fusion.4 = (bf16[768,3072]{1,0:T(8,128)(2,1)}, bf16[768,3072]{1,0:T(8,128)(2,1)}) fusion(f32[3072]{0:T(1024)S(1)} %add.122, bf16[768,768]{1,0:T(8,128)(2,1)} %get-tuple-element.63.h_ref, bf16[768,6912]{1,0:T(8,128)(2,1)} %all-gather.2.cloned.1.call-done.w_ref.fc2_ref.fc1_ref.late_out_ref), kind=kOutput, calls=%fused_computation.6 | convolution fusion | flops 3652190208 | bytes 15347712 | tf_op jit(solution)/shard_map/dot_general | solution.py:19
  120.8 20.8 %feed_back.1 = (bf16[768,3072]{1,0:T(8,128)(2,1)}, bf16[3072,768]{1,0:T(8,128)(2,1)}, bf16[768,768]{1,0:T(8,128)(2,1)}, bf16[768,384]{1,0:T(8,128)(2,1)}, bf16[7...) custom-call(s32[18]{0:T(128)} %pad_add_fusion.place_ref, ...), custom_call_target="tpu_custom_call" | custom-call | flops 7247757312 | bytes 23592960 | tf_op jit(solution)/shard_map/feed_back/pallas_call | solution.py:737
  141.6 9.0 %third_gradient.1 = (bf16[8,192,768]{2,1,0:T(8,128)(2,1)}, bf16[8,192,768]{2,1,0:T(8,128)(2,1)}) custom-call(s32[18]{0:T(128)} %pad_add_fusion.place_ref, bf16[768,3072]{1,0:T(8,128)(2,1)} %get-tuple-element.64.z_ref, bf16[1,750,768]{2,1,0:T(8,128)(2,1)} %cot_ref.3, bf16[768,384]{1,0:T(8,128)(2,1)} %get-tuple-element.67.token_ref), custom_call_target="tpu_custom_call" | custom-call | flops 3623878656 | bytes 9437184 | tf_op jit(solution)/shard_map/third_gradient/pallas_call | solution.py:629
  150.9 10.9 %second_gradient.1 = bf16[768,3840]{1,0:T(8,128)(2,1)} custom-call(s32[18]{0:T(128)} %pad_add_fusion.place_ref, bf16[8,192,768]{2,1,0:T(8,128)(2,1)} %get-tuple-element.69.token_ref, bf16[768,384]{1,0:T(8,128)(2,1)} %get-tuple-element.60.mine_ref.o_mine_ref, bf16[768,384]{1,0:T(8,128)(2,1)} %copy-done.7, ...), custom_call_target="tpu_custom_call" | custom-call | flops 4529848320 | bytes 9437184 | tf_op jit(solution)/shard_map/second_gradient/pallas_call | solution.py:559
  163.4 2.2 convert_add_fusion
  167.4 11.0 %collective-permute-done.8.got_ref = bf16[768,384]{1,0:T(8,128)(2,1)} collective-permute-done((bf16[768,384]{1,0:T(8,128)(2,1)}, bf16[768,384]{1,0:T(8,128)(2,1)}, u32[]{:S(2)}, u32[]{:S(2)}) %collective-permute-start.8) | collective-permute-done | bytes 589856 | tf_op jit(solution)/shard_map/ppermute | solution.py:907
  178.4 42.8 %attention_backward.1.token_ref.refs_0_ = bf16[3,1536,384]{2,1,0:T(8,128)(2,1)} custom-call(bf16[1536,1152]{1,0:T(8,128)(2,1)} %get-tuple-element.59.q_ref.k_ref.v_ref, bf16[1536,1152]{1,0:T(8,128)(2,1)} %get-tuple-element.59.q_ref.k_ref.v_ref, bf16[1536,1152]{1,0:T(8,128)(2,1)} %get-tuple-element.59.q_ref.k_ref.v_ref, ...), custom_call_target="tpu_custom_call" | custom-call | flops 28991029248 | bytes 9437184 | tf_op jit(solution)/shard_map/attention_backward/pallas_call | solution.py:162
  221.2 4.5 %projection_input_gradient.2 = bf16[768,768]{1,0:T(8,128)(2,1)} custom-call(bf16[3,1536,384]{2,1,0:T(8,128)(2,1)} %attention_backward.1.token_ref.refs_0_, bf16[1152,768]{1,0:T(8,128)(2,1)} %get-tuple-element.72.wt_ref, bf16[3,1536,384]{2,1,0:T(8,128)(2,1)} %attention_backward.1.token_ref.refs_0_), custom_call_target="tpu_custom_call" | custom-call | flops 1358954496 | bytes 3538944 | tf_op jit(solution)/shard_map/projection_input_gradient/pallas_call | solution.py:520
  227.1 12.5 %spread_weight_gradient.1 = (bf16[8,48,1280]{2,1,0:T(8,128)(2,1)}, bf16[8,48,1280]{2,1,0:T(8,128)(2,1)}) custom-call(s32[18]{0:T(128)} %pad_add_fusion.place_ref, bf16[4,96,768]{2,1,0:T(8,128)(2,1)} %get-tuple-element.105.token_ref, bf16[784,1536]{1,0:T(8,128)(2,1)} %get-tuple-element.74.xt_ref, bf16[768,1152]{1,0:T(8,128)(2,1)} %get-tuple-element.75.w_ref, ...), custom_call_target="tpu_custom_call" | custom-call | flops 2717908992 | bytes 4718592 | tf_op jit(solution)/shard_map/spread_weight_gradient/pallas_call | solution.py:481
  245.3 12.1 %collective-permute-done.10 = bf16[4,96,768]{2,1,0:T(8,128)(2,1)S(1)} collective-permute-done((bf16[4,96,768]{2,1,0:T(8,128)(2,1)}, bf16[4,96,768]{2,1,0:T(8,128)(2,1)S(1)}, u32[]{:S(2)}, u32[]{:S(2)}) %collective-permute-start.10) | collective-permute-done | bytes 589856 | tf_op jit(solution)/shard_map/ppermute | solution.py:907
  260.9 1.8 collective-permute-start.19
  262.7 4.5 %projection_input_gradient.3.mine_ref = bf16[768,768]{1,0:T(8,128)(2,1)} custom-call(bf16[96,768]{1,0:T(8,128)(2,1)} %copy-done.8, bf16[1152,768]{1,0:T(8,128)(2,1)} %get-tuple-element.72.wt_ref, bf16[3,1536,384]{2,1,0:T(8,128)(2,1)} %attention_backward.1.token_ref.refs_0_), custom_call_target="tpu_custom_call" | custom-call | flops 1358954496 | bytes 3538944 | tf_op jit(solution)/shard_map/projection_input_gradient/pallas_call | solution.py:520
  268.3 5.1 %input_end.1 = f32[750,1,768]{2,1,0:T(1,128)} custom-call(bf16[768,768]{1,0:T(8,128)(2,1)} %projection_input_gradient.3.mine_ref, bf16[768,768]{1,0:T(8,128)(2,1)} %collective-permute-done.12.got_ref, bf16[768,768]{1,0:T(8,128)(2,1)} %get-tuple-element.84.residual_ref.drb_ref, f32[1536,768]{1,0:T(8,128)} %get-tuple-element.58.x_ref.normed_ref, ...), custom_call_target="tpu_custom_call" | custom-call | flops 5898240 | bytes 10616832 | tf_op jit(solution)/shard_map/input_end/pallas_call | solution.py:890
  273.4 8.1 %output_end.1 = bf16[1,750,768]{2,1,0:T(8,128)(2,1)} custom-call(bf16[96,768]{1,0:T(8,128)(2,1)} %copy-done.8, bf16[768,3072]{1,0:T(8,128)(2,1)} %get-tuple-element.64.z_ref, bf16[3072,768]{1,0:T(8,128)(2,1)} %get-tuple-element.83.w_ref, f32[768,768]{1,0:T(8,128)} %get-tuple-element.66.late_ref, f32[1,768]{1,0:T(1,128)} %get-tuple-element.126.rows_ref), custom_call_target="tpu_custom_call" | custom-call | flops 3623878656 | bytes 9437184 | tf_op jit(solution)/shard_map/output_end/pallas_call | solution.py:835
  285.1 2.0 collective-permute-start.14
  290.8 5.3 %collective-permute-done.15 = bf16[48,1280]{1,0:T(8,128)(2,1)S(1)} collective-permute-done((bf16[48,1280]{1,0:T(8,128)(2,1)S(1)}, bf16[48,1280]{1,0:T(8,128)(2,1)S(1)}, u32[]{:S(2)}, u32[]{:S(2)}) %collective-permute-start.15) | collective-permute-done | bytes 122912 | tf_op jit(solution)/shard_map/ppermute | solution.py:907
  299.7 3.7 %collective-permute-done.17.theirs_ref = bf16[48,1280]{1,0:T(8,128)(2,1)S(1)} collective-permute-done((bf16[48,1280]{1,0:T(8,128)(2,1)S(1)}, bf16[48,1280]{1,0:T(8,128)(2,1)S(1)}, u32[]{:S(2)}, u32[]{:S(2)}) %collective-permute-start.17) | collective-permute-done | bytes 122912 | tf_op jit(solution)/shard_map/ppermute | solution.py:907
  304.0 2.5 finish.1
  307.3 2.0 join_second.1
  (117 shorter events, 41.8 us)
Async XLA Ops:
  7.3 8.4 %copy-start.1 = (bf16[1,750,768]{2,1,0:T(8,128)(2,1)S(1)}, bf16[1,750,768]{2,1,0:T(8,128)(2,1)}, u32[]{:S(2)}) copy-start(bf16[1,750,768]{2,1,0:T(8,128)(2,1)} %x_ref.3) | copy-start | bytes 3456004
  7.3 96.7 %all-gather.2.cloned.1.call-start = ((), (), s32[]{:S(2)}) async-start(), calls=%async_computation.1 | async-start | bytes 11280384 | tf_op jit(solution)/shard_map/all_gather | solution.py:1000
  9.5 280.2 %reduce-scatter.2.cloned.1.call-start = ((), (), s32[]{:S(2)}) async-start(), calls=%async_computation.2 | async-start | bytes 6266880 | tf_op jit(solution)/shard_map/reduce_scatter | solution.py:1039
  10.0 33.8 %copy-start = (s32[16]{0:T(128)S(1)}, s32[16]{0:T(128)}, u32[]{:S(2)}) copy-start(s32[16]{0:T(128)} %constant.112.clone) | copy-start | bytes 196
  10.0 8.1 %collective-permute-start = (bf16[48,1280]{1,0:T(8,128)(2,1)S(1)}, bf16[48,1280]{1,0:T(8,128)(2,1)S(1)}, u32[]{:S(2)}, u32[]{:S(2)}) collective-permute-start(bf16[48,1280]{1,0:T(8,128)(2,1)S(1)} %get-tuple-element.124), channel_id=1, source_target_pairs={{0,8},{2,10},{4,12},{6,14},{8,0},{10,2},{12,4},{14,6},{16,24},{18,... | collective-permute-start | bytes 368648 | tf_op jit(solution)/shard_map/ppermute | solution.py:907
  13.1 12.3 %collective-permute-start.1 = (bf16[48,1280]{1,0:T(8,128)(2,1)S(1)}, bf16[48,1280]{1,0:T(8,128)(2,1)S(1)}, u32[]{:S(2)}, u32[]{:S(2)}) collective-permute-start(bf16[48,1280]{1,0:T(8,128)(2,1)S(1)} %get-tuple-element.124), channel_id=1, source_target_pairs={{0,16},{2,18},{4,20},{6,22},{8,24},{10,26},{12,28},{14,30},{16,0},... | collective-permute-start | bytes 368648 | tf_op jit(solution)/shard_map/ppermute | solution.py:907
  15.7 9.7 %collective-permute-start.2 = (bf16[48,1280]{1,0:T(8,128)(2,1)S(1)}, bf16[48,1280]{1,0:T(8,128)(2,1)S(1)}, u32[]{:S(2)}, u32[]{:S(2)}) collective-permute-start(bf16[48,1280]{1,0:T(8,128)(2,1)S(1)} %get-tuple-element.124), channel_id=1, source_target_pairs={{0,24},{2,26},{4,28},{6,30},{8,16},{10,18},{12,20},{14,22},{16,8},... | collective-permute-start | bytes 368648 | tf_op jit(solution)/shard_map/ppermute | solution.py:907
  15.7 32.7 %collective-permute-start.5 = (bf16[1,750,768]{2,1,0:T(8,128)(2,1)S(1)}, bf16[1,750,768]{2,1,0:T(8,128)(2,1)S(1)}, u32[]{:S(2)}, u32[]{:S(2)}) collective-permute-start(bf16[1,750,768]{2,1,0:T(8,128)(2,1)S(1)} %copy-done.1), channel_id=1, source_target_pairs={{0,1},{1,0},{2,3},{3,2},{4,5},{5,4},{6,7},{7,6},{8,9},{9,8},{10,11... | collective-permute-start | bytes 3456008 | tf_op jit(solution)/shard_map/ppermute | solution.py:907
  25.5 16.1 %collective-permute-start.3 = (bf16[4,48,1280]{2,1,0:T(8,128)(2,1)S(1)}, bf16[4,48,1280]{2,1,0:T(8,128)(2,1)S(1)}, u32[]{:S(2)}, u32[]{:S(2)}) collective-permute-start(bf16[4,48,1280]{2,1,0:T(8,128)(2,1)S(1)} %pad_maximum_fusion), channel_id=1, source_target_pairs={{0,4},{2,6},{4,0},{6,2},{8,12},{10,14},{12,8},{14,10},{16,20},{18,... | collective-permute-start | bytes 1474568 | tf_op jit(solution)/shard_map/ppermute | solution.py:907
  43.7 9.1 %collective-permute-start.4 = (bf16[8,48,1280]{2,1,0:T(8,128)(2,1)}, bf16[8,48,1280]{2,1,0:T(8,128)(2,1)S(1)}, u32[]{:S(2)}, u32[]{:S(2)}) collective-permute-start(bf16[8,48,1280]{2,1,0:T(8,128)(2,1)} %get-tuple-element.110), channel_id=1, source_target_pairs={{0,2},{2,0},{4,6},{6,4},{8,10},{10,8},{12,14},{14,12},{16,18},{18,... | collective-permute-start | bytes 2949128 | tf_op jit(solution)/shard_map/ppermute | solution.py:907
  84.1 16.0 %collective-permute-start.6 = (bf16[768,384]{1,0:T(8,128)(2,1)}, bf16[768,384]{1,0:T(8,128)(2,1)S(1)}, u32[]{:S(2)}, u32[]{:S(2)}) collective-permute-start(bf16[768,384]{1,0:T(8,128)(2,1)} %get-tuple-element.61.o_sent_ref), channel_id=1, source_target_pairs={{0,1},{1,0},{2,3},{3,2},{4,5},{5,4},{6,7},{7,6},{8,9},{9,8},{10,11... | collective-permute-start | bytes 1769480 | tf_op jit(solution)/shard_map/ppermute | solution.py:907
  150.6 12.7 %collective-permute-start.7 = (bf16[8,192,768]{2,1,0:T(8,128)(2,1)}, bf16[8,192,768]{2,1,0:T(8,128)(2,1)}, u32[]{:S(2)}, u32[]{:S(2)}) collective-permute-start(bf16[8,192,768]{2,1,0:T(8,128)(2,1)} %get-tuple-element.69.token_ref), channel_id=1, source_target_pairs={{0,2},{2,0},{4,6},{6,4},{8,10},{10,8},{12,14},{14,12},{16,18},{18,... | collective-permute-start | bytes 7077896 | tf_op jit(solution)/shard_map/ppermute | solution.py:907
  161.8 16.6 %collective-permute-start.8 = (bf16[768,384]{1,0:T(8,128)(2,1)}, bf16[768,384]{1,0:T(8,128)(2,1)}, u32[]{:S(2)}, u32[]{:S(2)}) collective-permute-start(bf16[768,384]{1,0:T(8,128)(2,1)} %get-tuple-element.67.token_ref), channel_id=1, source_target_pairs={{0,1},{1,0},{2,3},{3,2},{4,5},{5,4},{6,7},{7,6},{8,9},{9,8},{10,11... | collective-permute-start | bytes 1769480 | tf_op jit(solution)/shard_map/ppermute | solution.py:907
  165.9 12.5 %copy-start.5 = (bf16[8,96,768]{2,1,0:T(8,128)(2,1)}, bf16[8,96,768]{2,1,0:T(8,128)(2,1)S(1)}, u32[]{:S(2)}) copy-start(bf16[8,96,768]{2,1,0:T(8,128)(2,1)S(1)} %get-tuple-element.101.token_ref) | copy-start | bytes 3538948
  165.9 59.8 %collective-permute-start.9 = (bf16[8,96,768]{2,1,0:T(8,128)(2,1)S(1)}, bf16[8,96,768]{2,1,0:T(8,128)(2,1)S(1)}, u32[]{:S(2)}, u32[]{:S(2)}) collective-permute-start(bf16[8,96,768]{2,1,0:T(8,128)(2,1)S(1)} %get-tuple-element.101.token_ref), channel_id=1, source_target_pairs={{0,1},{1,0},{2,3},{3,2},{4,5},{5,4},{6,7},{7,6},{8,9},{9,8},{10,11... | collective-permute-start | bytes 3538952 | tf_op jit(solution)/shard_map/ppermute | solution.py:907
  239.6 2.8 collective-permute-start.11
  239.6 28.7 %collective-permute-start.12 = (bf16[768,768]{1,0:T(8,128)(2,1)}, bf16[768,768]{1,0:T(8,128)(2,1)}, u32[]{:S(2)}, u32[]{:S(2)}) collective-permute-start(bf16[768,768]{1,0:T(8,128)(2,1)} %projection_input_gradient.2), channel_id=1, source_target_pairs={{0,1},{1,0},{2,3},{3,2},{4,5},{5,4},{6,7},{7,6},{8,9},{9,8},{10,11... | collective-permute-start | bytes 3538952 | tf_op jit(solution)/shard_map/ppermute | solution.py:907
  241.0 16.4 %collective-permute-start.10 = (bf16[4,96,768]{2,1,0:T(8,128)(2,1)}, bf16[4,96,768]{2,1,0:T(8,128)(2,1)S(1)}, u32[]{:S(2)}, u32[]{:S(2)}) collective-permute-start(bf16[4,96,768]{2,1,0:T(8,128)(2,1)} %get-tuple-element.105.token_ref), channel_id=1, source_target_pairs={{0,4},{2,6},{4,0},{6,2},{8,12},{10,14},{12,8},{14,10},{16,20},{18,... | collective-permute-start | bytes 1769480 | tf_op jit(solution)/shard_map/ppermute | solution.py:907
  242.3 15.1 %copy-start.4 = (bf16[4,96,768]{2,1,0:T(8,128)(2,1)S(1)}, bf16[4,96,768]{2,1,0:T(8,128)(2,1)}, u32[]{:S(2)}) copy-start(bf16[4,96,768]{2,1,0:T(8,128)(2,1)} %get-tuple-element.81) | copy-start | bytes 1769476
  244.7 36.8 %collective-permute-start.13 = (bf16[4,48,1280]{2,1,0:T(8,128)(2,1)}, bf16[4,48,1280]{2,1,0:T(8,128)(2,1)}, u32[]{:S(2)}, u32[]{:S(2)}) collective-permute-start(bf16[4,48,1280]{2,1,0:T(8,128)(2,1)} %fusion.11), channel_id=1, source_target_pairs={{0,4},{2,6},{4,0},{6,2},{8,12},{10,14},{12,8},{14,10},{16,20},{18,... | collective-permute-start | bytes 1474568 | tf_op jit(solution)/shard_map/ppermute | solution.py:907
  258.3 4.4 %copy-start.8 = (bf16[96,768]{1,0:T(8,128)(2,1)}, bf16[96,768]{1,0:T(8,128)(2,1)S(1)}, u32[]{:S(2)}) copy-start(bf16[96,768]{1,0:T(8,128)(2,1)S(1)} %get-tuple-element.104.token_ref) | copy-start | bytes 442372
  258.3 26.8 %collective-permute-start.21 = (bf16[96,768]{1,0:T(8,128)(2,1)S(1)}, bf16[96,768]{1,0:T(8,128)(2,1)S(1)}, u32[]{:S(2)}, u32[]{:S(2)}) collective-permute-start(bf16[96,768]{1,0:T(8,128)(2,1)S(1)} %get-tuple-element.104.token_ref), channel_id=1, source_target_pairs={{0,24},{2,26},{4,28},{6,30},{8,16},{10,18},{12,20},{14,22},{16,8},... | collective-permute-start | bytes 442376 | tf_op jit(solution)/shard_map/ppermute | solution.py:907
  259.6 27.5 %collective-permute-start.20 = (bf16[96,768]{1,0:T(8,128)(2,1)}, bf16[96,768]{1,0:T(8,128)(2,1)}, u32[]{:S(2)}, u32[]{:S(2)}) collective-permute-start(bf16[96,768]{1,0:T(8,128)(2,1)} %get-tuple-element.103), channel_id=1, source_target_pairs={{0,16},{2,18},{4,20},{6,22},{8,24},{10,26},{12,28},{14,30},{16,0},... | collective-permute-start | bytes 442376 | tf_op jit(solution)/shard_map/ppermute | solution.py:907
  260.9 26.2 %collective-permute-start.19 = (bf16[96,768]{1,0:T(8,128)(2,1)}, bf16[96,768]{1,0:T(8,128)(2,1)}, u32[]{:S(2)}, u32[]{:S(2)}) collective-permute-start(bf16[96,768]{1,0:T(8,128)(2,1)} %get-tuple-element.102), channel_id=1, source_target_pairs={{0,8},{2,10},{4,12},{6,14},{8,0},{10,2},{12,4},{14,6},{16,24},{18,... | collective-permute-start | bytes 442376 | tf_op jit(solution)/shard_map/ppermute | solution.py:907
  282.6 5.6 %copy-start.2 = (f32[4,48,1280]{2,1,0:T(8,128)}, f32[4,48,1280]{2,1,0:T(8,128)S(1)}, u32[]{:S(2)}) copy-start(f32[4,48,1280]{2,1,0:T(8,128)S(1)} %bitcast_add_fusion) | copy-start | bytes 2949124
  282.7 8.1 %collective-permute-start.16 = (bf16[48,1280]{1,0:T(8,128)(2,1)S(1)}, bf16[48,1280]{1,0:T(8,128)(2,1)S(1)}, u32[]{:S(2)}, u32[]{:S(2)}) collective-permute-start(bf16[48,1280]{1,0:T(8,128)(2,1)S(1)} %get-tuple-element.108), channel_id=1, source_target_pairs={{0,24},{2,26},{4,28},{6,30},{8,16},{10,18},{12,20},{14,22},{16,8},... | collective-permute-start | bytes 368648 | tf_op jit(solution)/shard_map/ppermute | solution.py:907
  284.1 12.0 %collective-permute-start.15 = (bf16[48,1280]{1,0:T(8,128)(2,1)S(1)}, bf16[48,1280]{1,0:T(8,128)(2,1)S(1)}, u32[]{:S(2)}, u32[]{:S(2)}) collective-permute-start(bf16[48,1280]{1,0:T(8,128)(2,1)S(1)} %get-tuple-element.109), channel_id=1, source_target_pairs={{0,16},{2,18},{4,20},{6,22},{8,24},{10,26},{12,28},{14,30},{16,0},... | collective-permute-start | bytes 368648 | tf_op jit(solution)/shard_map/ppermute | solution.py:907
  285.1 11.0 %collective-permute-start.14 = (bf16[48,1280]{1,0:T(8,128)(2,1)S(1)}, bf16[48,1280]{1,0:T(8,128)(2,1)S(1)}, u32[]{:S(2)}, u32[]{:S(2)}) collective-permute-start(bf16[48,1280]{1,0:T(8,128)(2,1)S(1)} %get-tuple-element.107), channel_id=1, source_target_pairs={{0,8},{2,10},{4,12},{6,14},{8,0},{10,2},{12,4},{14,6},{16,24},{18,... | collective-permute-start | bytes 368648 | tf_op jit(solution)/shard_map/ppermute | solution.py:907
  288.2 10.6 %collective-permute-start.22 = (bf16[96,768]{1,0:T(8,128)(2,1)S(1)}, bf16[96,768]{1,0:T(8,128)(2,1)S(1)}, u32[]{:S(2)}, u32[]{:S(2)}) collective-permute-start(bf16[96,768]{1,0:T(8,128)(2,1)S(1)} %fusion.15), channel_id=1, source_target_pairs={{0,1},{1,0},{2,3},{3,2},{4,5},{5,4},{6,7},{7,6},{8,9},{9,8},{10,11... | collective-permute-start | bytes 442376 | tf_op jit(solution)/shard_map/ppermute | solution.py:907
  289.7 16.8 %collective-permute-start.18 = (bf16[48,3840]{1,0:T(8,128)(2,1)}, bf16[48,3840]{1,0:T(8,128)(2,1)S(1)}, u32[]{:S(2)}, u32[]{:S(2)}) collective-permute-start(bf16[48,3840]{1,0:T(8,128)(2,1)} %reduce-scatter.2.cloned.1.call-done.mine_ref), channel_id=1, source_target_pairs={{0,1},{1,0},{2,3},{3,2},{4,5},{5,4},{6,7},{7,6},{8,9},{9,8},{10,11... | collective-permute-start | bytes 1105928 | tf_op jit(solution)/shard_map/ppermute | solution.py:907
  297.1 6.3 %copy-start.9 = (bf16[48,1280]{1,0:T(8,128)(2,1)}, bf16[48,1280]{1,0:T(8,128)(2,1)S(1)}, u32[]{:S(2)}) copy-start(bf16[48,1280]{1,0:T(8,128)(2,1)S(1)} %fusion.18.mine_ref) | copy-start | bytes 368644
  297.1 6.3 %collective-permute-start.17 = (bf16[48,1280]{1,0:T(8,128)(2,1)S(1)}, bf16[48,1280]{1,0:T(8,128)(2,1)S(1)}, u32[]{:S(2)}, u32[]{:S(2)}) collective-permute-start(bf16[48,1280]{1,0:T(8,128)(2,1)S(1)} %fusion.18.mine_ref), channel_id=1, source_target_pairs={{0,1},{1,0},{2,3},{3,2},{4,5},{5,4},{6,7},{7,6},{8,9},{9,8},{10,11... | collective-permute-start | bytes 368648 | tf_op jit(solution)/shard_map/ppermute | solution.py:907
  (15 other events, 30.8 us)
Sparse Core Ops, SparseCore 0:
  10.4 93.6 all-gather.1
  161.9 83.4 reduce-scatter.1

commit v6 on v4

--- a/solution.py
+++ b/solution.py
@@ -809,18 +809,24 @@
     )(here, mine, theirs)
 
 
-def output_kernel(token_ref, z_ref, w_ref, residual_ref, rows_ref, out_ref, total_ref):
+def output_kernel(
+    token_ref, z_ref, w_ref, late_ref, rows_ref, out_ref, total_ref, residual_ref, sem_ref
+):
     step = pl.program_id(0)
+    copy = pltpu.make_async_copy(late_ref, residual_ref, sem_ref)
 
     @pl.when(step == 0)
     def _():
-        total_ref[...] = residual_ref[...] + rows_ref[-1:, :]
+        copy.start()
+        total_ref[...] = jnp.zeros_like(total_ref)
 
     total_ref[...] += dot(z_ref[...], w_ref[...])
 
     @pl.when(step == pl.num_programs(0) - 1)
     def _():
-        out_ref[0] = total_ref[: out_ref.shape[1], :].astype(BF)
+        copy.wait()
+        total = total_ref[...] + residual_ref[...] + rows_ref[-1:, :]
+        out_ref[0] = total[: out_ref.shape[1], :].astype(BF)
 
 
 def output_end(token, activated, w, residual, bias, valid):
@@ -833,12 +839,16 @@
             pl.BlockSpec(memory_space=pl.ANY),
             pl.BlockSpec((rows, wide), lambda i: (0, i)),
             pl.BlockSpec((wide, wide), lambda i: (i, 0)),
-            pl.BlockSpec((rows, wide), lambda i: (0, 0)),
+            pl.BlockSpec(memory_space=pl.ANY),
             pl.BlockSpec((1, wide), lambda i: (0, 0)),
         ],
         out_specs=pl.BlockSpec((1, valid, wide), lambda i: (0, 0, 0)),
         out_shape=jax.ShapeDtypeStruct((1, valid, wide), BF),
-        scratch_shapes=[pltpu.VMEM((rows, wide), F32)],
+        scratch_shapes=[
+            pltpu.VMEM((rows, wide), F32),
+            pltpu.VMEM((rows, wide), F32),
+            pltpu.SemaphoreType.DMA,
+        ],
         cost_estimate=pl.CostEstimate(
             flops=2 * rows * wide * ff, bytes_accessed=rows * ff * 4, transcendentals=0
         ),

time: 314 us -> 314 us (level)
  transfers between devices with their start and end apart: 25 -> 25, of which waited for: 10 -> 10; matrix products, arithmetic and copies ran while one was open for 6% -> 6% of each run, Pallas kernels for 41% -> 40%
where the time goes in v6:
time: 314 us; the launch traced here: 313 us
  Pallas kernels  164 us (52%)
  waiting for transfers between devices  70.6 us (22%)
  starting transfers between devices  28.4 us (9%)
  between operations  14.4 us (5%)
  local copies, waits for them, and re-layouts  13.9 us (4%)
  matrix products  10.9 us (3%)
  other arithmetic  10.1 us (3%)
    ppermute x23, waiting for transfers between devices, swap(): return lax.ppermute(x, axis, [(i, i ^ bit) for i in range(size)])  66.7 us
    pallas_call x1, Pallas kernels, attention_backward(): pl.pallas_call(functools.partial(backward_kernel, half, valid), grid=(cou...  42.8 us
    ppermute x23, starting transfers between devices, swap(): return lax.ppermute(x, axis, [(i, i ^ bit) for i in range(size)])  28.3 us
    pallas_call x1, Pallas kernels, attention_forward(): pl.pallas_call(functools.partial(forward_kernel, half, valid), grid=(pair...  20.7 us
    pallas_call x1, Pallas kernels, feed_back(): pl.pallas_call(functools.partial(feed_back_kernel, part), grid_spec=pltpu...  20.1 us
    pallas_call x1, Pallas kernels, spread_weight_gradient(): pl.pallas_call(functools.partial(spread_kernel, part, len(ds), bias.shape...  12.5 us
    dot_general x1, matrix products, dot(): lax.dot_general(a, b, (((ca,), (cb,)), ((), ())), preferred_element_type=...  10.9 us
    pallas_call x1, Pallas kernels, second_gradient(): pl.pallas_call(second_kernel, grid_spec=pltpu.PrefetchScalarGridSpec(num_...  10.2 us
  transfers between devices with their start and end apart: 25, of which 10 were waited for; matrix products, arithmetic and copies ran while one was open for 6% of the time, Pallas kernels for 40%

profile of v6, /device:TPU:0, one launch (start us, length us, event | category | flops | bytes accessed | tf_op | source)
XLA Modules:
  0.0 312.7 jit_solution(1747365745296513390)
XLA Ops:
  7.3 2.1 pack.1
  10.0 3.1 collective-permute-start
  13.1 2.6 collective-permute-start.1
  18.1 7.3 %collective-permute-done.1 = bf16[48,1280]{1,0:T(8,128)(2,1)S(1)} collective-permute-done((bf16[48,1280]{1,0:T(8,128)(2,1)S(1)}, bf16[48,1280]{1,0:T(8,128)(2,1)S(1)}, u32[]{:S(2)}, u32[]{:S(2)}) %collective-permute-start.1) | collective-permute-done | bytes 122912 | tf_op jit(solution)/shard_map/ppermute | solution.py:907
  29.1 12.5 %collective-permute-done.3 = bf16[4,48,1280]{2,1,0:T(8,128)(2,1)S(1)} collective-permute-done((bf16[4,48,1280]{2,1,0:T(8,128)(2,1)S(1)}, bf16[4,48,1280]{2,1,0:T(8,128)(2,1)S(1)}, u32[]{:S(2)}, u32[]{:S(2)}) %collective-permute-start.3) | collective-permute-done | bytes 491552 | tf_op jit(solution)/shard_map/ppermute | solution.py:907
  44.4 3.5 %prepare.2 = (f32[1536,768]{1,0:T(8,128)}, bf16[784,1536]{1,0:T(8,128)(2,1)}, f32[768,128]{1,0:T(8,128)}) custom-call(bf16[1,750,768]{2,1,0:T(8,128)(2,1)} %x_ref.3), custom_call_target="tpu_custom_call" | custom-call | flops 9437184 | bytes 4718592 | tf_op jit(solution)/shard_map/prepare/pallas_call | solution.py:209
  49.5 3.4 %prepare.3 = (f32[1536,768]{1,0:T(8,128)}, bf16[784,1536]{1,0:T(8,128)(2,1)}, f32[768,128]{1,0:T(8,128)}) custom-call(bf16[1,750,768]{2,1,0:T(8,128)(2,1)} %copy-done.6, f32[1536,768]{1,0:T(8,128)} %get-tuple-element.56.refs_0_, bf16[784,1536]{1,0:T(8,128)(2,1)} %get-tuple-element.57.refs_1_), custom_call_target="tpu_custom_call", output_to_operand_aliasing={{0}: (1, {}), {1}: (2, {})} | custom-call | flops 9437184 | bytes 4718592 | tf_op jit(solution)/shard_map/prepare/pallas_call | solution.py:209
  53.9 9.5 %projection.1 = (bf16[1536,1152]{1,0:T(8,128)(2,1)}, bf16[768,1152]{1,0:T(8,128)(2,1)}, bf16[1152,768]{1,0:T(8,128)(2,1)}, f32[16,768]{1,0:T(8,128)}, f32[768,256]{1,0:T(8,128)}) custom-call(s32[17]{0:T(128)} %pad_add_fusion.place_ref, bf16[16,48,1280]{2,1,0:T(8,128)(2,1)} %constant_dynamic-update-slice_fusion.5.held_ref, ...), custom_call_target="tpu_custom_call" | custom-call | flops 2717908992 | bytes 9437184 | tf_op jit(solution)/shard_map/projection/pallas_call | solution.py:324
  63.4 20.7 %attention_forward.1 = (bf16[768,384]{1,0:T(8,128)(2,1)}, bf16[768,384]{1,0:T(8,128)(2,1)}, f32[3,8,1536]{2,1,0:T(8,128)}) custom-call(bf16[1536,1152]{1,0:T(8,128)(2,1)} %get-tuple-element.59.q_ref.k_ref.v_ref, bf16[1536,1152]{1,0:T(8,128)(2,1)} %get-tuple-element.59.q_ref.k_ref.v_ref, bf16[1536,1152]{1,0:T(8,128)(2,1)} %get-tuple-element.59.q_ref.k_ref.v_ref), custom_call_target="tpu_custom_call" | custom-call | flops 14495514624 | bytes 5308416 | tf_op jit(solution)/shard_map/attention_forward/pallas_call | solution.py:68
  88.2 11.9 %collective-permute-done.6.got_ref = bf16[768,384]{1,0:T(8,128)(2,1)S(1)} collective-permute-done((bf16[768,384]{1,0:T(8,128)(2,1)}, bf16[768,384]{1,0:T(8,128)(2,1)S(1)}, u32[]{:S(2)}, u32[]{:S(2)}) %collective-permute-start.6) | collective-permute-done | bytes 589856 | tf_op jit(solution)/shard_map/ppermute | solution.py:907
  100.2 3.9 %all-gather.2.cloned.1.call-done.w_ref.fc2_ref.fc1_ref.late_out_ref = bf16[768,6912]{1,0:T(8,128)(2,1)} async-done(((bf16[48,6912]{1,0:T(8,128)(2,1)}), bf16[768,6912]{1,0:T(8,128)(2,1)}) %all-gather.2.cloned.1.call-update) | async-done | bytes 10616848 | tf_op jit(solution)/shard_map/all_gather | solution.py:1000
  104.0 5.3 %attend.1 = (f32[768,768]{1,0:T(8,128)}, bf16[768,768]{1,0:T(8,128)(2,1)}) custom-call(s32[1]{0:T(128)} %bitcast.1.place_ref, bf16[1,750,768]{2,1,0:T(8,128)(2,1)} %x_ref.3, bf16[768,384]{1,0:T(8,128)(2,1)} %get-tuple-element.60.mine_ref.o_mine_ref, bf16[768,384]{1,0:T(8,128)(2,1)} %copy-done.7, ...), custom_call_target="tpu_custom_call" | custom-call | flops 905969664 | bytes 5898240 | tf_op jit(solution)/shard_map/attend/pallas_call | solution.py:253
  109.3 10.9 %fusion.4 = (bf16[768,3072]{1,0:T(8,128)(2,1)}, bf16[768,3072]{1,0:T(8,128)(2,1)}) fusion(f32[3072]{0:T(1024)S(1)} %add.122, bf16[768,768]{1,0:T(8,128)(2,1)} %get-tuple-element.63.h_ref, bf16[768,6912]{1,0:T(8,128)(2,1)} %all-gather.2.cloned.1.call-done.w_ref.fc2_ref.fc1_ref.late_out_ref), kind=kOutput, calls=%fused_computation.6 | convolution fusion | flops 3652190208 | bytes 15347712 | tf_op jit(solution)/shard_map/dot_general | solution.py:19
  120.2 20.1 %feed_back.1 = (bf16[768,3072]{1,0:T(8,128)(2,1)}, bf16[3072,768]{1,0:T(8,128)(2,1)}, bf16[768,768]{1,0:T(8,128)(2,1)}, bf16[768,384]{1,0:T(8,128)(2,1)}, bf16[7...) custom-call(s32[1]{0:T(128)} %bitcast.1.place_ref, ...), custom_call_target="tpu_custom_call" | custom-call | flops 7247757312 | bytes 23592960 | tf_op jit(solution)/shard_map/feed_back/pallas_call | solution.py:737
  140.3 8.3 %third_gradient.1 = (bf16[8,192,768]{2,1,0:T(8,128)(2,1)}, bf16[8,192,768]{2,1,0:T(8,128)(2,1)}) custom-call(s32[1]{0:T(128)} %bitcast.place_ref, bf16[768,3072]{1,0:T(8,128)(2,1)} %get-tuple-element.64.z_ref, bf16[1,750,768]{2,1,0:T(8,128)(2,1)} %cot_ref.3, bf16[768,384]{1,0:T(8,128)(2,1)} %get-tuple-element.67.token_ref), custom_call_target="tpu_custom_call" | custom-call | flops 3623878656 | bytes 9437184 | tf_op jit(solution)/shard_map/third_gradient/pallas_call | solution.py:629
  148.9 10.2 %second_gradient.1 = bf16[768,3840]{1,0:T(8,128)(2,1)} custom-call(s32[1]{0:T(128)} %bitcast.1.place_ref, bf16[8,192,768]{2,1,0:T(8,128)(2,1)} %get-tuple-element.69.token_ref, bf16[768,384]{1,0:T(8,128)(2,1)} %get-tuple-element.60.mine_ref.o_mine_ref, bf16[768,384]{1,0:T(8,128)(2,1)} %copy-done.7, bf16[768,768]{1,0:T(8,128)(2,1)} %get-tuple-element.84.residual_ref.drb_ref, ...), custom_call_target="tpu_custom_call" | custom-call | flops 4529848320 | bytes 9437184 | tf_op jit(solution)/shard_map/second_gradient/pallas_call | solution.py:559
  161.2 2.2 convert_add_fusion
  164.7 11.0 %collective-permute-done.8.got_ref = bf16[768,384]{1,0:T(8,128)(2,1)} collective-permute-done((bf16[768,384]{1,0:T(8,128)(2,1)}, bf16[768,384]{1,0:T(8,128)(2,1)}, u32[]{:S(2)}, u32[]{:S(2)}) %collective-permute-start.8) | collective-permute-done | bytes 589856 | tf_op jit(solution)/shard_map/ppermute | solution.py:907
  175.7 42.8 %attention_backward.1.token_ref.refs_0_ = bf16[3,1536,384]{2,1,0:T(8,128)(2,1)} custom-call(bf16[1536,1152]{1,0:T(8,128)(2,1)} %get-tuple-element.59.q_ref.k_ref.v_ref, bf16[1536,1152]{1,0:T(8,128)(2,1)} %get-tuple-element.59.q_ref.k_ref.v_ref, bf16[1536,1152]{1,0:T(8,128)(2,1)} %get-tuple-element.59.q_ref.k_ref.v_ref, ...), custom_call_target="tpu_custom_call" | custom-call | flops 28991029248 | bytes 9437184 | tf_op jit(solution)/shard_map/attention_backward/pallas_call | solution.py:162
  218.5 4.5 %projection_input_gradient.2 = bf16[768,768]{1,0:T(8,128)(2,1)} custom-call(bf16[3,1536,384]{2,1,0:T(8,128)(2,1)} %attention_backward.1.token_ref.refs_0_, bf16[1152,768]{1,0:T(8,128)(2,1)} %get-tuple-element.72.wt_ref, bf16[3,1536,384]{2,1,0:T(8,128)(2,1)} %attention_backward.1.token_ref.refs_0_), custom_call_target="tpu_custom_call" | custom-call | flops 1358954496 | bytes 3538944 | tf_op jit(solution)/shard_map/projection_input_gradient/pallas_call | solution.py:520
  224.3 12.5 %spread_weight_gradient.1 = (bf16[8,48,1280]{2,1,0:T(8,128)(2,1)}, bf16[8,48,1280]{2,1,0:T(8,128)(2,1)}) custom-call(s32[2]{0:T(128)} %pad_add_fusion.1.place_ref, bf16[4,96,768]{2,1,0:T(8,128)(2,1)} %get-tuple-element.105.token_ref, bf16[784,1536]{1,0:T(8,128)(2,1)} %get-tuple-element.74.xt_ref, bf16[768,1152]{1,0:T(8,128)(2,1)} %get-tuple-element.75.w_ref, ...), custom_call_target="tpu_custom_call" | custom-call | flops 2717908992 | bytes 4718592 | tf_op jit(solution)/shard_map/spread_weight_gradient/pallas_call | solution.py:481
  242.6 12.1 %collective-permute-done.10 = bf16[4,96,768]{2,1,0:T(8,128)(2,1)S(1)} collective-permute-done((bf16[4,96,768]{2,1,0:T(8,128)(2,1)}, bf16[4,96,768]{2,1,0:T(8,128)(2,1)S(1)}, u32[]{:S(2)}, u32[]{:S(2)}) %collective-permute-start.10) | collective-permute-done | bytes 589856 | tf_op jit(solution)/shard_map/ppermute | solution.py:907
  256.2 2.0 collective-permute-start.20
  260.0 4.5 %projection_input_gradient.3.mine_ref = bf16[768,768]{1,0:T(8,128)(2,1)} custom-call(bf16[96,768]{1,0:T(8,128)(2,1)} %copy-done.8, bf16[1152,768]{1,0:T(8,128)(2,1)} %get-tuple-element.72.wt_ref, bf16[3,1536,384]{2,1,0:T(8,128)(2,1)} %attention_backward.1.token_ref.refs_0_), custom_call_target="tpu_custom_call" | custom-call | flops 1358954496 | bytes 3538944 | tf_op jit(solution)/shard_map/projection_input_gradient/pallas_call | solution.py:520
  265.5 5.1 %input_end.1 = f32[750,1,768]{2,1,0:T(1,128)} custom-call(bf16[768,768]{1,0:T(8,128)(2,1)} %projection_input_gradient.3.mine_ref, bf16[768,768]{1,0:T(8,128)(2,1)} %collective-permute-done.12.got_ref, bf16[768,768]{1,0:T(8,128)(2,1)} %get-tuple-element.84.residual_ref.drb_ref, f32[1536,768]{1,0:T(8,128)} %get-tuple-element.58.x_ref.normed_ref, ...), custom_call_target="tpu_custom_call" | custom-call | flops 5898240 | bytes 10616832 | tf_op jit(solution)/shard_map/input_end/pallas_call | solution.py:890
  270.7 8.1 %output_end.1 = bf16[1,750,768]{2,1,0:T(8,128)(2,1)} custom-call(bf16[96,768]{1,0:T(8,128)(2,1)} %copy-done.8, bf16[768,3072]{1,0:T(8,128)(2,1)} %get-tuple-element.64.z_ref, bf16[3072,768]{1,0:T(8,128)(2,1)} %get-tuple-element.83.w_ref, f32[768,768]{1,0:T(8,128)} %get-tuple-element.66.late_ref, f32[1,768]{1,0:T(1,128)} %get-tuple-element.126.rows_ref), custom_call_target="tpu_custom_call" | custom-call | flops 3623878656 | bytes 9437184 | tf_op jit(solution)/shard_map/output_end/pallas_call | solution.py:835
  280.6 1.9 collective-permute-start.15
  282.5 2.0 collective-permute-start.16
  287.6 4.9 %collective-permute-done.15 = bf16[48,1280]{1,0:T(8,128)(2,1)S(1)} collective-permute-done((bf16[48,1280]{1,0:T(8,128)(2,1)S(1)}, bf16[48,1280]{1,0:T(8,128)(2,1)S(1)}, u32[]{:S(2)}, u32[]{:S(2)}) %collective-permute-start.15) | collective-permute-done | bytes 122912 | tf_op jit(solution)/shard_map/ppermute | solution.py:907
  295.8 4.8 %collective-permute-done.17.theirs_ref = bf16[48,1280]{1,0:T(8,128)(2,1)S(1)} collective-permute-done((bf16[48,1280]{1,0:T(8,128)(2,1)S(1)}, bf16[48,1280]{1,0:T(8,128)(2,1)S(1)}, u32[]{:S(2)}, u32[]{:S(2)}) %collective-permute-start.17) | collective-permute-done | bytes 122912 | tf_op jit(solution)/shard_map/ppermute | solution.py:907
  301.3 1.8 finish.1
  303.9 2.0 join_second.1
  (118 shorter events, 40.7 us)
Async XLA Ops:
  7.3 8.4 %copy-start.1 = (bf16[1,750,768]{2,1,0:T(8,128)(2,1)S(1)}, bf16[1,750,768]{2,1,0:T(8,128)(2,1)}, u32[]{:S(2)}) copy-start(bf16[1,750,768]{2,1,0:T(8,128)(2,1)} %x_ref.3) | copy-start | bytes 3456004
  7.3 96.7 %all-gather.2.cloned.1.call-start = ((), (), s32[]{:S(2)}) async-start(), calls=%async_computation.1 | async-start | bytes 11280384 | tf_op jit(solution)/shard_map/all_gather | solution.py:1000
  9.5 277.5 %reduce-scatter.2.cloned.1.call-start = ((), (), s32[]{:S(2)}) async-start(), calls=%async_computation.2 | async-start | bytes 6266880 | tf_op jit(solution)/shard_map/reduce_scatter | solution.py:1041
  10.0 33.8 %copy-start = (s32[16]{0:T(128)S(1)}, s32[16]{0:T(128)}, u32[]{:S(2)}) copy-start(s32[16]{0:T(128)} %constant.112.clone) | copy-start | bytes 196
  10.0 8.1 %collective-permute-start = (bf16[48,1280]{1,0:T(8,128)(2,1)S(1)}, bf16[48,1280]{1,0:T(8,128)(2,1)S(1)}, u32[]{:S(2)}, u32[]{:S(2)}) collective-permute-start(bf16[48,1280]{1,0:T(8,128)(2,1)S(1)} %get-tuple-element.124), channel_id=1, source_target_pairs={{0,8},{2,10},{4,12},{6,14},{8,0},{10,2},{12,4},{14,6},{16,24},{18,... | collective-permute-start | bytes 368648 | tf_op jit(solution)/shard_map/ppermute | solution.py:907
  13.1 12.3 %collective-permute-start.1 = (bf16[48,1280]{1,0:T(8,128)(2,1)S(1)}, bf16[48,1280]{1,0:T(8,128)(2,1)S(1)}, u32[]{:S(2)}, u32[]{:S(2)}) collective-permute-start(bf16[48,1280]{1,0:T(8,128)(2,1)S(1)} %get-tuple-element.124), channel_id=1, source_target_pairs={{0,16},{2,18},{4,20},{6,22},{8,24},{10,26},{12,28},{14,30},{16,0},... | collective-permute-start | bytes 368648 | tf_op jit(solution)/shard_map/ppermute | solution.py:907
  15.7 9.7 %collective-permute-start.2 = (bf16[48,1280]{1,0:T(8,128)(2,1)S(1)}, bf16[48,1280]{1,0:T(8,128)(2,1)S(1)}, u32[]{:S(2)}, u32[]{:S(2)}) collective-permute-start(bf16[48,1280]{1,0:T(8,128)(2,1)S(1)} %get-tuple-element.124), channel_id=1, source_target_pairs={{0,24},{2,26},{4,28},{6,30},{8,16},{10,18},{12,20},{14,22},{16,8},... | collective-permute-start | bytes 368648 | tf_op jit(solution)/shard_map/ppermute | solution.py:907
  15.7 32.7 %collective-permute-start.5 = (bf16[1,750,768]{2,1,0:T(8,128)(2,1)S(1)}, bf16[1,750,768]{2,1,0:T(8,128)(2,1)S(1)}, u32[]{:S(2)}, u32[]{:S(2)}) collective-permute-start(bf16[1,750,768]{2,1,0:T(8,128)(2,1)S(1)} %copy-done.1), channel_id=1, source_target_pairs={{0,1},{1,0},{2,3},{3,2},{4,5},{5,4},{6,7},{7,6},{8,9},{9,8},{10,11... | collective-permute-start | bytes 3456008 | tf_op jit(solution)/shard_map/ppermute | solution.py:907
  25.5 16.1 %collective-permute-start.3 = (bf16[4,48,1280]{2,1,0:T(8,128)(2,1)S(1)}, bf16[4,48,1280]{2,1,0:T(8,128)(2,1)S(1)}, u32[]{:S(2)}, u32[]{:S(2)}) collective-permute-start(bf16[4,48,1280]{2,1,0:T(8,128)(2,1)S(1)} %pad_maximum_fusion), channel_id=1, source_target_pairs={{0,4},{2,6},{4,0},{6,2},{8,12},{10,14},{12,8},{14,10},{16,20},{18,... | collective-permute-start | bytes 1474568 | tf_op jit(solution)/shard_map/ppermute | solution.py:907
  43.7 9.2 %collective-permute-start.4 = (bf16[8,48,1280]{2,1,0:T(8,128)(2,1)}, bf16[8,48,1280]{2,1,0:T(8,128)(2,1)S(1)}, u32[]{:S(2)}, u32[]{:S(2)}) collective-permute-start(bf16[8,48,1280]{2,1,0:T(8,128)(2,1)} %get-tuple-element.110), channel_id=1, source_target_pairs={{0,2},{2,0},{4,6},{6,4},{8,10},{10,8},{12,14},{14,12},{16,18},{18,... | collective-permute-start | bytes 2949128 | tf_op jit(solution)/shard_map/ppermute | solution.py:907
  84.2 16.0 %collective-permute-start.6 = (bf16[768,384]{1,0:T(8,128)(2,1)}, bf16[768,384]{1,0:T(8,128)(2,1)S(1)}, u32[]{:S(2)}, u32[]{:S(2)}) collective-permute-start(bf16[768,384]{1,0:T(8,128)(2,1)} %get-tuple-element.61.o_sent_ref), channel_id=1, source_target_pairs={{0,1},{1,0},{2,3},{3,2},{4,5},{5,4},{6,7},{7,6},{8,9},{9,8},{10,11... | collective-permute-start | bytes 1769480 | tf_op jit(solution)/shard_map/ppermute | solution.py:907
  148.6 12.6 %collective-permute-start.7 = (bf16[8,192,768]{2,1,0:T(8,128)(2,1)}, bf16[8,192,768]{2,1,0:T(8,128)(2,1)}, u32[]{:S(2)}, u32[]{:S(2)}) collective-permute-start(bf16[8,192,768]{2,1,0:T(8,128)(2,1)} %get-tuple-element.69.token_ref), channel_id=1, source_target_pairs={{0,2},{2,0},{4,6},{6,4},{8,10},{10,8},{12,14},{14,12},{16,18},{18,... | collective-permute-start | bytes 7077896 | tf_op jit(solution)/shard_map/ppermute | solution.py:907
  159.1 16.6 %collective-permute-start.8 = (bf16[768,384]{1,0:T(8,128)(2,1)}, bf16[768,384]{1,0:T(8,128)(2,1)}, u32[]{:S(2)}, u32[]{:S(2)}) collective-permute-start(bf16[768,384]{1,0:T(8,128)(2,1)} %get-tuple-element.67.token_ref), channel_id=1, source_target_pairs={{0,1},{1,0},{2,3},{3,2},{4,5},{5,4},{6,7},{7,6},{8,9},{9,8},{10,11... | collective-permute-start | bytes 1769480 | tf_op jit(solution)/shard_map/ppermute | solution.py:907
  163.7 12.0 %copy-start.5 = (bf16[8,96,768]{2,1,0:T(8,128)(2,1)}, bf16[8,96,768]{2,1,0:T(8,128)(2,1)S(1)}, u32[]{:S(2)}) copy-start(bf16[8,96,768]{2,1,0:T(8,128)(2,1)S(1)} %get-tuple-element.101.token_ref) | copy-start | bytes 3538948
  163.7 59.3 %collective-permute-start.9 = (bf16[8,96,768]{2,1,0:T(8,128)(2,1)S(1)}, bf16[8,96,768]{2,1,0:T(8,128)(2,1)S(1)}, u32[]{:S(2)}, u32[]{:S(2)}) collective-permute-start(bf16[8,96,768]{2,1,0:T(8,128)(2,1)S(1)} %get-tuple-element.101.token_ref), channel_id=1, source_target_pairs={{0,1},{1,0},{2,3},{3,2},{4,5},{5,4},{6,7},{7,6},{8,9},{9,8},{10,11... | collective-permute-start | bytes 3538952 | tf_op jit(solution)/shard_map/ppermute | solution.py:907
  236.8 2.8 collective-permute-start.11
  236.8 28.7 %collective-permute-start.12 = (bf16[768,768]{1,0:T(8,128)(2,1)}, bf16[768,768]{1,0:T(8,128)(2,1)}, u32[]{:S(2)}, u32[]{:S(2)}) collective-permute-start(bf16[768,768]{1,0:T(8,128)(2,1)} %projection_input_gradient.2), channel_id=1, source_target_pairs={{0,1},{1,0},{2,3},{3,2},{4,5},{5,4},{6,7},{7,6},{8,9},{9,8},{10,11... | collective-permute-start | bytes 3538952 | tf_op jit(solution)/shard_map/ppermute | solution.py:907
  238.3 16.4 %collective-permute-start.10 = (bf16[4,96,768]{2,1,0:T(8,128)(2,1)}, bf16[4,96,768]{2,1,0:T(8,128)(2,1)S(1)}, u32[]{:S(2)}, u32[]{:S(2)}) collective-permute-start(bf16[4,96,768]{2,1,0:T(8,128)(2,1)} %get-tuple-element.105.token_ref), channel_id=1, source_target_pairs={{0,4},{2,6},{4,0},{6,2},{8,12},{10,14},{12,8},{14,10},{16,20},{18,... | collective-permute-start | bytes 1769480 | tf_op jit(solution)/shard_map/ppermute | solution.py:907
  239.6 15.1 %copy-start.4 = (bf16[4,96,768]{2,1,0:T(8,128)(2,1)S(1)}, bf16[4,96,768]{2,1,0:T(8,128)(2,1)}, u32[]{:S(2)}) copy-start(bf16[4,96,768]{2,1,0:T(8,128)(2,1)} %get-tuple-element.81) | copy-start | bytes 1769476
  241.9 36.8 %collective-permute-start.13 = (bf16[4,48,1280]{2,1,0:T(8,128)(2,1)}, bf16[4,48,1280]{2,1,0:T(8,128)(2,1)}, u32[]{:S(2)}, u32[]{:S(2)}) collective-permute-start(bf16[4,48,1280]{2,1,0:T(8,128)(2,1)} %fusion.11), channel_id=1, source_target_pairs={{0,4},{2,6},{4,0},{6,2},{8,12},{10,14},{12,8},{14,10},{16,20},{18,... | collective-permute-start | bytes 1474568 | tf_op jit(solution)/shard_map/ppermute | solution.py:907
  255.6 4.4 %copy-start.8 = (bf16[96,768]{1,0:T(8,128)(2,1)}, bf16[96,768]{1,0:T(8,128)(2,1)S(1)}, u32[]{:S(2)}) copy-start(bf16[96,768]{1,0:T(8,128)(2,1)S(1)} %get-tuple-element.104.token_ref) | copy-start | bytes 442372
  255.6 26.9 %collective-permute-start.19 = (bf16[96,768]{1,0:T(8,128)(2,1)}, bf16[96,768]{1,0:T(8,128)(2,1)S(1)}, u32[]{:S(2)}, u32[]{:S(2)}) collective-permute-start(bf16[96,768]{1,0:T(8,128)(2,1)} %get-tuple-element.102), channel_id=1, source_target_pairs={{0,8},{2,10},{4,12},{6,14},{8,0},{10,2},{12,4},{14,6},{16,24},{18,... | collective-permute-start | bytes 442376 | tf_op jit(solution)/shard_map/ppermute | solution.py:907
  256.2 28.2 %collective-permute-start.20 = (bf16[96,768]{1,0:T(8,128)(2,1)}, bf16[96,768]{1,0:T(8,128)(2,1)}, u32[]{:S(2)}, u32[]{:S(2)}) collective-permute-start(bf16[96,768]{1,0:T(8,128)(2,1)} %get-tuple-element.103), channel_id=1, source_target_pairs={{0,16},{2,18},{4,20},{6,22},{8,24},{10,26},{12,28},{14,30},{16,0},... | collective-permute-start | bytes 442376 | tf_op jit(solution)/shard_map/ppermute | solution.py:907
  258.2 26.2 %collective-permute-start.21 = (bf16[96,768]{1,0:T(8,128)(2,1)S(1)}, bf16[96,768]{1,0:T(8,128)(2,1)}, u32[]{:S(2)}, u32[]{:S(2)}) collective-permute-start(bf16[96,768]{1,0:T(8,128)(2,1)S(1)} %get-tuple-element.104.token_ref), channel_id=1, source_target_pairs={{0,24},{2,26},{4,28},{6,30},{8,16},{10,18},{12,20},{14,22},{16,8},... | collective-permute-start | bytes 442376 | tf_op jit(solution)/shard_map/ppermute | solution.py:907
  279.9 5.6 %copy-start.2 = (f32[4,48,1280]{2,1,0:T(8,128)}, f32[4,48,1280]{2,1,0:T(8,128)S(1)}, u32[]{:S(2)}) copy-start(f32[4,48,1280]{2,1,0:T(8,128)S(1)} %bitcast_add_fusion) | copy-start | bytes 2949124
  280.0 7.6 %collective-permute-start.14 = (bf16[48,1280]{1,0:T(8,128)(2,1)S(1)}, bf16[48,1280]{1,0:T(8,128)(2,1)S(1)}, u32[]{:S(2)}, u32[]{:S(2)}) collective-permute-start(bf16[48,1280]{1,0:T(8,128)(2,1)S(1)} %get-tuple-element.107), channel_id=1, source_target_pairs={{0,8},{2,10},{4,12},{6,14},{8,0},{10,2},{12,4},{14,6},{16,24},{18,... | collective-permute-start | bytes 368648 | tf_op jit(solution)/shard_map/ppermute | solution.py:907
  280.6 11.9 %collective-permute-start.15 = (bf16[48,1280]{1,0:T(8,128)(2,1)S(1)}, bf16[48,1280]{1,0:T(8,128)(2,1)S(1)}, u32[]{:S(2)}, u32[]{:S(2)}) collective-permute-start(bf16[48,1280]{1,0:T(8,128)(2,1)S(1)} %get-tuple-element.109), channel_id=1, source_target_pairs={{0,16},{2,18},{4,20},{6,22},{8,24},{10,26},{12,28},{14,30},{16,0},... | collective-permute-start | bytes 368648 | tf_op jit(solution)/shard_map/ppermute | solution.py:907
  282.5 10.0 %collective-permute-start.16 = (bf16[48,1280]{1,0:T(8,128)(2,1)S(1)}, bf16[48,1280]{1,0:T(8,128)(2,1)S(1)}, u32[]{:S(2)}, u32[]{:S(2)}) collective-permute-start(bf16[48,1280]{1,0:T(8,128)(2,1)S(1)} %get-tuple-element.108), channel_id=1, source_target_pairs={{0,24},{2,26},{4,28},{6,30},{8,16},{10,18},{12,20},{14,22},{16,8},... | collective-permute-start | bytes 368648 | tf_op jit(solution)/shard_map/ppermute | solution.py:907
  285.5 9.5 %collective-permute-start.22 = (bf16[96,768]{1,0:T(8,128)(2,1)S(1)}, bf16[96,768]{1,0:T(8,128)(2,1)S(1)}, u32[]{:S(2)}, u32[]{:S(2)}) collective-permute-start(bf16[96,768]{1,0:T(8,128)(2,1)S(1)} %fusion.15), channel_id=1, source_target_pairs={{0,1},{1,0},{2,3},{3,2},{4,5},{5,4},{6,7},{7,6},{8,9},{9,8},{10,11... | collective-permute-start | bytes 442376 | tf_op jit(solution)/shard_map/ppermute | solution.py:907
  287.0 16.1 %collective-permute-start.18 = (bf16[48,3840]{1,0:T(8,128)(2,1)}, bf16[48,3840]{1,0:T(8,128)(2,1)S(1)}, u32[]{:S(2)}, u32[]{:S(2)}) collective-permute-start(bf16[48,3840]{1,0:T(8,128)(2,1)} %reduce-scatter.2.cloned.1.call-done.mine_ref), channel_id=1, source_target_pairs={{0,1},{1,0},{2,3},{3,2},{4,5},{5,4},{6,7},{7,6},{8,9},{9,8},{10,11... | collective-permute-start | bytes 1105928 | tf_op jit(solution)/shard_map/ppermute | solution.py:907
  293.5 7.1 %copy-start.9 = (bf16[48,1280]{1,0:T(8,128)(2,1)}, bf16[48,1280]{1,0:T(8,128)(2,1)S(1)}, u32[]{:S(2)}) copy-start(bf16[48,1280]{1,0:T(8,128)(2,1)S(1)} %fusion.18.mine_ref) | copy-start | bytes 368644
  293.5 7.1 %collective-permute-start.17 = (bf16[48,1280]{1,0:T(8,128)(2,1)S(1)}, bf16[48,1280]{1,0:T(8,128)(2,1)S(1)}, u32[]{:S(2)}, u32[]{:S(2)}) collective-permute-start(bf16[48,1280]{1,0:T(8,128)(2,1)S(1)} %fusion.18.mine_ref), channel_id=1, source_target_pairs={{0,1},{1,0},{2,3},{3,2},{4,5},{5,4},{6,7},{7,6},{8,9},{9,8},{10,11... | collective-permute-start | bytes 368648 | tf_op jit(solution)/shard_map/ppermute | solution.py:907
  (15 other events, 31.2 us)
Sparse Core Ops, SparseCore 0:
  10.4 93.6 all-gather.1
  159.2 83.3 reduce-scatter.1

commit v7 on v6

--- a/solution.py
+++ b/solution.py
@@ -124,7 +124,10 @@
         tail = jnp.where(lane == 2, b, jnp.where(lane == 3, c, 0.0))
         return jnp.where(lane == 0, first, jnp.where(lane == 1, a, tail)).astype(BF)
 
-    dq = []
+    def scores(h, at):
+        return dot(left[h][0], kt_ref[:, at]), dot(left[h][1], vt_ref[:, at])
+
+    left = []
     for h in range(2):
         mine = (lane < 64) if h == 0 else (lane >= 64)
         delta = jnp.sum(jnp.where(mine, product, 0.0), axis=1, keepdims=True)
@@ -132,13 +135,21 @@
             [jnp.where(mine, q, jnp.zeros_like(q)), extra(lse[:, h : h + 1], 1.0)], axis=1
         )
         dx = jnp.concatenate([jnp.where(mine, do, jnp.zeros_like(do)), extra(delta, 0.0)], axis=1)
-        p = jnp.exp(dot(qx, kt_ref[...]))
+        left.append((qx, dx))
+    work = [(h, slice(k, k + 512)) for h in range(2) for k in range(0, rows, 512)]
+    dq = [jnp.zeros((tile, 128), F32)] * 2
+    ahead = scores(*work[0])
+    for i, (h, at) in enumerate(work):
+        s, dp = ahead
+        if i + 1 < len(work):
+            ahead = scores(*work[i + 1])
+        p = jnp.exp(s)
         low = p.astype(BF)
-        ds = (p * dot(dx, vt_ref[...])).astype(BF)
-        dq.append(dot(ds, k_ref[...]))
+        ds = (p * dp).astype(BF)
+        dq[h] = dq[h] + dot(ds, k_ref[at, :])
         part = slice(64 * h, 64 * h + 64)
-        dkt_ref[part, :] += dot(qt[part, :], ds)
-        dvt_ref[part, :] += dot(dot_t[part, :], low)
+        dkt_ref[part, at] += dot(qt[part, :], ds)
+        dvt_ref[part, at] += dot(dot_t[part, :], low)
     dq = (jnp.where(lane < 64, dq[0], dq[1]) * 0.125).astype(BF)
     d_ref[0, pl.ds(pl.multiple_of(step * tile, 128), tile), :] = dq
 

time: 314 us -> 314 us (level)
  no operation moved by 1% of the time
where the time goes in v7:
time: 314 us; the launch traced here: 313 us
  Pallas kernels  164 us (52%)
  waiting for transfers between devices  70.6 us (22%)
  starting transfers between devices  28.4 us (9%)
  between operations  14.4 us (5%)
  local copies, waits for them, and re-layouts  13.9 us (4%)
  matrix products  10.9 us (3%)
  other arithmetic  10.1 us (3%)
    ppermute x23, waiting for transfers between devices, swap(): return lax.ppermute(x, axis, [(i, i ^ bit) for i in range(size)])  66.7 us
    pallas_call x1, Pallas kernels, attention_backward(): pl.pallas_call(functools.partial(backward_kernel, half, valid), grid=(cou...  42.7 us
    ppermute x23, starting transfers between devices, swap(): return lax.ppermute(x, axis, [(i, i ^ bit) for i in range(size)])  28.3 us
    pallas_call x1, Pallas kernels, attention_forward(): pl.pallas_call(functools.partial(forward_kernel, half, valid), grid=(pair...  20.7 us
    pallas_call x1, Pallas kernels, feed_back(): pl.pallas_call(functools.partial(feed_back_kernel, part), grid_spec=pltpu...  20.1 us
    pallas_call x1, Pallas kernels, spread_weight_gradient(): pl.pallas_call(functools.partial(spread_kernel, part, len(ds), bias.shape...  12.5 us
    dot_general x1, matrix products, dot(): lax.dot_general(a, b, (((ca,), (cb,)), ((), ())), preferred_element_type=...  10.9 us
    pallas_call x1, Pallas kernels, second_gradient(): pl.pallas_call(second_kernel, grid_spec=pltpu.PrefetchScalarGridSpec(num_...  10.2 us
  transfers between devices with their start and end apart: 25, of which 10 were waited for; matrix products, arithmetic and copies ran while one was open for 6% of the time, Pallas kernels for 40%

profile of v7, /device:TPU:0, one launch (start us, length us, event | category | flops | bytes accessed | tf_op | source)
XLA Modules:
  0.0 312.6 jit_solution(15048950210884045209)
XLA Ops:
  7.3 2.1 pack.1
  10.0 3.1 collective-permute-start
  13.1 2.6 collective-permute-start.1
  18.1 7.3 %collective-permute-done.1 = bf16[48,1280]{1,0:T(8,128)(2,1)S(1)} collective-permute-done((bf16[48,1280]{1,0:T(8,128)(2,1)S(1)}, bf16[48,1280]{1,0:T(8,128)(2,1)S(1)}, u32[]{:S(2)}, u32[]{:S(2)}) %collective-permute-start.1) | collective-permute-done | bytes 122912 | tf_op jit(solution)/shard_map/ppermute | solution.py:918
  29.1 12.5 %collective-permute-done.3 = bf16[4,48,1280]{2,1,0:T(8,128)(2,1)S(1)} collective-permute-done((bf16[4,48,1280]{2,1,0:T(8,128)(2,1)S(1)}, bf16[4,48,1280]{2,1,0:T(8,128)(2,1)S(1)}, u32[]{:S(2)}, u32[]{:S(2)}) %collective-permute-start.3) | collective-permute-done | bytes 491552 | tf_op jit(solution)/shard_map/ppermute | solution.py:918
  44.4 3.5 %prepare.2 = (f32[1536,768]{1,0:T(8,128)}, bf16[784,1536]{1,0:T(8,128)(2,1)}, f32[768,128]{1,0:T(8,128)}) custom-call(bf16[1,750,768]{2,1,0:T(8,128)(2,1)} %x_ref.3), custom_call_target="tpu_custom_call" | custom-call | flops 9437184 | bytes 4718592 | tf_op jit(solution)/shard_map/prepare/pallas_call | solution.py:220
  49.5 3.4 %prepare.3 = (f32[1536,768]{1,0:T(8,128)}, bf16[784,1536]{1,0:T(8,128)(2,1)}, f32[768,128]{1,0:T(8,128)}) custom-call(bf16[1,750,768]{2,1,0:T(8,128)(2,1)} %copy-done.6, f32[1536,768]{1,0:T(8,128)} %get-tuple-element.56.refs_0_, bf16[784,1536]{1,0:T(8,128)(2,1)} %get-tuple-element.57.refs_1_), custom_call_target="tpu_custom_call", output_to_operand_aliasing={{0}: (1, {}), {1}: (2, {})} | custom-call | flops 9437184 | bytes 4718592 | tf_op jit(solution)/shard_map/prepare/pallas_call | solution.py:220
  53.9 9.5 %projection.1 = (bf16[1536,1152]{1,0:T(8,128)(2,1)}, bf16[768,1152]{1,0:T(8,128)(2,1)}, bf16[1152,768]{1,0:T(8,128)(2,1)}, f32[16,768]{1,0:T(8,128)}, f32[768,256]{1,0:T(8,128)}) custom-call(s32[17]{0:T(128)} %pad_add_fusion.place_ref, bf16[16,48,1280]{2,1,0:T(8,128)(2,1)} %constant_dynamic-update-slice_fusion.5.held_ref, ...), custom_call_target="tpu_custom_call" | custom-call | flops 2717908992 | bytes 9437184 | tf_op jit(solution)/shard_map/projection/pallas_call | solution.py:335
  63.4 20.7 %attention_forward.1 = (bf16[768,384]{1,0:T(8,128)(2,1)}, bf16[768,384]{1,0:T(8,128)(2,1)}, f32[3,8,1536]{2,1,0:T(8,128)}) custom-call(bf16[1536,1152]{1,0:T(8,128)(2,1)} %get-tuple-element.59.q_ref.k_ref.v_ref, bf16[1536,1152]{1,0:T(8,128)(2,1)} %get-tuple-element.59.q_ref.k_ref.v_ref, bf16[1536,1152]{1,0:T(8,128)(2,1)} %get-tuple-element.59.q_ref.k_ref.v_ref), custom_call_target="tpu_custom_call" | custom-call | flops 14495514624 | bytes 5308416 | tf_op jit(solution)/shard_map/attention_forward/pallas_call | solution.py:68
  88.2 11.9 %collective-permute-done.6.got_ref = bf16[768,384]{1,0:T(8,128)(2,1)S(1)} collective-permute-done((bf16[768,384]{1,0:T(8,128)(2,1)}, bf16[768,384]{1,0:T(8,128)(2,1)S(1)}, u32[]{:S(2)}, u32[]{:S(2)}) %collective-permute-start.6) | collective-permute-done | bytes 589856 | tf_op jit(solution)/shard_map/ppermute | solution.py:918
  100.2 3.9 %all-gather.2.cloned.1.call-done.w_ref.fc2_ref.fc1_ref.late_out_ref = bf16[768,6912]{1,0:T(8,128)(2,1)} async-done(((bf16[48,6912]{1,0:T(8,128)(2,1)}), bf16[768,6912]{1,0:T(8,128)(2,1)}) %all-gather.2.cloned.1.call-update) | async-done | bytes 10616848 | tf_op jit(solution)/shard_map/all_gather | solution.py:1011
  104.0 5.3 %attend.1 = (f32[768,768]{1,0:T(8,128)}, bf16[768,768]{1,0:T(8,128)(2,1)}) custom-call(s32[1]{0:T(128)} %bitcast.1.place_ref, bf16[1,750,768]{2,1,0:T(8,128)(2,1)} %x_ref.3, bf16[768,384]{1,0:T(8,128)(2,1)} %get-tuple-element.60.mine_ref.o_mine_ref, bf16[768,384]{1,0:T(8,128)(2,1)} %copy-done.7, ...), custom_call_target="tpu_custom_call" | custom-call | flops 905969664 | bytes 5898240 | tf_op jit(solution)/shard_map/attend/pallas_call | solution.py:264
  109.3 10.9 %fusion.4 = (bf16[768,3072]{1,0:T(8,128)(2,1)}, bf16[768,3072]{1,0:T(8,128)(2,1)}) fusion(f32[3072]{0:T(1024)S(1)} %add.122, bf16[768,768]{1,0:T(8,128)(2,1)} %get-tuple-element.63.h_ref, bf16[768,6912]{1,0:T(8,128)(2,1)} %all-gather.2.cloned.1.call-done.w_ref.fc2_ref.fc1_ref.late_out_ref), kind=kOutput, calls=%fused_computation.6 | convolution fusion | flops 3652190208 | bytes 15347712 | tf_op jit(solution)/shard_map/dot_general | solution.py:19
  120.2 20.1 %feed_back.1 = (bf16[768,3072]{1,0:T(8,128)(2,1)}, bf16[3072,768]{1,0:T(8,128)(2,1)}, bf16[768,768]{1,0:T(8,128)(2,1)}, bf16[768,384]{1,0:T(8,128)(2,1)}, bf16[7...) custom-call(s32[1]{0:T(128)} %bitcast.1.place_ref, ...), custom_call_target="tpu_custom_call" | custom-call | flops 7247757312 | bytes 23592960 | tf_op jit(solution)/shard_map/feed_back/pallas_call | solution.py:748
  140.3 8.3 %third_gradient.1 = (bf16[8,192,768]{2,1,0:T(8,128)(2,1)}, bf16[8,192,768]{2,1,0:T(8,128)(2,1)}) custom-call(s32[1]{0:T(128)} %bitcast.place_ref, bf16[768,3072]{1,0:T(8,128)(2,1)} %get-tuple-element.64.z_ref, bf16[1,750,768]{2,1,0:T(8,128)(2,1)} %cot_ref.3, bf16[768,384]{1,0:T(8,128)(2,1)} %get-tuple-element.67.token_ref), custom_call_target="tpu_custom_call" | custom-call | flops 3623878656 | bytes 9437184 | tf_op jit(solution)/shard_map/third_gradient/pallas_call | solution.py:640
  148.9 10.2 %second_gradient.1 = bf16[768,3840]{1,0:T(8,128)(2,1)} custom-call(s32[1]{0:T(128)} %bitcast.1.place_ref, bf16[8,192,768]{2,1,0:T(8,128)(2,1)} %get-tuple-element.69.token_ref, bf16[768,384]{1,0:T(8,128)(2,1)} %get-tuple-element.60.mine_ref.o_mine_ref, bf16[768,384]{1,0:T(8,128)(2,1)} %copy-done.7, bf16[768,768]{1,0:T(8,128)(2,1)} %get-tuple-element.84.residual_ref.drb_ref, ...), custom_call_target="tpu_custom_call" | custom-call | flops 4529848320 | bytes 9437184 | tf_op jit(solution)/shard_map/second_gradient/pallas_call | solution.py:570
  161.2 2.2 convert_add_fusion
  164.7 11.0 %collective-permute-done.8.got_ref = bf16[768,384]{1,0:T(8,128)(2,1)} collective-permute-done((bf16[768,384]{1,0:T(8,128)(2,1)}, bf16[768,384]{1,0:T(8,128)(2,1)}, u32[]{:S(2)}, u32[]{:S(2)}) %collective-permute-start.8) | collective-permute-done | bytes 589856 | tf_op jit(solution)/shard_map/ppermute | solution.py:918
  175.7 42.7 %attention_backward.1.token_ref.refs_0_ = bf16[3,1536,384]{2,1,0:T(8,128)(2,1)} custom-call(bf16[1536,1152]{1,0:T(8,128)(2,1)} %get-tuple-element.59.q_ref.k_ref.v_ref, bf16[1536,1152]{1,0:T(8,128)(2,1)} %get-tuple-element.59.q_ref.k_ref.v_ref, bf16[1536,1152]{1,0:T(8,128)(2,1)} %get-tuple-element.59.q_ref.k_ref.v_ref, ...), custom_call_target="tpu_custom_call" | custom-call | flops 28991029248 | bytes 9437184 | tf_op jit(solution)/shard_map/attention_backward/pallas_call | solution.py:173
  218.4 4.5 %projection_input_gradient.2 = bf16[768,768]{1,0:T(8,128)(2,1)} custom-call(bf16[3,1536,384]{2,1,0:T(8,128)(2,1)} %attention_backward.1.token_ref.refs_0_, bf16[1152,768]{1,0:T(8,128)(2,1)} %get-tuple-element.72.wt_ref, bf16[3,1536,384]{2,1,0:T(8,128)(2,1)} %attention_backward.1.token_ref.refs_0_), custom_call_target="tpu_custom_call" | custom-call | flops 1358954496 | bytes 3538944 | tf_op jit(solution)/shard_map/projection_input_gradient/pallas_call | solution.py:531
  224.2 12.5 %spread_weight_gradient.1 = (bf16[8,48,1280]{2,1,0:T(8,128)(2,1)}, bf16[8,48,1280]{2,1,0:T(8,128)(2,1)}) custom-call(s32[2]{0:T(128)} %pad_add_fusion.1.place_ref, bf16[4,96,768]{2,1,0:T(8,128)(2,1)} %get-tuple-element.105.token_ref, bf16[784,1536]{1,0:T(8,128)(2,1)} %get-tuple-element.74.xt_ref, bf16[768,1152]{1,0:T(8,128)(2,1)} %get-tuple-element.75.w_ref, ...), custom_call_target="tpu_custom_call" | custom-call | flops 2717908992 | bytes 4718592 | tf_op jit(solution)/shard_map/spread_weight_gradient/pallas_call | solution.py:492
  242.5 12.1 %collective-permute-done.10 = bf16[4,96,768]{2,1,0:T(8,128)(2,1)S(1)} collective-permute-done((bf16[4,96,768]{2,1,0:T(8,128)(2,1)}, bf16[4,96,768]{2,1,0:T(8,128)(2,1)S(1)}, u32[]{:S(2)}, u32[]{:S(2)}) %collective-permute-start.10) | collective-permute-done | bytes 589856 | tf_op jit(solution)/shard_map/ppermute | solution.py:918
  256.0 2.2 collective-permute-start.20
  259.9 4.5 %projection_input_gradient.3.mine_ref = bf16[768,768]{1,0:T(8,128)(2,1)} custom-call(bf16[96,768]{1,0:T(8,128)(2,1)} %copy-done.8, bf16[1152,768]{1,0:T(8,128)(2,1)} %get-tuple-element.72.wt_ref, bf16[3,1536,384]{2,1,0:T(8,128)(2,1)} %attention_backward.1.token_ref.refs_0_), custom_call_target="tpu_custom_call" | custom-call | flops 1358954496 | bytes 3538944 | tf_op jit(solution)/shard_map/projection_input_gradient/pallas_call | solution.py:531
  265.4 5.1 %input_end.1 = f32[750,1,768]{2,1,0:T(1,128)} custom-call(bf16[768,768]{1,0:T(8,128)(2,1)} %projection_input_gradient.3.mine_ref, bf16[768,768]{1,0:T(8,128)(2,1)} %collective-permute-done.12.got_ref, bf16[768,768]{1,0:T(8,128)(2,1)} %get-tuple-element.84.residual_ref.drb_ref, f32[1536,768]{1,0:T(8,128)} %get-tuple-element.58.x_ref.normed_ref, ...), custom_call_target="tpu_custom_call" | custom-call | flops 5898240 | bytes 10616832 | tf_op jit(solution)/shard_map/input_end/pallas_call | solution.py:901
  270.5 8.1 %output_end.1 = bf16[1,750,768]{2,1,0:T(8,128)(2,1)} custom-call(bf16[96,768]{1,0:T(8,128)(2,1)} %copy-done.8, bf16[768,3072]{1,0:T(8,128)(2,1)} %get-tuple-element.64.z_ref, bf16[3072,768]{1,0:T(8,128)(2,1)} %get-tuple-element.83.w_ref, f32[768,768]{1,0:T(8,128)} %get-tuple-element.66.late_ref, f32[1,768]{1,0:T(1,128)} %get-tuple-element.126.rows_ref), custom_call_target="tpu_custom_call" | custom-call | flops 3623878656 | bytes 9437184 | tf_op jit(solution)/shard_map/output_end/pallas_call | solution.py:846
  280.4 2.0 collective-permute-start.15
  282.4 1.9 collective-permute-start.16
  287.5 4.8 %collective-permute-done.15 = bf16[48,1280]{1,0:T(8,128)(2,1)S(1)} collective-permute-done((bf16[48,1280]{1,0:T(8,128)(2,1)S(1)}, bf16[48,1280]{1,0:T(8,128)(2,1)S(1)}, u32[]{:S(2)}, u32[]{:S(2)}) %collective-permute-start.15) | collective-permute-done | bytes 122912 | tf_op jit(solution)/shard_map/ppermute | solution.py:918
  295.6 4.9 %collective-permute-done.17.theirs_ref = bf16[48,1280]{1,0:T(8,128)(2,1)S(1)} collective-permute-done((bf16[48,1280]{1,0:T(8,128)(2,1)S(1)}, bf16[48,1280]{1,0:T(8,128)(2,1)S(1)}, u32[]{:S(2)}, u32[]{:S(2)}) %collective-permute-start.17) | collective-permute-done | bytes 122912 | tf_op jit(solution)/shard_map/ppermute | solution.py:918
  301.2 1.8 finish.1
  303.8 2.0 join_second.1
  (118 shorter events, 40.5 us)
Async XLA Ops:
  7.3 8.4 %copy-start.1 = (bf16[1,750,768]{2,1,0:T(8,128)(2,1)S(1)}, bf16[1,750,768]{2,1,0:T(8,128)(2,1)}, u32[]{:S(2)}) copy-start(bf16[1,750,768]{2,1,0:T(8,128)(2,1)} %x_ref.3) | copy-start | bytes 3456004
  7.3 96.7 %all-gather.2.cloned.1.call-start = ((), (), s32[]{:S(2)}) async-start(), calls=%async_computation.1 | async-start | bytes 11280384 | tf_op jit(solution)/shard_map/all_gather | solution.py:1011
  9.5 277.4 %reduce-scatter.2.cloned.1.call-start = ((), (), s32[]{:S(2)}) async-start(), calls=%async_computation.2 | async-start | bytes 6266880 | tf_op jit(solution)/shard_map/reduce_scatter | solution.py:1052
  10.0 33.8 %copy-start = (s32[16]{0:T(128)S(1)}, s32[16]{0:T(128)}, u32[]{:S(2)}) copy-start(s32[16]{0:T(128)} %constant.112.clone) | copy-start | bytes 196
  10.0 8.1 %collective-permute-start = (bf16[48,1280]{1,0:T(8,128)(2,1)S(1)}, bf16[48,1280]{1,0:T(8,128)(2,1)S(1)}, u32[]{:S(2)}, u32[]{:S(2)}) collective-permute-start(bf16[48,1280]{1,0:T(8,128)(2,1)S(1)} %get-tuple-element.124), channel_id=1, source_target_pairs={{0,8},{2,10},{4,12},{6,14},{8,0},{10,2},{12,4},{14,6},{16,24},{18,... | collective-permute-start | bytes 368648 | tf_op jit(solution)/shard_map/ppermute | solution.py:918
  13.1 12.3 %collective-permute-start.1 = (bf16[48,1280]{1,0:T(8,128)(2,1)S(1)}, bf16[48,1280]{1,0:T(8,128)(2,1)S(1)}, u32[]{:S(2)}, u32[]{:S(2)}) collective-permute-start(bf16[48,1280]{1,0:T(8,128)(2,1)S(1)} %get-tuple-element.124), channel_id=1, source_target_pairs={{0,16},{2,18},{4,20},{6,22},{8,24},{10,26},{12,28},{14,30},{16,0},... | collective-permute-start | bytes 368648 | tf_op jit(solution)/shard_map/ppermute | solution.py:918
  15.7 9.7 %collective-permute-start.2 = (bf16[48,1280]{1,0:T(8,128)(2,1)S(1)}, bf16[48,1280]{1,0:T(8,128)(2,1)S(1)}, u32[]{:S(2)}, u32[]{:S(2)}) collective-permute-start(bf16[48,1280]{1,0:T(8,128)(2,1)S(1)} %get-tuple-element.124), channel_id=1, source_target_pairs={{0,24},{2,26},{4,28},{6,30},{8,16},{10,18},{12,20},{14,22},{16,8},... | collective-permute-start | bytes 368648 | tf_op jit(solution)/shard_map/ppermute | solution.py:918
  15.7 32.7 %collective-permute-start.5 = (bf16[1,750,768]{2,1,0:T(8,128)(2,1)S(1)}, bf16[1,750,768]{2,1,0:T(8,128)(2,1)S(1)}, u32[]{:S(2)}, u32[]{:S(2)}) collective-permute-start(bf16[1,750,768]{2,1,0:T(8,128)(2,1)S(1)} %copy-done.1), channel_id=1, source_target_pairs={{0,1},{1,0},{2,3},{3,2},{4,5},{5,4},{6,7},{7,6},{8,9},{9,8},{10,11... | collective-permute-start | bytes 3456008 | tf_op jit(solution)/shard_map/ppermute | solution.py:918
  25.5 16.1 %collective-permute-start.3 = (bf16[4,48,1280]{2,1,0:T(8,128)(2,1)S(1)}, bf16[4,48,1280]{2,1,0:T(8,128)(2,1)S(1)}, u32[]{:S(2)}, u32[]{:S(2)}) collective-permute-start(bf16[4,48,1280]{2,1,0:T(8,128)(2,1)S(1)} %pad_maximum_fusion), channel_id=1, source_target_pairs={{0,4},{2,6},{4,0},{6,2},{8,12},{10,14},{12,8},{14,10},{16,20},{18,... | collective-permute-start | bytes 1474568 | tf_op jit(solution)/shard_map/ppermute | solution.py:918
  43.7 9.2 %collective-permute-start.4 = (bf16[8,48,1280]{2,1,0:T(8,128)(2,1)}, bf16[8,48,1280]{2,1,0:T(8,128)(2,1)S(1)}, u32[]{:S(2)}, u32[]{:S(2)}) collective-permute-start(bf16[8,48,1280]{2,1,0:T(8,128)(2,1)} %get-tuple-element.110), channel_id=1, source_target_pairs={{0,2},{2,0},{4,6},{6,4},{8,10},{10,8},{12,14},{14,12},{16,18},{18,... | collective-permute-start | bytes 2949128 | tf_op jit(solution)/shard_map/ppermute | solution.py:918
  84.2 16.0 %collective-permute-start.6 = (bf16[768,384]{1,0:T(8,128)(2,1)}, bf16[768,384]{1,0:T(8,128)(2,1)S(1)}, u32[]{:S(2)}, u32[]{:S(2)}) collective-permute-start(bf16[768,384]{1,0:T(8,128)(2,1)} %get-tuple-element.61.o_sent_ref), channel_id=1, source_target_pairs={{0,1},{1,0},{2,3},{3,2},{4,5},{5,4},{6,7},{7,6},{8,9},{9,8},{10,11... | collective-permute-start | bytes 1769480 | tf_op jit(solution)/shard_map/ppermute | solution.py:918
  148.6 12.6 %collective-permute-start.7 = (bf16[8,192,768]{2,1,0:T(8,128)(2,1)}, bf16[8,192,768]{2,1,0:T(8,128)(2,1)}, u32[]{:S(2)}, u32[]{:S(2)}) collective-permute-start(bf16[8,192,768]{2,1,0:T(8,128)(2,1)} %get-tuple-element.69.token_ref), channel_id=1, source_target_pairs={{0,2},{2,0},{4,6},{6,4},{8,10},{10,8},{12,14},{14,12},{16,18},{18,... | collective-permute-start | bytes 7077896 | tf_op jit(solution)/shard_map/ppermute | solution.py:918
  159.1 16.6 %collective-permute-start.8 = (bf16[768,384]{1,0:T(8,128)(2,1)}, bf16[768,384]{1,0:T(8,128)(2,1)}, u32[]{:S(2)}, u32[]{:S(2)}) collective-permute-start(bf16[768,384]{1,0:T(8,128)(2,1)} %get-tuple-element.67.token_ref), channel_id=1, source_target_pairs={{0,1},{1,0},{2,3},{3,2},{4,5},{5,4},{6,7},{7,6},{8,9},{9,8},{10,11... | collective-permute-start | bytes 1769480 | tf_op jit(solution)/shard_map/ppermute | solution.py:918
  163.7 12.0 %copy-start.5 = (bf16[8,96,768]{2,1,0:T(8,128)(2,1)}, bf16[8,96,768]{2,1,0:T(8,128)(2,1)S(1)}, u32[]{:S(2)}) copy-start(bf16[8,96,768]{2,1,0:T(8,128)(2,1)S(1)} %get-tuple-element.101.token_ref) | copy-start | bytes 3538948
  163.7 59.2 %collective-permute-start.9 = (bf16[8,96,768]{2,1,0:T(8,128)(2,1)S(1)}, bf16[8,96,768]{2,1,0:T(8,128)(2,1)S(1)}, u32[]{:S(2)}, u32[]{:S(2)}) collective-permute-start(bf16[8,96,768]{2,1,0:T(8,128)(2,1)S(1)} %get-tuple-element.101.token_ref), channel_id=1, source_target_pairs={{0,1},{1,0},{2,3},{3,2},{4,5},{5,4},{6,7},{7,6},{8,9},{9,8},{10,11... | collective-permute-start | bytes 3538952 | tf_op jit(solution)/shard_map/ppermute | solution.py:918
  236.7 2.8 collective-permute-start.11
  236.7 28.7 %collective-permute-start.12 = (bf16[768,768]{1,0:T(8,128)(2,1)}, bf16[768,768]{1,0:T(8,128)(2,1)}, u32[]{:S(2)}, u32[]{:S(2)}) collective-permute-start(bf16[768,768]{1,0:T(8,128)(2,1)} %projection_input_gradient.2), channel_id=1, source_target_pairs={{0,1},{1,0},{2,3},{3,2},{4,5},{5,4},{6,7},{7,6},{8,9},{9,8},{10,11... | collective-permute-start | bytes 3538952 | tf_op jit(solution)/shard_map/ppermute | solution.py:918
  238.2 16.4 %collective-permute-start.10 = (bf16[4,96,768]{2,1,0:T(8,128)(2,1)}, bf16[4,96,768]{2,1,0:T(8,128)(2,1)S(1)}, u32[]{:S(2)}, u32[]{:S(2)}) collective-permute-start(bf16[4,96,768]{2,1,0:T(8,128)(2,1)} %get-tuple-element.105.token_ref), channel_id=1, source_target_pairs={{0,4},{2,6},{4,0},{6,2},{8,12},{10,14},{12,8},{14,10},{16,20},{18,... | collective-permute-start | bytes 1769480 | tf_op jit(solution)/shard_map/ppermute | solution.py:918
  239.5 15.1 %copy-start.4 = (bf16[4,96,768]{2,1,0:T(8,128)(2,1)S(1)}, bf16[4,96,768]{2,1,0:T(8,128)(2,1)}, u32[]{:S(2)}) copy-start(bf16[4,96,768]{2,1,0:T(8,128)(2,1)} %get-tuple-element.81) | copy-start | bytes 1769476
  241.8 36.8 %collective-permute-start.13 = (bf16[4,48,1280]{2,1,0:T(8,128)(2,1)}, bf16[4,48,1280]{2,1,0:T(8,128)(2,1)}, u32[]{:S(2)}, u32[]{:S(2)}) collective-permute-start(bf16[4,48,1280]{2,1,0:T(8,128)(2,1)} %fusion.11), channel_id=1, source_target_pairs={{0,4},{2,6},{4,0},{6,2},{8,12},{10,14},{12,8},{14,10},{16,20},{18,... | collective-permute-start | bytes 1474568 | tf_op jit(solution)/shard_map/ppermute | solution.py:918
  255.5 4.4 %copy-start.8 = (bf16[96,768]{1,0:T(8,128)(2,1)}, bf16[96,768]{1,0:T(8,128)(2,1)S(1)}, u32[]{:S(2)}) copy-start(bf16[96,768]{1,0:T(8,128)(2,1)S(1)} %get-tuple-element.104.token_ref) | copy-start | bytes 442372
  255.5 26.9 %collective-permute-start.19 = (bf16[96,768]{1,0:T(8,128)(2,1)}, bf16[96,768]{1,0:T(8,128)(2,1)S(1)}, u32[]{:S(2)}, u32[]{:S(2)}) collective-permute-start(bf16[96,768]{1,0:T(8,128)(2,1)} %get-tuple-element.102), channel_id=1, source_target_pairs={{0,8},{2,10},{4,12},{6,14},{8,0},{10,2},{12,4},{14,6},{16,24},{18,... | collective-permute-start | bytes 442376 | tf_op jit(solution)/shard_map/ppermute | solution.py:918
  256.0 28.3 %collective-permute-start.20 = (bf16[96,768]{1,0:T(8,128)(2,1)}, bf16[96,768]{1,0:T(8,128)(2,1)}, u32[]{:S(2)}, u32[]{:S(2)}) collective-permute-start(bf16[96,768]{1,0:T(8,128)(2,1)} %get-tuple-element.103), channel_id=1, source_target_pairs={{0,16},{2,18},{4,20},{6,22},{8,24},{10,26},{12,28},{14,30},{16,0},... | collective-permute-start | bytes 442376 | tf_op jit(solution)/shard_map/ppermute | solution.py:918
  258.2 26.1 %collective-permute-start.21 = (bf16[96,768]{1,0:T(8,128)(2,1)S(1)}, bf16[96,768]{1,0:T(8,128)(2,1)}, u32[]{:S(2)}, u32[]{:S(2)}) collective-permute-start(bf16[96,768]{1,0:T(8,128)(2,1)S(1)} %get-tuple-element.104.token_ref), channel_id=1, source_target_pairs={{0,24},{2,26},{4,28},{6,30},{8,16},{10,18},{12,20},{14,22},{16,8},... | collective-permute-start | bytes 442376 | tf_op jit(solution)/shard_map/ppermute | solution.py:918
  279.8 5.6 %copy-start.2 = (f32[4,48,1280]{2,1,0:T(8,128)}, f32[4,48,1280]{2,1,0:T(8,128)S(1)}, u32[]{:S(2)}) copy-start(f32[4,48,1280]{2,1,0:T(8,128)S(1)} %bitcast_add_fusion) | copy-start | bytes 2949124
  279.8 7.6 %collective-permute-start.14 = (bf16[48,1280]{1,0:T(8,128)(2,1)S(1)}, bf16[48,1280]{1,0:T(8,128)(2,1)S(1)}, u32[]{:S(2)}, u32[]{:S(2)}) collective-permute-start(bf16[48,1280]{1,0:T(8,128)(2,1)S(1)} %get-tuple-element.107), channel_id=1, source_target_pairs={{0,8},{2,10},{4,12},{6,14},{8,0},{10,2},{12,4},{14,6},{16,24},{18,... | collective-permute-start | bytes 368648 | tf_op jit(solution)/shard_map/ppermute | solution.py:918
  280.4 11.9 %collective-permute-start.15 = (bf16[48,1280]{1,0:T(8,128)(2,1)S(1)}, bf16[48,1280]{1,0:T(8,128)(2,1)S(1)}, u32[]{:S(2)}, u32[]{:S(2)}) collective-permute-start(bf16[48,1280]{1,0:T(8,128)(2,1)S(1)} %get-tuple-element.109), channel_id=1, source_target_pairs={{0,16},{2,18},{4,20},{6,22},{8,24},{10,26},{12,28},{14,30},{16,0},... | collective-permute-start | bytes 368648 | tf_op jit(solution)/shard_map/ppermute | solution.py:918
  282.4 9.9 %collective-permute-start.16 = (bf16[48,1280]{1,0:T(8,128)(2,1)S(1)}, bf16[48,1280]{1,0:T(8,128)(2,1)S(1)}, u32[]{:S(2)}, u32[]{:S(2)}) collective-permute-start(bf16[48,1280]{1,0:T(8,128)(2,1)S(1)} %get-tuple-element.108), channel_id=1, source_target_pairs={{0,24},{2,26},{4,28},{6,30},{8,16},{10,18},{12,20},{14,22},{16,8},... | collective-permute-start | bytes 368648 | tf_op jit(solution)/shard_map/ppermute | solution.py:918
  285.4 9.4 %collective-permute-start.22 = (bf16[96,768]{1,0:T(8,128)(2,1)S(1)}, bf16[96,768]{1,0:T(8,128)(2,1)S(1)}, u32[]{:S(2)}, u32[]{:S(2)}) collective-permute-start(bf16[96,768]{1,0:T(8,128)(2,1)S(1)} %fusion.15), channel_id=1, source_target_pairs={{0,1},{1,0},{2,3},{3,2},{4,5},{5,4},{6,7},{7,6},{8,9},{9,8},{10,11... | collective-permute-start | bytes 442376 | tf_op jit(solution)/shard_map/ppermute | solution.py:918
  286.9 16.1 %collective-permute-start.18 = (bf16[48,3840]{1,0:T(8,128)(2,1)}, bf16[48,3840]{1,0:T(8,128)(2,1)S(1)}, u32[]{:S(2)}, u32[]{:S(2)}) collective-permute-start(bf16[48,3840]{1,0:T(8,128)(2,1)} %reduce-scatter.2.cloned.1.call-done.mine_ref), channel_id=1, source_target_pairs={{0,1},{1,0},{2,3},{3,2},{4,5},{5,4},{6,7},{7,6},{8,9},{9,8},{10,11... | collective-permute-start | bytes 1105928 | tf_op jit(solution)/shard_map/ppermute | solution.py:918
  293.3 7.3 %copy-start.9 = (bf16[48,1280]{1,0:T(8,128)(2,1)}, bf16[48,1280]{1,0:T(8,128)(2,1)S(1)}, u32[]{:S(2)}) copy-start(bf16[48,1280]{1,0:T(8,128)(2,1)S(1)} %fusion.18.mine_ref) | copy-start | bytes 368644
  293.3 7.3 %collective-permute-start.17 = (bf16[48,1280]{1,0:T(8,128)(2,1)S(1)}, bf16[48,1280]{1,0:T(8,128)(2,1)S(1)}, u32[]{:S(2)}, u32[]{:S(2)}) collective-permute-start(bf16[48,1280]{1,0:T(8,128)(2,1)S(1)} %fusion.18.mine_ref), channel_id=1, source_target_pairs={{0,1},{1,0},{2,3},{3,2},{4,5},{5,4},{6,7},{7,6},{8,9},{9,8},{10,11... | collective-permute-start | bytes 368648 | tf_op jit(solution)/shard_map/ppermute | solution.py:918
  (15 other events, 31.2 us)
Sparse Core Ops, SparseCore 0:
  10.4 93.6 all-gather.1
  159.2 83.3 reduce-scatter.1
